TPU v7x, 32 devices: a whole 2x2x4 slice. The times are simulated.
32 devices in a mesh: group: 2 (over y), seq: 4 (over z), tensor: 4 (over x, core).
Axes of the slice: x: 2, y: 2, z: 4, core: 2. Of those that a mesh axis runs over, the one named last changes fastest.
Arguments:
- spans: bfloat16 [1024, 3072], P(('group', 'seq')), parts along dimension 0, may hold values from -6 to 6
- w_in: bfloat16 [3072, 1024], P(None, 'tensor'), may hold values from -0.109375 to 0.109375
- band_weights: bfloat16 [4096, 128], P(('group', 'seq')), parts along dimension 0
- offsets: int32 [32], P(('group', 'seq')), parts along dimension 0, may hold values from 0 to 384, as said below
- w_up: bfloat16 [1024, 4096], P(None, 'tensor'), may hold values from -0.1875 to 0.1875
- d_up: bfloat16 [4096, 4096], P(('group', 'seq'), 'tensor'), parts along dimension 0, may hold values from -3 to 3
Outputs:
- up_proj: bfloat16 [4096, 4096], P(('group', 'seq'), 'tensor'), parts along dimension 0
- d_spans: bfloat16 [1024, 3072], P(('group', 'seq'), 'tensor'), parts along dimension 0
There are 2 independent parts, one for each index of `group`. A program takes and returns all parts, laid end to end along the dimension named above; an argument that names none is the same for every part. Nothing has to cross between parts.
Inputs may be any that keep to these rules, and one draw needn't show every extreme that they name: offsets[b] differs from b * 384 // 15 by at most 128, and both differences -128 and +128 occur in every draw; offsets[0] = 0 and offsets[15] = 384. Hence the bands of the bytes of seq index i lie within the span rows of seq indices i - 3 to i + 3.
All inputs are finite; a program needn't handle non-finite values.
Results may differ from a plain program's by a relative error of at most 0.0058.
Values may be sent and summed in bfloat16 or wider, within the bound.
No kernel may reach another device: no remote copies, remote signals or barrier semaphores. Data moves between devices by JAX's collectives and lax.ppermute only.
A program may use at most 64 MiB of HBM per device.

v0:
```python
import jax
import jax.numpy as jnp
from jax import lax
from jax.sharding import PartitionSpec as P


def band_matrix(band_weights, offsets, anchor, length):
    blocks = offsets.shape[0]
    breadth = band_weights.shape[1]
    band_cube = band_weights.reshape(blocks, -1, breadth)
    relative = anchor + jnp.arange(length, dtype=jnp.int32)[None, :] - offsets[:, None]
    picker = (relative[:, None, :] == jnp.arange(breadth, dtype=jnp.int32)[None, :, None]).astype(
        jnp.bfloat16
    )
    spread = jnp.einsum("bij,bjr->bir", band_cube, picker, preferred_element_type=jnp.float32)
    return spread.astype(jnp.bfloat16).reshape(-1, length)


def touches(offsets, breadth, anchor, length):
    return jnp.any((offsets < anchor + length) & (offsets + breadth > anchor))


def body(spans, w_in, band_weights, offsets, w_up, d_up):
    breadth = band_weights.shape[1]
    reduced = jnp.dot(spans, w_in, preferred_element_type=jnp.float32).astype(jnp.bfloat16)
    feature_count = reduced.shape[1]
    span_rows = reduced.shape[0]
    initial = jnp.zeros((band_weights.shape[0], feature_count), jnp.float32)
    shard_rows = lax.all_gather(reduced, "seq", axis=0, tiled=True)
    anchor = jnp.int32(0)
    length = shard_rows.shape[0]

    def accumulate(current):
        spread = band_matrix(band_weights, offsets, anchor, length)
        return jnp.dot(spread, shard_rows, preferred_element_type=jnp.float32)

    def unchanged(current):
        return current

    upsampled = lax.cond(
        touches(offsets, breadth, anchor, length), accumulate, unchanged, initial
    ).astype(jnp.bfloat16)
    gathered = lax.all_gather(upsampled, "tensor", axis=1, tiled=True)
    up_proj = jnp.dot(gathered, w_up, preferred_element_type=jnp.float32).astype(jnp.bfloat16)
    grad_cols = lax.psum_scatter(
        lax.dot_general(w_up, d_up, (((1,), (1,)), ((), ())), preferred_element_type=jnp.float32),
        "tensor",
        scatter_dimension=0,
        tiled=True,
    ).astype(jnp.bfloat16)

    def compute(operand):
        spread = band_matrix(band_weights, offsets, 0, span_rows * lax.axis_size("seq"))
        return lax.dot_general(
            spread, grad_cols, (((0,), (1,)), ((), ())), preferred_element_type=jnp.float32
        )

    def nothing(operand):
        return jnp.zeros((span_rows * lax.axis_size("seq"), feature_count), jnp.float32)

    every_row = lax.psum(
        lax.cond(
            touches(offsets, breadth, 0, span_rows * lax.axis_size("seq")), compute, nothing, 0
        ),
        "seq",
    )
    d_reduced = lax.dynamic_slice_in_dim(every_row, lax.axis_index("seq") * span_rows, span_rows, 0)
    d_reduced = d_reduced.astype(jnp.bfloat16)
    feature_parts = lax.dot_general(
        d_reduced, w_in, (((1,), (1,)), ((), ())), preferred_element_type=jnp.float32
    )
    d_spans = lax.psum_scatter(feature_parts, "tensor", scatter_dimension=1, tiled=True).astype(
        jnp.bfloat16
    )
    return (up_proj, d_spans)


def solution(mesh):
    placed = (
        P(("group", "seq"), None),
        P(None, "tensor"),
        P(("group", "seq"), None),
        P(("group", "seq")),
        P(None, "tensor"),
        P(("group", "seq"), "tensor"),
    )
    return jax.shard_map(
        body,
        mesh=mesh,
        in_specs=placed,
        out_specs=(P(("group", "seq"), "tensor"), P(("group", "seq"), "tensor")),
        check_vma=False,
    )
```

profile of v0, /device:TPU:0, one launch (start us, length us, event | category | flops | bytes accessed | tf_op | source)
XLA Modules:
  0.0 116.6 jit_solution(14578127177563211295)
XLA Ops:
  7.2 0.0 copy-start
  7.2 0.0 reduce-scatter.3.cloned.1.call-start
  7.2 1.5 %copy-done = bf16[1024,1024]{1,0:T(8,128)(2,1)S(1)} copy-done((bf16[1024,1024]{1,0:T(8,128)(2,1)S(1)}, bf16[1024,1024]{1,0:T(8,128)(2,1)}, u32[]{:S(2)}) %copy-start) | copy-done | bytes 2097176
  8.8 3.9 %fusion.6 = f32[1024,512]{1,0:T(8,128)} fusion(bf16[1024,1024]{1,0:T(8,128)(2,1)S(1)} %copy-done, bf16[512,1024]{1,0:T(8,128)(2,1)} %param.15), kind=kOutput, calls=%fused_computation.16 | convolution fusion | flops 1073741824 | bytes 5242880 | tf_op jit(solution)/shard_map/dot_general | solution.py:46
  12.6 0.0 copy-start.4
  12.6 0.0 copy-start.2
  12.6 0.0 copy-start.3
  12.6 0.0 reduce-scatter.3.cloned.1.call-update
  12.7 0.0 all-gather.2.cloned.1.call-start
  12.7 0.6 copy-done.4
  13.3 0.6 and_reduce_fusion
  14.6 0.0 copy-done.2
  14.6 1.8 %convolution_convert_fusion.3 = bf16[128,256]{1,0:T(8,128)(2,1)S(1)} fusion(bf16[128,3072]{1,0:T(8,128)(2,1)S(1)} %copy-done.2, bf16[3072,256]{1,0:T(8,128)(2,1)} %param.11), kind=kOutput, calls=%fused_computation.9 | convolution fusion | flops 201359360 | bytes 2424832 | tf_op jit(solution)/shard_map/dot_general | solution.py:25
  16.4 15.6 %all_gather.6 = bf16[512,256]{1,0:T(8,128)(2,1)S(1)} all-gather(bf16[128,256]{1,0:T(8,128)(2,1)S(1)} %convolution_convert_fusion.3), channel_id=1, replica_groups=mesh['group'=2,'seq'=4,'tensor'=4] {'seq'}, dimensions={0}, use_global_device_ids=true | all-gather | bytes 327680 | tf_op jit(solution)/shard_map/all_gather | solution.py:29
  32.0 0.0 copy-done.3
  32.0 0.7 conditional.2
  32.0 0.1 iota_subtract_fusion
  32.1 0.3 convolution_convert_fusion
  32.4 0.3 fusion.4
  32.7 0.0 copy-start.1
  32.7 0.7 copy-done.1
  33.4 0.0 all-gather.2.cloned.1.call-update
  33.5 0.0 reduce-scatter.5.cloned.1.call-start
  33.5 13.4 %reduce-scatter.3.cloned.1.call-done = f32[256,512]{1,0:T(8,128)} async-done(((f32[1024,512]{1,0:T(8,128)}), f32[256,512]{1,0:T(8,128)}) %reduce-scatter.3.cloned.1.call-update) | async-done | bytes 524304 | tf_op jit(solution)/shard_map/reduce_scatter | solution.py:45
  46.9 1.1 convert_element_type.40
  48.0 0.8 conditional.3
  48.0 0.1 iota_subtract_fusion.1
  48.1 0.3 convolution_convert_fusion.1
  48.5 0.3 fusion.5
  48.8 30.5 %all-reduce.1 = bf16[512,256]{1,0:T(8,128)(2,1)S(1)} all-reduce(f32[512,256]{1,0:T(8,128)S(1)} %get-tuple-element.27), channel_id=1, replica_groups=mesh['group'=2,'seq'=4,'tensor'=4] {'seq'}, use_global_device_ids=true, to_apply=%region_6.0 | all-reduce | flops 131072 | bytes 786432 | tf_op jit(solution)/shard_map/psum | solution.py:61
  79.3 3.2 %fusion.2 = f32[128,3072]{1,0:T(8,128)} fusion(bf16[3072,256]{1,0:T(8,128)(2,1)} %param.11, bf16[512,256]{1,0:T(8,128)(2,1)S(1)} %all-reduce.1, s32[]{:T(128)S(6)} %select_n.3), kind=kOutput, calls=%fused_computation.11 | convolution fusion | flops 201326592 | bytes 3211268 | tf_op jit(solution)/shard_map/dot_general | solution.py:69
  82.5 0.0 reduce-scatter.5.cloned.1.call-update
  82.5 0.0 all-gather.2.cloned.1.call-done
  82.5 3.4 %convolution_convert_fusion.2 = bf16[512,1024]{1,0:T(8,128)(2,1)} fusion(bf16[512,1024]{1,0:T(8,128)(2,1)} %all-gather.2.cloned.1.call-done, bf16[1024,1024]{1,0:T(8,128)(2,1)S(1)} %copy-done), kind=kOutput, calls=%fused_computation.8 | convolution fusion | flops 1074266112 | bytes 4194304 | tf_op jit(solution)/shard_map/dot_general | solution.py:44
  86.0 22.4 %reduce-scatter.5.cloned.1.call-done = f32[128,768]{1,0:T(8,128)} async-done(((f32[128,3072]{1,0:T(8,128)}), f32[128,768]{1,0:T(8,128)}) %reduce-scatter.5.cloned.1.call-update) | async-done | bytes 393232 | tf_op jit(solution)/shard_map/reduce_scatter | solution.py:72
  108.4 1.7 %convert_element_type.42 = bf16[128,768]{1,0:T(8,128)(2,1)} convert(f32[128,768]{1,0:T(8,128)} %reduce-scatter.5.cloned.1.call-done) | non-fusion elementwise | flops 98304 | bytes 589824 | tf_op jit(solution)/shard_map/convert_element_type | solution.py:72
Async XLA Ops:
  7.2 1.6 %copy-start = (bf16[1024,1024]{1,0:T(8,128)(2,1)S(1)}, bf16[1024,1024]{1,0:T(8,128)(2,1)}, u32[]{:S(2)}) copy-start(bf16[1024,1024]{1,0:T(8,128)(2,1)} %param.14) | copy-start | bytes 6291460
  7.2 39.8 %reduce-scatter.3.cloned.1.call-start = ((), (), s32[]{:S(2)}) async-start(), calls=%async_computation.3 | async-start | bytes 2621440 | tf_op jit(solution)/shard_map/reduce_scatter | solution.py:45
  12.6 0.7 copy-start.4
  12.6 1.9 %copy-start.2 = (bf16[128,3072]{1,0:T(8,128)(2,1)S(1)}, bf16[128,3072]{1,0:T(8,128)(2,1)}, u32[]{:S(2)}) copy-start(bf16[128,3072]{1,0:T(8,128)(2,1)} %param.10) | copy-start | bytes 2359300
  12.6 19.4 %copy-start.3 = (bf16[512,128]{1,0:T(8,128)(2,1)S(1)}, bf16[512,128]{1,0:T(8,128)(2,1)}, u32[]{:S(2)}) copy-start(bf16[512,128]{1,0:T(8,128)(2,1)} %param.12) | copy-start | bytes 393220
  12.7 69.9 %all-gather.2.cloned.1.call-start = ((), (), s32[]{:S(2)}) async-start(), calls=%async_computation.2 | async-start | bytes 1310720 | tf_op jit(solution)/shard_map/all_gather | solution.py:43
  32.7 0.7 copy-start.1
  33.5 74.9 %reduce-scatter.5.cloned.1.call-start = ((), (), s32[]{:S(2)}) async-start(), calls=%async_computation.4 | async-start | bytes 1966080 | tf_op jit(solution)/shard_map/reduce_scatter | solution.py:72
Sparse Core Ops, SparseCore 0:
  12.8 34.1 reduce-scatter.2
  49.1 16.8 all-gather.1
  82.6 25.7 reduce-scatter.4
where the time goes:
time: 117 us
  blocking collectives  46.1 us (39%)
  waiting for transfers between devices  35.9 us (31%)
  between operations  14.5 us (12%)
  matrix products  13.6 us (12%)
  other arithmetic  3.54 us (3%)
  local copies, waits for them, and re-layouts  2.83 us (2%)
    psum x1, blocking collectives, body(): lax.psum(lax.cond(touches(offsets, breadth, 0, span_rows * lax.axis_size(...  30.5 us
    reduce_scatter x1, waiting for transfers between devices, body(): lax.psum_scatter(feature_parts, 'tensor', scatter_dimension=1, tiled=True)  22.4 us
    all_gather x1, blocking collectives, body(): shard_rows = lax.all_gather(reduced, 'seq', axis=0, tiled=True)  15.6 us
    reduce_scatter x1, waiting for transfers between devices, body(): lax.psum_scatter(lax.dot_general(w_up, d_up, (((1,), (1,)), ((), ())), pr...  13.4 us
    dot_general x1, matrix products, body(): lax.dot_general(w_up, d_up, (((1,), (1,)), ((), ())), preferred_element_t...  3.86 us
    dot_general x1, matrix products, body(): jnp.dot(gathered, w_up, preferred_element_type=jnp.float32)  3.45 us
    dot_general x1, matrix products, body(): lax.dot_general(d_reduced, w_in, (((1,), (1,)), ((), ())), preferred_elem...  3.22 us
    unnamed x10, local copies, waits for them, and re-layouts  2.83 us
  transfers between devices with their start and end apart: 3, of which 2 were waited for; matrix products, arithmetic and copies ran while one was open for 10% of the time, Pallas kernels for 0%

commit v1 on v0

v1 whole, which is shorter than its diff:
```python
import jax
import jax.numpy as jnp
from jax import lax
from jax.sharding import PartitionSpec as P


def reach(seq_count, blocks, breadth, span_rows):
    usable = seq_count * span_rows - breadth
    last = seq_count * blocks - 1
    slack = span_rows
    most = 0
    for index in range(seq_count):
        low = max((index * blocks) * usable // last - slack, 0)
        high = min(((index + 1) * blocks - 1) * usable // last + slack, usable) + breadth
        most = max(most, (index - 1) * span_rows - low, high - (index + 2) * span_rows)
    most = max(16, -(-most // 16) * 16)
    assert most <= span_rows
    return most


def shift(value, count, step):
    pairs = [(i, i + step) for i in range(count) if 0 <= i + step < count]
    return lax.ppermute(value, "seq", pairs)


def swap(value, mask):
    return lax.ppermute(value, "tensor", [(i, i ^ mask) for i in range(4)])


def body(spans, w_in, band_weights, offsets, w_up, d_up):
    f32, bf16 = jnp.float32, jnp.bfloat16
    count = lax.axis_size("seq")
    here = lax.axis_index("tensor")
    blocks, breadth = offsets.shape[0], band_weights.shape[1]
    span_rows = spans.shape[0]
    slice_width = w_in.shape[1]
    far = reach(count, blocks, breadth, span_rows)
    length = 3 * span_rows + 2 * far
    anchor = lax.axis_index("seq") * span_rows - span_rows - far
    first = far + span_rows

    def rows_of(matrix, pieces):
        cube = matrix.reshape(4, -1, matrix.shape[1])
        return jnp.concatenate(
            [lax.dynamic_index_in_dim(cube, here ^ k, 0, keepdims=False) for k in pieces], 0
        )

    reduced = jnp.dot(spans, w_in, preferred_element_type=f32).astype(bf16)
    above = shift(reduced, count, 1)
    below = shift(reduced, count, -1)
    far_above = shift(reduced[span_rows - far :], count, 2)
    far_below = shift(reduced[:far], count, -2)

    w_send = rows_of(w_up, (1, 3))
    w_keep = rows_of(w_up, (0, 2))
    over_hidden = (((1,), (1,)), ((), ()))
    grad_sent = lax.dot_general(d_up, w_send, over_hidden, preferred_element_type=f32).astype(bf16)
    grad_got = swap(grad_sent, 1)

    relative = anchor + jnp.arange(length, dtype=jnp.int32)[None, :] - offsets[:, None]
    picker = (relative[:, None, :] == jnp.arange(breadth, dtype=jnp.int32)[None, :, None]).astype(bf16)
    band_cube = band_weights.reshape(blocks, -1, breadth)
    spread = (
        jnp.einsum("bij,bjr->bir", band_cube, picker, preferred_element_type=f32)
        .astype(bf16)
        .reshape(-1, length)
    )

    window = jnp.concatenate([far_above, above, reduced, below, far_below], 0)
    upsampled = jnp.dot(spread, window, preferred_element_type=f32).astype(bf16)
    up_x = swap(upsampled, 2)
    up_core = swap(upsampled, 1)

    grad_kept = lax.dot_general(d_up, w_keep, over_hidden, preferred_element_type=f32)
    grad = (grad_kept + grad_got.astype(f32)).astype(bf16)
    shares = lax.dot_general(spread, grad, (((0,), (0,)), ((), ())), preferred_element_type=f32)
    sent = shares.astype(bf16)
    from_below = shift(sent[far:first], count, -1)
    from_above = shift(sent[first + span_rows : first + 2 * span_rows], count, 1)
    from_far_below = shift(sent[:far], count, -2)
    from_far_above = shift(sent[first + 2 * span_rows :], count, 2)
    total = shares[first : first + span_rows] + from_below.astype(f32) + from_above.astype(f32)
    rest = span_rows - far
    total = total + jnp.pad(from_far_below.astype(f32), ((rest, 0), (0, 0)))
    total = total + jnp.pad(from_far_above.astype(f32), ((0, rest), (0, 0)))

    over_x = swap(total[:, slice_width:].astype(bf16), 2)
    d_reduced = (total[:, :slice_width] + over_x.astype(f32)).astype(bf16)

    def parts(k):
        return lax.dot_general(
            d_reduced, rows_of(w_in, (k,)), over_hidden, preferred_element_type=f32
        )

    part_x = parts(2) + swap(parts(3).astype(bf16), 1).astype(f32)
    other_x = swap(part_x.astype(bf16), 2)
    part = parts(0) + swap(parts(1).astype(bf16), 1).astype(f32)
    d_spans = (part + other_x.astype(f32)).astype(bf16)

    up_x_core = swap(up_x, 1)
    gathered = jnp.concatenate([upsampled, up_core, up_x, up_x_core], 1)
    up_proj = jnp.dot(
        gathered, rows_of(w_up, (0, 1, 2, 3)), preferred_element_type=f32
    ).astype(bf16)
    return (up_proj, d_spans)


def solution(mesh):
    placed = (
        P(("group", "seq"), None),
        P(None, "tensor"),
        P(("group", "seq"), None),
        P(("group", "seq")),
        P(None, "tensor"),
        P(("group", "seq"), "tensor"),
    )
    return jax.shard_map(
        body,
        mesh=mesh,
        in_specs=placed,
        out_specs=(P(("group", "seq"), "tensor"), P(("group", "seq"), "tensor")),
        check_vma=False,
    )
```

time: 117 us -> 69.3 us (0.59)
  blocking collectives: 46.1 us -> 0 us
  starting transfers between devices: 0.12 us -> 32.8 us
  waiting for transfers between devices: 35.9 us -> 8.74 us
  between operations: 14.5 us -> 0.82 us
  local copies, waits for them, and re-layouts: 2.83 us -> 12.1 us
  other arithmetic: 3.54 us -> 1.11 us
    reduce_scatter x2 -> x0, waiting for transfers between devices: 35.8 us -> none  [the longest x1 22.4 us: body(): lax.psum_scatter(feature_parts, 'tensor', scatter_dimension=1, tiled=True)]
    ppermute x0 -> x16, starting transfers between devices: none -> 32.8 us  [the longest x8 27.4 us: shift(): return lax.ppermute(value, 'seq', pairs)]
    psum x1 -> x0, blocking collectives: 30.5 us -> none  [body(): lax.psum(lax.cond(touches(offsets, breadth, 0, span_rows * lax.axis_size(...]
    all_gather x1 -> x0, blocking collectives: 15.6 us -> none  [body(): shard_rows = lax.all_gather(reduced, 'seq', axis=0, tiled=True)]
    ppermute x0 -> x16, waiting for transfers between devices: none -> 8.74 us  [the longest x8 8.72 us: swap(): return lax.ppermute(value, 'tensor', [(i, i ^ mask) for i in range(4)])]
    convert_element_type x2 -> x1, other arithmetic: 2.77 us -> 0.01 us  [body(): d_reduced = (total[:, :slice_width] + over_x.astype(f32)).astype(bf16)]
    unnamed x10 -> x18, local copies, waits for them, and re-layouts: 2.83 us -> 5.5 us
    squeeze x0 -> x1, local copies, waits for them, and re-layouts: none -> 2.61 us  [rows_of(): lax.dynamic_index_in_dim(cube, here ^ k, 0, keepdims=False)]
  transfers between devices with their start and end apart: 3 -> 16, of which waited for: 2 -> 4; matrix products, arithmetic and copies ran while one was open for 10% -> 23% of each run, Pallas kernels for 0% -> 0%
where the time goes in v1:
time: 69.3 us; the launch traced here: 68.7 us
  starting transfers between devices  32.8 us (47%)
  matrix products  13.1 us (19%)
  local copies, waits for them, and re-layouts  12.1 us (17%)
  waiting for transfers between devices  8.74 us (13%)
  other arithmetic  1.11 us (2%)
  between operations  0.82 us (1%)
    ppermute x8, starting transfers between devices, shift(): return lax.ppermute(value, 'seq', pairs)  27.4 us
    ppermute x8, waiting for transfers between devices, swap(): return lax.ppermute(value, 'tensor', [(i, i ^ mask) for i in range(4)])  8.72 us
    unnamed x18, local copies, waits for them, and re-layouts  5.5 us
    ppermute x8, starting transfers between devices, swap(): return lax.ppermute(value, 'tensor', [(i, i ^ mask) for i in range(4)])  5.49 us
    dot_general x1, matrix products, body(): lax.dot_general(spread, grad, (((0,), (0,)), ((), ())), preferred_element...  3.84 us
    squeeze x1, local copies, waits for them, and re-layouts, rows_of(): lax.dynamic_index_in_dim(cube, here ^ k, 0, keepdims=False)  2.61 us
    dot_general x1, matrix products, body(): jnp.dot(gathered, rows_of(w_up, (0, 1, 2, 3)), preferred_element_type=f32)  2.27 us
    dot_general x4, matrix products, parts(): lax.dot_general(d_reduced, rows_of(w_in, (k,)), over_hidden, preferred_el...  1.86 us
  transfers between devices with their start and end apart: 16, of which 4 were waited for; matrix products, arithmetic and copies ran while one was open for 23% of the time, Pallas kernels for 0%

profile of v1, /device:TPU:0, one launch (start us, length us, event | category | flops | bytes accessed | tf_op | source)
XLA Modules:
  0.0 68.7 jit_solution(1596177977110012830)
XLA Ops:
  0.6 0.0 copy-start
  0.6 1.4 %copy-done = bf16[3072,256]{1,0:T(8,128)(2,1)S(1)} copy-done((bf16[3072,256]{1,0:T(8,128)(2,1)S(1)}, bf16[3072,256]{1,0:T(8,128)(2,1)}, u32[]{:S(2)}) %copy-start) | copy-done | bytes 1572888
  2.0 1.5 %convolution_convert_fusion.5 = bf16[128,256]{1,0:T(8,128)(2,1)S(1)} fusion(bf16[128,3072]{1,0:T(8,128)(2,1)} %param.6, bf16[3072,256]{1,0:T(8,128)(2,1)S(1)} %copy-done), kind=kOutput, calls=%fused_computation.22 | convolution fusion | flops 201359360 | bytes 2424832 | tf_op jit(solution)/shard_map/dot_general | solution.py:48
  3.6 1.3 %collective-permute-start.2 = (bf16[128,256]{1,0:T(8,128)(2,1)S(1)}, bf16[128,256]{1,0:T(8,128)(2,1)S(1)}, u32[]{:S(2)}, u32[]{:S(2)}) collective-permute-start(bf16[128,256]{1,0:T(8,128)(2,1)S(1)} %convolution_convert_fusion.5), channel_id=1, source_target_pairs={{4,0},{8,4},{12,8},{5,1},{9,5},{13,9},{6,2},{10,6},{14,10},{7,3},{... | collective-permute-start | bytes 196616 | tf_op jit(solution)/shard_map/ppermute | solution.py:23
  4.9 5.6 %collective-permute-start.1 = (bf16[128,256]{1,0:T(8,128)(2,1)S(1)}, bf16[128,256]{1,0:T(8,128)(2,1)S(1)}, u32[]{:S(2)}, u32[]{:S(2)}) collective-permute-start(bf16[128,256]{1,0:T(8,128)(2,1)S(1)} %convolution_convert_fusion.5), channel_id=1, source_target_pairs={{0,4},{4,8},{8,12},{1,5},{5,9},{9,13},{2,6},{6,10},{10,14},{3,7},{... | collective-permute-start | bytes 196616 | tf_op jit(solution)/shard_map/ppermute | solution.py:23
  10.4 0.6 fusion.61
  11.0 1.3 %collective-permute-start.3 = (bf16[80,256]{1,0:T(8,128)(2,1)S(1)}, bf16[80,256]{1,0:T(8,128)(2,1)}, u32[]{:S(2)}, u32[]{:S(2)}) collective-permute-start(bf16[80,256]{1,0:T(8,128)(2,1)S(1)} %get-tuple-element.10), channel_id=1, source_target_pairs={{8,0},{12,4},{9,1},{13,5},{10,2},{14,6},{11,3},{15,7},{24,16},{28,... | collective-permute-start | bytes 122888 | tf_op jit(solution)/shard_map/ppermute | solution.py:23
  12.3 6.6 %collective-permute-start = (bf16[80,256]{1,0:T(8,128)(2,1)}, bf16[80,256]{1,0:T(8,128)(2,1)}, u32[]{:S(2)}, u32[]{:S(2)}) collective-permute-start(bf16[80,256]{1,0:T(8,128)(2,1)} %get-tuple-element.11), channel_id=1, source_target_pairs={{0,8},{4,12},{1,9},{5,13},{2,10},{6,14},{3,11},{7,15},{16,24},{20,... | collective-permute-start | bytes 122888 | tf_op jit(solution)/shard_map/ppermute | solution.py:23
  19.0 2.6 %dynamic-slice_bitcast_fusion.3 = (bf16[256,1024]{1,0:T(8,128)(2,1)S(1)}, bf16[256,1024]{1,0:T(8,128)(2,1)S(1)}, bf16[256,1024]{1,0:T(8,128)(2,1)}, bf16[256,1024]{1,0:T(8,128)(2,1)S(1)}) fusion(bf16[4,256,1024]{2,1,0:T(8,128)(2,1)} %bitcast.57, s32[]{:T(128)S(6)} %select_n.22, s32[]{:T(128)S(6)} %select_n.25, s32[]{:T(128)S(6)} %select_n.24, s32[]{:T(128)S(6)} %select_n.23), kind=kLoop, calls=%fused_computation.45 | loop fusion | bytes 4194320 | tf_op jit(solution)/shard_map/jit(dynamic_index_in_dim)/squeeze | solution.py:45
  21.6 0.8 %copy-done.2 = bf16[256,1024]{1,0:T(8,128)(2,1)} copy-done((bf16[256,1024]{1,0:T(8,128)(2,1)}, bf16[256,1024]{1,0:T(8,128)(2,1)S(1)}, u32[]{:S(2)}) %copy-start.2) | copy-done | bytes 524312
  22.4 1.5 %fusion.12 = bf16[512,512]{0,1:T(8,128)(2,1)} fusion(bf16[512,1024]{1,0:T(8,128)(2,1)S(1)} %copy-done.6, bf16[256,1024]{1,0:T(8,128)(2,1)S(1)} %get-tuple-element.3, bf16[256,1024]{1,0:T(8,128)(2,1)S(1)} %get-tuple-element.5), kind=kOutput, calls=%fused_computation.13 | convolution fusion | flops 539230208 | bytes 2621440 | tf_op jit(solution)/shard_map/dot_general | solution.py:57
  24.0 0.1 broadcast_subtract_fusion
  24.0 0.7 %fusion.11 = bf16[4,68,8,128]{3,2,1,0:T(8,128)(2,1)S(1)} fusion(bf16[4,128,128]{2,1,0:T(8,128)(2,1)S(1)} %bitcast.58, s32[4,544]{1,0:T(4,128)S(1)} %broadcast_subtract_fusion), kind=kOutput, calls=%fused_computation.12 | convolution fusion | flops 71860224 | bytes 696832 | tf_op jit(solution)/shard_map/bij,bjr->bir/dot_general | solution.py:64
  24.7 1.4 %constant_dynamic-update-slice_fusion.4 = bf16[544,256]{1,0:T(8,128)(2,1)} fusion(bf16[80,256]{1,0:T(8,128)(2,1)} %collective-permute-done), kind=kLoop, calls=%fused_computation.67 | loop fusion | bytes 81920
  26.1 0.6 constant_dynamic-update-slice_fusion.3
  26.8 0.6 constant_dynamic-update-slice_fusion.2
  27.4 0.0 collective-permute-done.2
  27.4 0.6 constant_dynamic-update-slice_fusion.1
  28.0 0.0 collective-permute-done.3
  28.0 1.4 %constant_dynamic-update-slice_fusion = bf16[544,256]{1,0:T(8,128)(2,1)} fusion(bf16[544,256]{1,0:T(8,128)(2,1)} %constant_dynamic-update-slice_fusion.1, bf16[80,256]{1,0:T(8,128)(2,1)} %collective-permute-done.3), kind=kLoop, calls=%fused_computation.63 | loop fusion | bytes 81920 | tf_op jit(solution)/shard_map/concatenate | solution.py:69
  29.4 3.8 %fusion.62 = (bf16[544,512]{1,0:T(8,128)(2,1)}, f32[544,512]{1,0:T(8,128)}) fusion(bf16[512,512]{0,1:T(8,128)(2,1)} %collective-permute-done.7, bf16[512,1024]{1,0:T(8,128)(2,1)} %param.11, bf16[256,1024]{1,0:T(8,128)(2,1)} %get-tuple-element.4, bf16[256,1024]{1,0:T(8,128)(2,1)S(1)} %get-tuple-element.2, bf16[4,68,8,128]{3,2,1,0:T(8,128)(2,1)S(1)} %fusion.11), kind=kOutput, calls=%fused_computation.80 | convolution fusion | flops 825245696 | bytes 4849664 | tf_op jit(solution)/shard_map/dot_general | solution.py:76
  33.3 0.9 %fusion.59 = (bf16[80,512]{1,0:T(8,128)(2,1)S(1)}, bf16[80,512]{1,0:T(8,128)(2,1)S(1)}) fusion(bf16[544,512]{1,0:T(8,128)(2,1)} %get-tuple-element.12), kind=kLoop, calls=%fused_computation.77 | loop fusion | bytes 327680 | tf_op jit(solution)/shard_map/slice | solution.py:80
  34.2 1.0 %fusion.60 = (bf16[128,512]{1,0:T(8,128)(2,1)S(1)}, bf16[128,512]{1,0:T(8,128)(2,1)S(1)}) fusion(bf16[544,512]{1,0:T(8,128)(2,1)} %get-tuple-element.12), kind=kLoop, calls=%fused_computation.78 | loop fusion | bytes 524288 | tf_op jit(solution)/shard_map/slice | solution.py:78
  35.2 1.3 %collective-permute-start.10 = (bf16[80,512]{1,0:T(8,128)(2,1)S(1)}, bf16[80,512]{1,0:T(8,128)(2,1)S(1)}, u32[]{:S(2)}, u32[]{:S(2)}) collective-permute-start(bf16[80,512]{1,0:T(8,128)(2,1)S(1)} %get-tuple-element.6), channel_id=1, source_target_pairs={{8,0},{12,4},{9,1},{13,5},{10,2},{14,6},{11,3},{15,7},{24,16},{28,... | collective-permute-start | bytes 245768 | tf_op jit(solution)/shard_map/ppermute | solution.py:23
  36.5 5.4 %collective-permute-start.11 = (bf16[80,512]{1,0:T(8,128)(2,1)S(1)}, bf16[80,512]{1,0:T(8,128)(2,1)S(1)}, u32[]{:S(2)}, u32[]{:S(2)}) collective-permute-start(bf16[80,512]{1,0:T(8,128)(2,1)S(1)} %get-tuple-element.7), channel_id=1, source_target_pairs={{0,8},{4,12},{1,9},{5,13},{2,10},{6,14},{3,11},{7,15},{16,24},{20,... | collective-permute-start | bytes 245768 | tf_op jit(solution)/shard_map/ppermute | solution.py:23
  42.0 1.3 %collective-permute-start.8 = (bf16[128,512]{1,0:T(8,128)(2,1)S(1)}, bf16[128,512]{1,0:T(8,128)(2,1)S(1)}, u32[]{:S(2)}, u32[]{:S(2)}) collective-permute-start(bf16[128,512]{1,0:T(8,128)(2,1)S(1)} %get-tuple-element.8), channel_id=1, source_target_pairs={{4,0},{8,4},{12,8},{5,1},{9,5},{13,9},{6,2},{10,6},{14,10},{7,3},{... | collective-permute-start | bytes 393224 | tf_op jit(solution)/shard_map/ppermute | solution.py:23
  43.3 4.6 %collective-permute-start.9 = (bf16[128,512]{1,0:T(8,128)(2,1)S(1)}, bf16[128,512]{1,0:T(8,128)(2,1)S(1)}, u32[]{:S(2)}, u32[]{:S(2)}) collective-permute-start(bf16[128,512]{1,0:T(8,128)(2,1)S(1)} %get-tuple-element.9), channel_id=1, source_target_pairs={{0,4},{4,8},{8,12},{1,5},{5,9},{9,13},{2,6},{6,10},{10,14},{3,7},{... | collective-permute-start | bytes 393224 | tf_op jit(solution)/shard_map/ppermute | solution.py:23
  47.8 1.4 %convolution_convert_fusion.2 = bf16[512,256]{0,1:T(8,128)(2,1)S(1)} fusion(bf16[544,256]{1,0:T(8,128)(2,1)} %constant_dynamic-update-slice_fusion, bf16[4,68,8,128]{3,2,1,0:T(8,128)(2,1)S(1)} %fusion.11), kind=kOutput, calls=%fused_computation.16 | convolution fusion | flops 142737408 | bytes 1097728 | tf_op jit(solution)/shard_map/dot_general | solution.py:70
  49.2 2.0 %collective-permute-start.5 = (bf16[512,256]{0,1:T(8,128)(2,1)S(1)}, bf16[512,256]{0,1:T(8,128)(2,1)S(1)}, u32[]{:S(2)}, u32[]{:S(2)}) collective-permute-start(bf16[512,256]{0,1:T(8,128)(2,1)S(1)} %convolution_convert_fusion.2), channel_id=1, source_target_pairs={{0,2},{1,3},{2,0},{3,1},{4,6},{5,7},{6,4},{7,5},{8,10},{9,11},{10,... | collective-permute-start | bytes 786440 | tf_op jit(solution)/shard_map/ppermute | solution.py:27
  51.2 0.0 collective-permute-done.10
  51.2 0.0 collective-permute-done.11
  51.2 0.0 collective-permute-done.8
  51.3 1.0 %fusion.49 = f32[128,512]{1,0:T(8,128)S(1)} fusion(f32[544,512]{1,0:T(8,128)} %get-tuple-element.13, bf16[128,512]{1,0:T(8,128)(2,1)S(1)} %collective-permute-done.9, bf16[128,512]{1,0:T(8,128)(2,1)S(1)} %collective-permute-done.8, bf16[80,512]{1,0:T(8,128)(2,1)S(1)} %collective-permute-done.11, bf16[80,512]{1,0:T(8,128)(2,1)S(1)} %collective-permute-done.10), kind=kLoop, calls=%fused_computation.59 | loop fusion | flops 524288 | bytes 950272 | tf_op jit(solution)/shard_map/add | solution.py:85
  52.3 1.1 %collective-permute-start.12 = (bf16[128,256]{1,0:T(8,128)(2,1)S(1)}, bf16[128,256]{1,0:T(8,128)(2,1)S(1)}, u32[]{:S(2)}, u32[]{:S(2)}) collective-permute-start(bf16[128,256]{1,0:T(8,128)(2,1)S(1)} %slice.57), channel_id=1, source_target_pairs={{0,2},{1,3},{2,0},{3,1},{4,6},{5,7},{6,4},{7,5},{8,10},{9,11},{10,... | collective-permute-start | bytes 196616 | tf_op jit(solution)/shard_map/ppermute | solution.py:27
  53.4 0.0 collective-permute-start.4
  53.4 4.4 %collective-permute-done.5 = bf16[512,256]{0,1:T(8,128)(2,1)S(1)} collective-permute-done((bf16[512,256]{0,1:T(8,128)(2,1)S(1)}, bf16[512,256]{0,1:T(8,128)(2,1)S(1)}, u32[]{:S(2)}, u32[]{:S(2)}) %collective-permute-start.5) | collective-permute-done | bytes 262176 | tf_op jit(solution)/shard_map/ppermute | solution.py:27
  57.9 0.0 collective-permute-start.6
  57.9 0.7 %collective-permute-done.12 = bf16[128,256]{1,0:T(8,128)(2,1)S(1)} collective-permute-done((bf16[128,256]{1,0:T(8,128)(2,1)S(1)}, bf16[128,256]{1,0:T(8,128)(2,1)S(1)}, u32[]{:S(2)}, u32[]{:S(2)}) %collective-permute-start.12) | collective-permute-done | bytes 65568 | tf_op jit(solution)/shard_map/ppermute | solution.py:27
  58.6 0.3 convolution_convert_fusion.3
  58.9 0.1 collective-permute-start.14
  59.0 0.3 convolution_convert_fusion.4
  59.3 0.6 collective-permute-start.13
  59.8 0.6 collective-permute-done.14
  60.4 0.3 fusion.15
  60.7 1.7 %collective-permute-start.15 = (bf16[128,768]{1,0:T(8,128)(2,1)S(1)}, bf16[128,768]{1,0:T(8,128)(2,1)S(1)}, u32[]{:S(2)}, u32[]{:S(2)}) collective-permute-start(bf16[128,768]{1,0:T(8,128)(2,1)S(1)} %fusion.15), channel_id=1, source_target_pairs={{0,2},{1,3},{2,0},{3,1},{4,6},{5,7},{6,4},{7,5},{8,10},{9,11},{10,... | collective-permute-start | bytes 589832 | tf_op jit(solution)/shard_map/ppermute | solution.py:27
  62.4 2.3 %fusion.8 = bf16[512,1024]{1,0:T(8,128)(2,1)} fusion(bf16[256,1024]{1,0:T(8,128)(2,1)S(1)} %get-tuple-element.3, bf16[256,1024]{1,0:T(8,128)(2,1)S(1)} %copy-done.1, bf16[256,1024]{1,0:T(8,128)(2,1)S(1)} %copy-done.3, bf16[256,1024]{1,0:T(8,128)(2,1)S(1)} %get-tuple-element.2, bf16[512,256]{0,1:T(8,128)(2,1)S(1)} %collective-permute-done.6, ...), kind=kOutput, calls=%fused_computation.8 | convolution fusion | flops 1086849024 | bytes 4194304 | tf_op jit(solution)/shard_map/dot_general | solution.py:102
  64.7 3.0 %collective-permute-done.15 = bf16[128,768]{1,0:T(8,128)(2,1)S(1)} collective-permute-done((bf16[128,768]{1,0:T(8,128)(2,1)S(1)}, bf16[128,768]{1,0:T(8,128)(2,1)S(1)}, u32[]{:S(2)}, u32[]{:S(2)}) %collective-permute-start.15) | collective-permute-done | bytes 196640 | tf_op jit(solution)/shard_map/ppermute | solution.py:27
  67.7 1.0 %fusion.14 = bf16[128,768]{1,0:T(8,128)(2,1)} fusion(bf16[128,256]{1,0:T(8,128)(2,1)S(1)} %fusion.50, bf16[128,768]{1,0:T(8,128)(2,1)S(1)} %collective-permute-done.15, bf16[128,768]{1,0:T(8,128)(2,1)S(1)} %collective-permute-done.13, bf16[4,768,256]{2,1,0:T(8,128)(2,1)S(1)} %bitcast.53, s32[]{:T(128)S(6)} %select_n.22), kind=kOutput, calls=%fused_computation.18 | convolution fusion | flops 50823168 | bytes 1048580 | tf_op jit(solution)/shard_map/dot_general | solution.py:91
  (22 shorter events, 0.1 us)
Async XLA Ops:
  0.6 1.4 %copy-start = (bf16[3072,256]{1,0:T(8,128)(2,1)S(1)}, bf16[3072,256]{1,0:T(8,128)(2,1)}, u32[]{:S(2)}) copy-start(bf16[3072,256]{1,0:T(8,128)(2,1)} %param.7) | copy-start | bytes 4718596
  3.6 23.8 %collective-permute-start.2 = (bf16[128,256]{1,0:T(8,128)(2,1)S(1)}, bf16[128,256]{1,0:T(8,128)(2,1)S(1)}, u32[]{:S(2)}, u32[]{:S(2)}) collective-permute-start(bf16[128,256]{1,0:T(8,128)(2,1)S(1)} %convolution_convert_fusion.5), channel_id=1, source_target_pairs={{4,0},{8,4},{12,8},{5,1},{9,5},{13,9},{6,2},{10,6},{14,10},{7,3},{... | collective-permute-start | bytes 196616 | tf_op jit(solution)/shard_map/ppermute | solution.py:23
  4.9 21.3 %collective-permute-start.1 = (bf16[128,256]{1,0:T(8,128)(2,1)S(1)}, bf16[128,256]{1,0:T(8,128)(2,1)S(1)}, u32[]{:S(2)}, u32[]{:S(2)}) collective-permute-start(bf16[128,256]{1,0:T(8,128)(2,1)S(1)} %convolution_convert_fusion.5), channel_id=1, source_target_pairs={{0,4},{4,8},{8,12},{1,5},{5,9},{9,13},{2,6},{6,10},{10,14},{3,7},{... | collective-permute-start | bytes 196616 | tf_op jit(solution)/shard_map/ppermute | solution.py:23
  11.0 17.0 %collective-permute-start.3 = (bf16[80,256]{1,0:T(8,128)(2,1)S(1)}, bf16[80,256]{1,0:T(8,128)(2,1)}, u32[]{:S(2)}, u32[]{:S(2)}) collective-permute-start(bf16[80,256]{1,0:T(8,128)(2,1)S(1)} %get-tuple-element.10), channel_id=1, source_target_pairs={{8,0},{12,4},{9,1},{13,5},{10,2},{14,6},{11,3},{15,7},{24,16},{28,... | collective-permute-start | bytes 122888 | tf_op jit(solution)/shard_map/ppermute | solution.py:23
  12.3 12.4 %collective-permute-start = (bf16[80,256]{1,0:T(8,128)(2,1)}, bf16[80,256]{1,0:T(8,128)(2,1)}, u32[]{:S(2)}, u32[]{:S(2)}) collective-permute-start(bf16[80,256]{1,0:T(8,128)(2,1)} %get-tuple-element.11), channel_id=1, source_target_pairs={{0,8},{4,12},{1,9},{5,13},{2,10},{6,14},{3,11},{7,15},{16,24},{20,... | collective-permute-start | bytes 122888 | tf_op jit(solution)/shard_map/ppermute | solution.py:23
  19.0 3.4 %copy-start.6 = (bf16[512,1024]{1,0:T(8,128)(2,1)S(1)}, bf16[512,1024]{1,0:T(8,128)(2,1)}, u32[]{:S(2)}) copy-start(bf16[512,1024]{1,0:T(8,128)(2,1)} %param.11) | copy-start | bytes 3145732
  21.6 0.8 %copy-start.2 = (bf16[256,1024]{1,0:T(8,128)(2,1)}, bf16[256,1024]{1,0:T(8,128)(2,1)S(1)}, u32[]{:S(2)}) copy-start(bf16[256,1024]{1,0:T(8,128)(2,1)S(1)} %get-tuple-element.5) | copy-start | bytes 1572868
  21.6 2.4 %copy-start.5 = (s32[4]{0:T(128)S(1)}, s32[4]{0:T(128)}, u32[]{:S(2)}) copy-start(s32[4]{0:T(128)} %param.9) | copy-start | bytes 52
  21.6 2.4 %copy-start.4 = (bf16[512,128]{1,0:T(8,128)(2,1)S(1)}, bf16[512,128]{1,0:T(8,128)(2,1)}, u32[]{:S(2)}) copy-start(bf16[512,128]{1,0:T(8,128)(2,1)} %param.8) | copy-start | bytes 393220
  23.9 5.5 %collective-permute-start.7 = (bf16[512,512]{0,1:T(8,128)(2,1)}, bf16[512,512]{0,1:T(8,128)(2,1)}, u32[]{:S(2)}, u32[]{:S(2)}) collective-permute-start(bf16[512,512]{0,1:T(8,128)(2,1)} %fusion.12), channel_id=1, source_target_pairs={{0,1},{1,0},{2,3},{3,2},{4,5},{5,4},{6,7},{7,6},{8,9},{9,8},{10,11... | collective-permute-start | bytes 1572872 | tf_op jit(solution)/shard_map/ppermute | solution.py:27
  35.2 16.0 %collective-permute-start.10 = (bf16[80,512]{1,0:T(8,128)(2,1)S(1)}, bf16[80,512]{1,0:T(8,128)(2,1)S(1)}, u32[]{:S(2)}, u32[]{:S(2)}) collective-permute-start(bf16[80,512]{1,0:T(8,128)(2,1)S(1)} %get-tuple-element.6), channel_id=1, source_target_pairs={{8,0},{12,4},{9,1},{13,5},{10,2},{14,6},{11,3},{15,7},{24,16},{28,... | collective-permute-start | bytes 245768 | tf_op jit(solution)/shard_map/ppermute | solution.py:23
  36.5 14.7 %collective-permute-start.11 = (bf16[80,512]{1,0:T(8,128)(2,1)S(1)}, bf16[80,512]{1,0:T(8,128)(2,1)S(1)}, u32[]{:S(2)}, u32[]{:S(2)}) collective-permute-start(bf16[80,512]{1,0:T(8,128)(2,1)S(1)} %get-tuple-element.7), channel_id=1, source_target_pairs={{0,8},{4,12},{1,9},{5,13},{2,10},{6,14},{3,11},{7,15},{16,24},{20,... | collective-permute-start | bytes 245768 | tf_op jit(solution)/shard_map/ppermute | solution.py:23
  42.0 9.3 %collective-permute-start.8 = (bf16[128,512]{1,0:T(8,128)(2,1)S(1)}, bf16[128,512]{1,0:T(8,128)(2,1)S(1)}, u32[]{:S(2)}, u32[]{:S(2)}) collective-permute-start(bf16[128,512]{1,0:T(8,128)(2,1)S(1)} %get-tuple-element.8), channel_id=1, source_target_pairs={{4,0},{8,4},{12,8},{5,1},{9,5},{13,9},{6,2},{10,6},{14,10},{7,3},{... | collective-permute-start | bytes 393224 | tf_op jit(solution)/shard_map/ppermute | solution.py:23
  43.3 8.0 %collective-permute-start.9 = (bf16[128,512]{1,0:T(8,128)(2,1)S(1)}, bf16[128,512]{1,0:T(8,128)(2,1)S(1)}, u32[]{:S(2)}, u32[]{:S(2)}) collective-permute-start(bf16[128,512]{1,0:T(8,128)(2,1)S(1)} %get-tuple-element.9), channel_id=1, source_target_pairs={{0,4},{4,8},{8,12},{1,5},{5,9},{9,13},{2,6},{6,10},{10,14},{3,7},{... | collective-permute-start | bytes 393224 | tf_op jit(solution)/shard_map/ppermute | solution.py:23
  49.2 13.2 %copy-start.1 = (bf16[256,1024]{1,0:T(8,128)(2,1)S(1)}, bf16[256,1024]{1,0:T(8,128)(2,1)}, u32[]{:S(2)}) copy-start(bf16[256,1024]{1,0:T(8,128)(2,1)} %get-tuple-element.4) | copy-start | bytes 1572868
  49.2 13.2 %copy-start.3 = (bf16[256,1024]{1,0:T(8,128)(2,1)S(1)}, bf16[256,1024]{1,0:T(8,128)(2,1)}, u32[]{:S(2)}) copy-start(bf16[256,1024]{1,0:T(8,128)(2,1)} %copy-done.2) | copy-start | bytes 1572868
  49.2 8.6 %collective-permute-start.5 = (bf16[512,256]{0,1:T(8,128)(2,1)S(1)}, bf16[512,256]{0,1:T(8,128)(2,1)S(1)}, u32[]{:S(2)}, u32[]{:S(2)}) collective-permute-start(bf16[512,256]{0,1:T(8,128)(2,1)S(1)} %convolution_convert_fusion.2), channel_id=1, source_target_pairs={{0,2},{1,3},{2,0},{3,1},{4,6},{5,7},{6,4},{7,5},{8,10},{9,11},{10,... | collective-permute-start | bytes 786440 | tf_op jit(solution)/shard_map/ppermute | solution.py:27
  52.3 6.3 %collective-permute-start.12 = (bf16[128,256]{1,0:T(8,128)(2,1)S(1)}, bf16[128,256]{1,0:T(8,128)(2,1)S(1)}, u32[]{:S(2)}, u32[]{:S(2)}) collective-permute-start(bf16[128,256]{1,0:T(8,128)(2,1)S(1)} %slice.57), channel_id=1, source_target_pairs={{0,2},{1,3},{2,0},{3,1},{4,6},{5,7},{6,4},{7,5},{8,10},{9,11},{10,... | collective-permute-start | bytes 196616 | tf_op jit(solution)/shard_map/ppermute | solution.py:27
  53.4 9.0 %collective-permute-start.4 = (bf16[512,256]{0,1:T(8,128)(2,1)S(1)}, bf16[512,256]{0,1:T(8,128)(2,1)S(1)}, u32[]{:S(2)}, u32[]{:S(2)}) collective-permute-start(bf16[512,256]{0,1:T(8,128)(2,1)S(1)} %convolution_convert_fusion.2), channel_id=1, source_target_pairs={{0,1},{1,0},{2,3},{3,2},{4,5},{5,4},{6,7},{7,6},{8,9},{9,8},{10,11... | collective-permute-start | bytes 786440 | tf_op jit(solution)/shard_map/ppermute | solution.py:27
  57.9 4.5 %collective-permute-start.6 = (bf16[512,256]{0,1:T(8,128)(2,1)S(1)}, bf16[512,256]{0,1:T(8,128)(2,1)S(1)}, u32[]{:S(2)}, u32[]{:S(2)}) collective-permute-start(bf16[512,256]{0,1:T(8,128)(2,1)S(1)} %collective-permute-done.5), channel_id=1, source_target_pairs={{0,1},{1,0},{2,3},{3,2},{4,5},{5,4},{6,7},{7,6},{8,9},{9,8},{10,11... | collective-permute-start | bytes 786440 | tf_op jit(solution)/shard_map/ppermute | solution.py:27
  58.9 1.5 %collective-permute-start.14 = (bf16[128,768]{1,0:T(8,128)(2,1)S(1)}, bf16[128,768]{1,0:T(8,128)(2,1)S(1)}, u32[]{:S(2)}, u32[]{:S(2)}) collective-permute-start(bf16[128,768]{1,0:T(8,128)(2,1)S(1)} %convolution_convert_fusion.3), channel_id=1, source_target_pairs={{0,1},{1,0},{2,3},{3,2},{4,5},{5,4},{6,7},{7,6},{8,9},{9,8},{10,11... | collective-permute-start | bytes 589832 | tf_op jit(solution)/shard_map/ppermute | solution.py:27
  59.3 5.4 %collective-permute-start.13 = (bf16[128,768]{1,0:T(8,128)(2,1)S(1)}, bf16[128,768]{1,0:T(8,128)(2,1)S(1)}, u32[]{:S(2)}, u32[]{:S(2)}) collective-permute-start(bf16[128,768]{1,0:T(8,128)(2,1)S(1)} %convolution_convert_fusion.4), channel_id=1, source_target_pairs={{0,1},{1,0},{2,3},{3,2},{4,5},{5,4},{6,7},{7,6},{8,9},{9,8},{10,11... | collective-permute-start | bytes 589832 | tf_op jit(solution)/shard_map/ppermute | solution.py:27
  60.7 7.0 %collective-permute-start.15 = (bf16[128,768]{1,0:T(8,128)(2,1)S(1)}, bf16[128,768]{1,0:T(8,128)(2,1)S(1)}, u32[]{:S(2)}, u32[]{:S(2)}) collective-permute-start(bf16[128,768]{1,0:T(8,128)(2,1)S(1)} %fusion.15), channel_id=1, source_target_pairs={{0,2},{1,3},{2,0},{3,1},{4,6},{5,7},{6,4},{7,5},{8,10},{9,11},{10,... | collective-permute-start | bytes 589832 | tf_op jit(solution)/shard_map/ppermute | solution.py:27

commit v2 on v0

v2 whole, which is shorter than its diff:
```python
import jax
import jax.numpy as jnp
from jax import lax
from jax.experimental import pallas as pl
from jax.experimental.pallas import tpu as pltpu
from jax.sharding import PartitionSpec as P

F32, BF16 = jnp.float32, jnp.bfloat16
NOWHERE = -(1 << 20)


def reach(count, blocks, breadth, span_rows):
    usable = count * span_rows - breadth
    last = count * blocks - 1
    most = 0
    for index in range(count):
        low = max(index * blocks * usable // last - span_rows, 0)
        high = min(((index + 1) * blocks - 1) * usable // last + span_rows, usable) + breadth
        most = max(most, (index - 1) * span_rows - low, high - (index + 2) * span_rows)
    most = max(16, -(-most // 16) * 16)
    assert most <= span_rows
    return most


def pairings(count):
    found = []
    for distance in (1, 2):
        for parity in (0, 1):
            if any(partner(i, distance, parity, count) != i for i in range(count)):
                found.append((distance, parity))
    return found


def partner(index, distance, parity, count):
    up = (index // distance) % 2 == parity
    other = index + distance if up else index - distance
    return other if 0 <= other < count else index


def partner_here(distance, parity, count):
    index = lax.axis_index("seq")
    up = lax.rem(lax.div(index, distance), 2) == parity
    other = jnp.where(up, index + distance, index - distance)
    return other, up, (other >= 0) & (other < count)


def trade(value, pairing, count):
    return lax.ppermute(value, "seq", [(i, partner(i, *pairing, count)) for i in range(count)])


def swap(value, mask):
    return lax.ppermute(value, "tensor", [(i, i ^ mask) for i in range(4)])


def call(kernel, outs, *args, flops, scalars=()):
    moved = sum(a.size * a.dtype.itemsize for a in args)
    moved += sum(o.size * o.dtype.itemsize for o in outs)
    spaces = [pltpu.SMEM if k in scalars else pltpu.VMEM for k in range(len(args))]
    got = pl.pallas_call(
        kernel,
        out_shape=outs,
        in_specs=[pl.BlockSpec(memory_space=s) for s in spaces],
        out_specs=[pl.BlockSpec(memory_space=pltpu.VMEM) for _ in outs],
        compiler_params=pltpu.CompilerParams(vmem_limit_bytes=16 << 20),
        cost_estimate=pl.CostEstimate(flops=flops, bytes_accessed=moved, transcendentals=0),
    )(*args)
    return got


def shape(dims, kind=BF16):
    return jax.ShapeDtypeStruct(dims, kind)


def dot(a, b):
    return jnp.dot(a, b, preferred_element_type=F32)


def dot_t(a, b):
    return lax.dot_general(a, b, (((1,), (1,)), ((), ())), preferred_element_type=F32)


def body(spans, w_in, band_weights, offsets, w_up, d_up):
    count = lax.axis_size("seq")
    groups = lax.axis_size("group")
    blocks, breadth = offsets.shape[0], band_weights.shape[1]
    bytes_here, hidden = d_up.shape
    block = bytes_here // blocks
    span_rows, depth = spans.shape
    width = w_in.shape[1]
    share = depth // 4
    far = reach(count, blocks, breadth, span_rows)
    pairs = pairings(count)
    rows = [span_rows] + [span_rows if d == 1 else far for d, _ in pairs]
    cols = [breadth * k for k in range(len(rows))]
    longs = [p for p in pairs if p[0] == 2]

    def cut_at(distance, parity):
        _, up, _ = partner_here(distance, parity, count)
        return pl.multiple_of(jnp.where(up, span_rows - far, 0), 16)

    def block_of(ref, mask, size):
        at = (lax.axis_index("tensor") ^ mask) * size
        return ref[pl.ds(pl.multiple_of(at, size), size), :]

    here = lax.axis_index("tensor")
    cube = w_in.reshape(4, share, width)

    def quarter(index):
        return lax.dynamic_index_in_dim(cube, index, 0, keepdims=False)

    half = lax.axis_index("group") if groups == 2 else 0
    w_core = swap(quarter(here ^ 1), 1)
    if groups == 2:
        w_x = swap(quarter((here ^ 2) ^ half), 2)
        ring = []
        for t in range(4):
            ring += [(t, 4 + t), (4 + t, t ^ 1)]
        w_ring = lax.ppermute(w_x, ("group", "tensor"), ring)
        w_side = swap(w_x, 1)
    else:
        w_x = swap(quarter(here ^ 2), 2)
        w_ring = swap(quarter(here ^ 3), 3)
        w_side = w_ring

    def project(spans_ref, w_ref, out_ref, *cut_refs):
        out_ref[...] = dot(spans_ref[...], w_ref[...]).astype(BF16)
        for ref, pairing in zip(cut_refs, longs):
            ref[...] = out_ref[pl.ds(cut_at(*pairing), far), :]

    reduced, *cuts = call(
        project,
        [shape((span_rows, width))] + [shape((far, width)) for _ in longs],
        spans,
        w_in,
        flops=2 * span_rows * depth * width,
    )
    sends = [reduced for _ in pairs if _[0] == 1] + cuts
    pieces = [reduced] + [trade(s, p, count) for s, p in zip(sends, pairs)]

    def grad_part(masks, kind):
        def kernel(d_ref, w_ref, out_ref):
            for k, mask in enumerate(masks):
                part = dot_t(d_ref[...], block_of(w_ref, mask, width))
                out_ref[:, k * width : (k + 1) * width] = part.astype(kind)

        return call(
            kernel,
            [shape((bytes_here, 2 * width), kind)],
            d_up,
            w_up,
            flops=4 * bytes_here * width * hidden,
        )[0]

    grad_got = swap(grad_part((1, 3), BF16), 1)
    grad_kept = grad_part((0, 2), F32)

    def spread(off_ref, weights_ref, band_ref, turned_ref):
        starts = [lax.axis_index("seq") * span_rows]
        for distance, parity in pairs:
            other, up, there = partner_here(distance, parity, count)
            skip = 0 if distance == 1 else jnp.where(up, 0, span_rows - far)
            starts.append(jnp.where(there, other * span_rows + skip, NOWHERE))
        down = lax.broadcasted_iota(jnp.int32, (breadth, breadth), 0)
        across = lax.broadcasted_iota(jnp.int32, (breadth, breadth), 1)
        for b in range(blocks):
            part = slice(b * block, (b + 1) * block)
            weights = weights_ref[part, :]
            for k, (start, size) in enumerate(zip(starts, rows)):
                piece = slice(cols[k], cols[k] + breadth)
                gap = start - off_ref[b]
                pick = ((across + gap == down) & (across < size)).astype(F32).astype(BF16)
                band_ref[part, piece] = dot(weights, pick).astype(BF16)
                pick = ((down + gap == across) & (down < size)).astype(F32).astype(BF16)
                turned_ref[piece, part] = dot_t(pick, weights).astype(BF16)

    total_cols = breadth * len(rows)
    band, turned = call(
        spread,
        [shape((bytes_here, total_cols)), shape((total_cols, bytes_here))],
        offsets,
        band_weights,
        flops=4 * bytes_here * breadth * total_cols,
        scalars=(0,),
    )

    def spread_grad(kept_ref, got_ref, turned_ref, own_ref, *out_refs):
        grad = (kept_ref[...] + got_ref[...].astype(F32)).astype(BF16)
        for k, ref in enumerate((own_ref,) + out_refs):
            part = dot(turned_ref[cols[k] : cols[k] + rows[k], :], grad)
            ref[...] = part.astype(ref.dtype)

    own, *shares = call(
        spread_grad,
        [shape((r, 2 * width), F32 if k == 0 else BF16) for k, r in enumerate(rows)],
        grad_kept,
        grad_got,
        turned,
        flops=4 * bytes_here * width * sum(rows),
    )
    came = [trade(s, p, count) for s, p in zip(shares, pairs)]

    def upsample(band_ref, *refs):
        *piece_refs, out_ref = refs
        acc = 0.0
        for k, ref in enumerate(piece_refs):
            acc += dot(band_ref[:, cols[k] : cols[k] + rows[k]], ref[...])
        out_ref[...] = acc.astype(BF16)

    (upsampled,) = call(
        upsample,
        [shape((bytes_here, width))],
        band,
        *pieces,
        flops=2 * bytes_here * width * sum(rows),
    )
    up_x = swap(upsampled, 2)
    up_core = swap(upsampled, 1)
    up_both = swap(up_x, 1)

    def collect(own_ref, *refs):
        *came_refs, sum_ref, sent_ref = refs
        sum_ref[...] = own_ref[...]
        for ref, (distance, parity) in zip(came_refs, pairs):
            if distance == 1:
                sum_ref[...] += ref[...].astype(F32)
            else:
                sum_ref[pl.ds(cut_at(distance, parity), far), :] += ref[...].astype(F32)
        sent_ref[:, width:] = sum_ref[:, :width].astype(BF16)
        sent_ref[:, :width] = sum_ref[:, width:].astype(BF16)

    summed, sent = call(
        collect,
        [shape((span_rows, 2 * width), F32), shape((span_rows, 2 * width))],
        own,
        *came,
        flops=8 * span_rows * width,
    )
    d_reduced = (summed + swap(sent, 2).astype(F32)).astype(BF16)
    d_other = swap(d_reduced, 1)

    def finish(mine_ref, other_ref, w_ref, core_ref, x_ref, ring_ref, side_ref, out_ref):
        acc = dot_t(mine_ref[:, :width], block_of(w_ref, 0, share))
        acc += dot_t(other_ref[:, :width], core_ref[...])
        if groups == 2:
            first = lax.axis_index("group") == 0
            near = jnp.where(first, x_ref[...], ring_ref[...])
            cross = jnp.where(first, ring_ref[...], side_ref[...])
        else:
            near, cross = x_ref[...], ring_ref[...]
        acc += dot_t(mine_ref[:, width:], near)
        acc += dot_t(other_ref[:, width:], cross)
        out_ref[...] = acc.astype(BF16)

    (d_spans,) = call(
        finish,
        [shape((span_rows, share))],
        d_reduced,
        d_other,
        w_in,
        w_core,
        w_x,
        w_ring,
        w_side,
        flops=8 * span_rows * width * share,
    )

    def up_project(a_ref, b_ref, c_ref, d_ref, w_ref, out_ref):
        acc = 0.0
        for mask, ref in enumerate((a_ref, b_ref, c_ref, d_ref)):
            acc += dot(ref[...], block_of(w_ref, mask, width))
        out_ref[...] = acc.astype(BF16)

    (up_proj,) = call(
        up_project,
        [shape((bytes_here, hidden))],
        upsampled,
        up_core,
        up_x,
        up_both,
        w_up,
        flops=8 * bytes_here * width * hidden,
    )
    return (up_proj, d_spans)


def solution(mesh):
    placed = (
        P(("group", "seq"), None),
        P(None, "tensor"),
        P(("group", "seq"), None),
        P(("group", "seq")),
        P(None, "tensor"),
        P(("group", "seq"), "tensor"),
    )
    return jax.shard_map(
        body,
        mesh=mesh,
        in_specs=placed,
        out_specs=(P(("group", "seq"), "tensor"), P(("group", "seq"), "tensor")),
        check_vma=False,
    )
```

time: 117 us -> 44.5 us (0.38)
  blocking collectives: 46.1 us -> 0 us
  waiting for transfers between devices: 35.9 us -> 12 us
  starting transfers between devices: 0.12 us -> 20.8 us
  between operations: 14.5 us -> 0.77 us
  matrix products: 13.6 us -> 0 us
  Pallas kernels: 0 us -> 7.63 us
  other arithmetic: 3.54 us -> 0.03 us
    reduce_scatter x2 -> x0, waiting for transfers between devices: 35.8 us -> none  [the longest x1 22.4 us: body(): lax.psum_scatter(feature_parts, 'tensor', scatter_dimension=1, tiled=True)]
    psum x1 -> x0, blocking collectives: 30.5 us -> none  [body(): lax.psum(lax.cond(touches(offsets, breadth, 0, span_rows * lax.axis_size(...]
    ppermute x0 -> x16, starting transfers between devices: none -> 20.8 us  [the longest x6 12.6 us: trade(): lax.ppermute(value, 'seq', [(i, partner(i, *pairing, count)) for i in ran...]
    all_gather x1 -> x0, blocking collectives: 15.6 us -> none  [body(): shard_rows = lax.all_gather(reduced, 'seq', axis=0, tiled=True)]
    dot_general x8 -> x0, matrix products: 13.6 us -> none  [the longest x1 3.86 us: body(): lax.dot_general(w_up, d_up, (((1,), (1,)), ((), ())), preferred_element_t...]
    ppermute x0 -> x16, waiting for transfers between devices: none -> 12 us  [the longest x6 5.1 us: trade(): lax.ppermute(value, 'seq', [(i, partner(i, *pairing, count)) for i in ran...]
    pallas_call x0 -> x9, Pallas kernels: none -> 7.63 us  [call(): pl.pallas_call(kernel, out_shape=outs, in_specs=[pl.BlockSpec(memory_spac...]
    convert_element_type x2 -> x1, other arithmetic: 2.77 us -> 0.03 us  [body(): d_reduced = (summed + swap(sent, 2).astype(F32)).astype(BF16)]
  transfers between devices with their start and end apart: 3 -> 16, of which waited for: 2 -> 5; matrix products, arithmetic and copies ran while one was open for 10% -> 0% of each run, Pallas kernels for 0% -> 13%
where the time goes in v2:
time: 44.5 us; the launch traced here: 44.3 us
  starting transfers between devices  20.8 us (47%)
  waiting for transfers between devices  12 us (27%)
  Pallas kernels  7.63 us (17%)
  local copies, waits for them, and re-layouts  3.02 us (7%)
  between operations  0.77 us (2%)
    ppermute x6, starting transfers between devices, trade(): lax.ppermute(value, 'seq', [(i, partner(i, *pairing, count)) for i in ran...  12.6 us
    pallas_call x9, Pallas kernels, call(): pl.pallas_call(kernel, out_shape=outs, in_specs=[pl.BlockSpec(memory_spac...  7.63 us
    ppermute x9, starting transfers between devices, swap(): return lax.ppermute(value, 'tensor', [(i, i ^ mask) for i in range(4)])  6.75 us
    ppermute x6, waiting for transfers between devices, trade(): lax.ppermute(value, 'seq', [(i, partner(i, *pairing, count)) for i in ran...  5.1 us
    ppermute x1, waiting for transfers between devices, body(): w_ring = lax.ppermute(w_x, ('group', 'tensor'), ring)  4.5 us
    unnamed x16, local copies, waits for them, and re-layouts  2.97 us
    ppermute x9, waiting for transfers between devices, swap(): return lax.ppermute(value, 'tensor', [(i, i ^ mask) for i in range(4)])  2.39 us
    ppermute x1, starting transfers between devices, body(): w_ring = lax.ppermute(w_x, ('group', 'tensor'), ring)  1.51 us
  transfers between devices with their start and end apart: 16, of which 5 were waited for; matrix products, arithmetic and copies ran while one was open for 0% of the time, Pallas kernels for 13%

profile of v2, /device:TPU:0, one launch (start us, length us, event | category | flops | bytes accessed | tf_op | source)
XLA Modules:
  0.0 44.3 jit_solution(8754182752269060203)
XLA Ops:
  0.6 0.0 copy-start
  0.6 1.6 %copy-done = bf16[1024,1024]{1,0:T(8,128)(2,1)S(1)} copy-done((bf16[1024,1024]{1,0:T(8,128)(2,1)S(1)}, bf16[1024,1024]{1,0:T(8,128)(2,1)}, u32[]{:S(2)}) %copy-start) | copy-done | bytes 2097176
  2.2 1.2 %copy-done.3 = bf16[512,1024]{1,0:T(8,128)(2,1)S(1)} copy-done((bf16[512,1024]{1,0:T(8,128)(2,1)S(1)}, bf16[512,1024]{1,0:T(8,128)(2,1)}, u32[]{:S(2)}) %copy-start.3) | copy-done | bytes 1048600
  3.5 0.7 %shard_map.82 = bf16[512,512]{1,0:T(8,128)(2,1)S(1)} custom-call(bf16[512,1024]{1,0:T(8,128)(2,1)S(1)} %copy-done.3, bf16[1024,1024]{1,0:T(8,128)(2,1)S(1)} %copy-done), custom_call_target="tpu_custom_call" | custom-call | flops 536870912 | bytes 3670016 | tf_op jit(solution)/shard_map/pallas_call | solution.py:59
  4.2 0.0 copy-start.5
  4.2 0.5 %collective-permute-start.6 = (bf16[512,512]{1,0:T(8,128)(2,1)S(1)}, bf16[512,512]{1,0:T(8,128)(2,1)S(1)}, u32[]{:S(2)}, u32[]{:S(2)}) collective-permute-start(bf16[512,512]{1,0:T(8,128)(2,1)S(1)} %shard_map.82), channel_id=1, source_target_pairs={{0,1},{1,0},{2,3},{3,2},{4,5},{5,4},{6,7},{7,6},{8,9},{9,8},{10,11... | collective-permute-start | bytes 1572872 | tf_op jit(solution)/shard_map/ppermute | solution.py:52
  4.7 0.1 copy-done.2
  4.9 0.1 dynamic-slice_bitcast_fusion
  4.9 0.0 copy-start.6
  4.9 0.0 copy-start.7
  4.9 0.0 copy-start.1
  4.9 0.0 copy-start.4
  5.0 3.0 %collective-permute-start.13 = (bf16[768,256]{1,0:T(8,128)(2,1)S(1)}, bf16[768,256]{1,0:T(8,128)(2,1)S(1)}, u32[]{:S(2)}, u32[]{:S(2)}) collective-permute-start(bf16[768,256]{1,0:T(8,128)(2,1)S(1)} %get-tuple-element.22), channel_id=1, source_target_pairs={{0,2},{1,3},{2,0},{3,1},{4,6},{5,7},{6,4},{7,5},{8,10},{9,11},{10,... | collective-permute-start | bytes 1179656 | tf_op jit(solution)/shard_map/ppermute | solution.py:52
  8.0 0.4 shard_map.78
  8.4 1.6 %collective-permute-start = (bf16[128,256]{1,0:T(8,128)(2,1)S(1)}, bf16[128,256]{1,0:T(8,128)(2,1)S(1)}, u32[]{:S(2)}, u32[]{:S(2)}) collective-permute-start(bf16[128,256]{1,0:T(8,128)(2,1)S(1)} %get-tuple-element.13.refs_0_), channel_id=1, source_target_pairs={{0,4},{4,0},{8,12},{12,8},{1,5},{5,1},{9,13},{13,9},{2,6},{6,2},{1... | collective-permute-start | bytes 196616 | tf_op jit(solution)/shard_map/ppermute | solution.py:48
  10.0 0.7 %collective-permute-start.1 = (bf16[128,256]{1,0:T(8,128)(2,1)S(1)}, bf16[128,256]{1,0:T(8,128)(2,1)S(1)}, u32[]{:S(2)}, u32[]{:S(2)}) collective-permute-start(bf16[128,256]{1,0:T(8,128)(2,1)S(1)} %get-tuple-element.13.refs_0_), channel_id=1, source_target_pairs={{0,0},{4,8},{8,4},{12,12},{1,1},{5,9},{9,5},{13,13},{2,2},{6,10},{... | collective-permute-start | bytes 196616 | tf_op jit(solution)/shard_map/ppermute | solution.py:48
  10.7 3.9 %collective-permute-start.2 = (bf16[80,256]{1,0:T(8,128)(2,1)S(1)}, bf16[80,256]{1,0:T(8,128)(2,1)S(1)}, u32[]{:S(2)}, u32[]{:S(2)}) collective-permute-start(bf16[80,256]{1,0:T(8,128)(2,1)S(1)} %get-tuple-element.14), channel_id=1, source_target_pairs={{0,8},{4,12},{8,0},{12,4},{1,9},{5,13},{9,1},{13,5},{2,10},{6,14},... | collective-permute-start | bytes 122888 | tf_op jit(solution)/shard_map/ppermute | solution.py:48
  14.6 1.2 %shard_map.77 = (bf16[512,512]{1,0:T(8,128)(2,1)S(1)}, bf16[512,512]{1,0:T(8,128)(2,1)S(1)}) custom-call(s32[4]{0:T(128)S(1)} %copy-done.7, bf16[512,128]{1,0:T(8,128)(2,1)S(1)} %copy-done.6), custom_call_target="tpu_custom_call" | custom-call | flops 134217728 | bytes 1179664 | tf_op jit(solution)/shard_map/pallas_call | solution.py:59
  15.8 1.4 %collective-permute-done.2.refs_3_ = bf16[80,256]{1,0:T(8,128)(2,1)S(1)} collective-permute-done((bf16[80,256]{1,0:T(8,128)(2,1)S(1)}, bf16[80,256]{1,0:T(8,128)(2,1)S(1)}, u32[]{:S(2)}, u32[]{:S(2)}) %collective-permute-start.2) | collective-permute-done | bytes 40992 | tf_op jit(solution)/shard_map/ppermute | solution.py:48
  17.2 0.0 collective-permute-done.refs_1_
  17.2 0.0 collective-permute-done.1.refs_2_
  17.2 0.4 shard_map.79.a_ref
  17.6 0.6 %collective-permute-start.4 = (bf16[512,256]{1,0:T(8,128)(2,1)S(1)}, bf16[512,256]{1,0:T(8,128)(2,1)S(1)}, u32[]{:S(2)}, u32[]{:S(2)}) collective-permute-start(bf16[512,256]{1,0:T(8,128)(2,1)S(1)} %shard_map.79.a_ref), channel_id=1, source_target_pairs={{0,2},{1,3},{2,0},{3,1},{4,6},{5,7},{6,4},{7,5},{8,10},{9,11},{10,... | collective-permute-start | bytes 786440 | tf_op jit(solution)/shard_map/ppermute | solution.py:52
  18.2 0.8 %shard_map.81.kept_ref = f32[512,512]{1,0:T(8,128)S(1)} custom-call(bf16[512,1024]{1,0:T(8,128)(2,1)S(1)} %copy-done.4, bf16[1024,1024]{1,0:T(8,128)(2,1)S(1)} %copy-done.1), custom_call_target="tpu_custom_call" | custom-call | flops 536870912 | bytes 4194304 | tf_op jit(solution)/shard_map/pallas_call | solution.py:59
  19.0 0.0 collective-permute-done.6.got_ref
  19.0 0.5 %shard_map.83 = (f32[128,512]{1,0:T(8,128)S(1)}, bf16[128,512]{1,0:T(8,128)(2,1)S(1)}, bf16[128,512]{1,0:T(8,128)(2,1)S(1)}, bf16[80,512]{1,0:T(8,128)(2,1)S(1)}) custom-call(f32[512,512]{1,0:T(8,128)S(1)} %shard_map.81.kept_ref, bf16[512,512]{1,0:T(8,128)(2,1)S(1)} %collective-permute-done.6.got_ref, bf16[512,512]{1,0:T(8,128)(2,1)S(1)} %get-tuple-element.15.turned_ref), custom_call_target="tpu_custom_call" | custom-call | flops 243269632 | bytes 2703360 | tf_op jit(solution)/shard_map/pallas_call | solution.py:59
  19.4 2.9 %collective-permute-start.7 = (bf16[128,512]{1,0:T(8,128)(2,1)S(1)}, bf16[128,512]{1,0:T(8,128)(2,1)S(1)}, u32[]{:S(2)}, u32[]{:S(2)}) collective-permute-start(bf16[128,512]{1,0:T(8,128)(2,1)S(1)} %get-tuple-element.17), channel_id=1, source_target_pairs={{0,4},{4,0},{8,12},{12,8},{1,5},{5,1},{9,13},{13,9},{2,6},{6,2},{1... | collective-permute-start | bytes 393224 | tf_op jit(solution)/shard_map/ppermute | solution.py:48
  22.4 0.7 %collective-permute-start.8 = (bf16[128,512]{1,0:T(8,128)(2,1)S(1)}, bf16[128,512]{1,0:T(8,128)(2,1)S(1)}, u32[]{:S(2)}, u32[]{:S(2)}) collective-permute-start(bf16[128,512]{1,0:T(8,128)(2,1)S(1)} %get-tuple-element.18), channel_id=1, source_target_pairs={{0,0},{4,8},{8,4},{12,12},{1,1},{5,9},{9,5},{13,13},{2,2},{6,10},{... | collective-permute-start | bytes 393224 | tf_op jit(solution)/shard_map/ppermute | solution.py:48
  23.1 2.8 %collective-permute-start.9 = (bf16[80,512]{1,0:T(8,128)(2,1)S(1)}, bf16[80,512]{1,0:T(8,128)(2,1)S(1)}, u32[]{:S(2)}, u32[]{:S(2)}) collective-permute-start(bf16[80,512]{1,0:T(8,128)(2,1)S(1)} %get-tuple-element.19), channel_id=1, source_target_pairs={{0,8},{4,12},{8,0},{12,4},{1,9},{5,13},{9,1},{13,5},{2,10},{6,14},... | collective-permute-start | bytes 245768 | tf_op jit(solution)/shard_map/ppermute | solution.py:48
  25.8 3.7 %collective-permute-done.9.refs_2_ = bf16[80,512]{1,0:T(8,128)(2,1)S(1)} collective-permute-done((bf16[80,512]{1,0:T(8,128)(2,1)S(1)}, bf16[80,512]{1,0:T(8,128)(2,1)S(1)}, u32[]{:S(2)}, u32[]{:S(2)}) %collective-permute-start.9) | collective-permute-done | bytes 81952 | tf_op jit(solution)/shard_map/ppermute | solution.py:48
  29.6 0.0 collective-permute-done.7.refs_0_
  29.6 0.0 collective-permute-done.8.refs_1_
  29.6 0.1 shard_map.84
  29.7 1.6 %collective-permute-start.10 = (bf16[128,512]{1,0:T(8,128)(2,1)S(1)}, bf16[128,512]{1,0:T(8,128)(2,1)S(1)}, u32[]{:S(2)}, u32[]{:S(2)}) collective-permute-start(bf16[128,512]{1,0:T(8,128)(2,1)S(1)} %get-tuple-element.21), channel_id=1, source_target_pairs={{0,2},{1,3},{2,0},{3,1},{4,6},{5,7},{6,4},{7,5},{8,10},{9,11},{10,... | collective-permute-start | bytes 393224 | tf_op jit(solution)/shard_map/ppermute | solution.py:52
  31.2 0.0 collective-permute-start.12
  31.2 0.5 %collective-permute-start.3 = (bf16[512,256]{1,0:T(8,128)(2,1)S(1)}, bf16[512,256]{1,0:T(8,128)(2,1)S(1)}, u32[]{:S(2)}, u32[]{:S(2)}) collective-permute-start(bf16[512,256]{1,0:T(8,128)(2,1)S(1)} %shard_map.79.a_ref), channel_id=1, source_target_pairs={{0,1},{1,0},{2,3},{3,2},{4,5},{5,4},{6,7},{7,6},{8,9},{9,8},{10,11... | collective-permute-start | bytes 786440 | tf_op jit(solution)/shard_map/ppermute | solution.py:52
  31.7 0.0 collective-permute-done.13.x_ref
  31.7 1.5 %collective-permute-start.14 = (bf16[768,256]{1,0:T(8,128)(2,1)S(1)}, bf16[768,256]{1,0:T(8,128)(2,1)S(1)}, u32[]{:S(2)}, u32[]{:S(2)}) collective-permute-start(bf16[768,256]{1,0:T(8,128)(2,1)S(1)} %collective-permute-done.13.x_ref), channel_id=1, source_target_pairs={{0,16},{16,1},{1,17},{17,0},{2,18},{18,3},{3,19},{19,2},{4,20},{20... | collective-permute-start | bytes 1179656 | tf_op jit(solution)/shard_map/ppermute | solution.py:118
  33.3 1.4 %collective-permute-done.10 = bf16[128,512]{1,0:T(8,128)(2,1)S(1)} collective-permute-done((bf16[128,512]{1,0:T(8,128)(2,1)S(1)}, bf16[128,512]{1,0:T(8,128)(2,1)S(1)}, u32[]{:S(2)}, u32[]{:S(2)}) %collective-permute-start.10) | collective-permute-done | bytes 131104 | tf_op jit(solution)/shard_map/ppermute | solution.py:52
  34.7 0.0 collective-permute-done.3.b_ref
  34.8 0.6 %collective-permute-start.11 = (bf16[128,512]{1,0:T(8,128)(2,1)S(1)}, bf16[128,512]{1,0:T(8,128)(2,1)S(1)}, u32[]{:S(2)}, u32[]{:S(2)}) collective-permute-start(bf16[128,512]{1,0:T(8,128)(2,1)S(1)} %add_convert_fusion.mine_ref), channel_id=1, source_target_pairs={{0,1},{1,0},{2,3},{3,2},{4,5},{5,4},{6,7},{7,6},{8,9},{9,8},{10,11... | collective-permute-start | bytes 393224 | tf_op jit(solution)/shard_map/ppermute | solution.py:52
  35.3 0.9 %collective-permute-done.5.d_ref = bf16[512,256]{1,0:T(8,128)(2,1)S(1)} collective-permute-done((bf16[512,256]{1,0:T(8,128)(2,1)S(1)}, bf16[512,256]{1,0:T(8,128)(2,1)S(1)}, u32[]{:S(2)}, u32[]{:S(2)}) %collective-permute-start.5) | collective-permute-done | bytes 262176 | tf_op jit(solution)/shard_map/ppermute | solution.py:52
  36.2 2.2 %shard_map.80 = bf16[512,1024]{1,0:T(8,128)(2,1)} custom-call(bf16[512,256]{1,0:T(8,128)(2,1)S(1)} %shard_map.79.a_ref, bf16[512,256]{1,0:T(8,128)(2,1)S(1)} %collective-permute-done.3.b_ref, bf16[512,256]{1,0:T(8,128)(2,1)S(1)} %collective-permute-done.4.c_ref, bf16[512,256]{1,0:T(8,128)(2,1)S(1)} %collective-permute-done.5.d_ref, ...), custom_call_target="tpu_custom_call" | custom-call | flops 1073741824 | bytes 4194304 | tf_op jit(solution)/shard_map/pallas_call | solution.py:59
  38.5 0.0 collective-permute-done.12.core_ref
  38.5 4.5 %collective-permute-done.14.ring_ref = bf16[768,256]{1,0:T(8,128)(2,1)S(1)} collective-permute-done((bf16[768,256]{1,0:T(8,128)(2,1)S(1)}, bf16[768,256]{1,0:T(8,128)(2,1)S(1)}, u32[]{:S(2)}, u32[]{:S(2)}) %collective-permute-start.14) | collective-permute-done | bytes 393248 | tf_op jit(solution)/shard_map/ppermute | solution.py:118
  43.0 0.0 collective-permute-done.15.side_ref
  43.0 0.0 collective-permute-done.11.other_ref
  43.0 1.3 %shard_map.85 = bf16[128,768]{1,0:T(8,128)(2,1)} custom-call(bf16[128,512]{1,0:T(8,128)(2,1)S(1)} %add_convert_fusion.mine_ref, bf16[128,512]{1,0:T(8,128)(2,1)S(1)} %collective-permute-done.11.other_ref, bf16[3072,256]{1,0:T(8,128)(2,1)S(1)} %copy-done.2, bf16[768,256]{1,0:T(8,128)(2,1)S(1)} %collective-permute-done.12.core_ref, ...), custom_call_target="tpu_custom_call" | custom-call | flops 201326592 | bytes 3604480 | tf_op jit(solution)/shard_map/pallas_call | solution.py:59
  (11 shorter events, 0.0 us)
Async XLA Ops:
  0.6 1.6 %copy-start = (bf16[1024,1024]{1,0:T(8,128)(2,1)S(1)}, bf16[1024,1024]{1,0:T(8,128)(2,1)}, u32[]{:S(2)}) copy-start(bf16[1024,1024]{1,0:T(8,128)(2,1)} %w_ref.8) | copy-start | bytes 6291460
  2.2 1.2 %copy-start.3 = (bf16[512,1024]{1,0:T(8,128)(2,1)S(1)}, bf16[512,1024]{1,0:T(8,128)(2,1)}, u32[]{:S(2)}) copy-start(bf16[512,1024]{1,0:T(8,128)(2,1)} %d_ref.3) | copy-start | bytes 3145732
  3.4 1.4 %copy-start.2 = (bf16[3072,256]{1,0:T(8,128)(2,1)S(1)}, bf16[3072,256]{1,0:T(8,128)(2,1)}, u32[]{:S(2)}) copy-start(bf16[3072,256]{1,0:T(8,128)(2,1)} %w_ref.9) | copy-start | bytes 4718596
  4.2 3.8 %copy-start.5 = (bf16[128,3072]{1,0:T(8,128)(2,1)S(1)}, bf16[128,3072]{1,0:T(8,128)(2,1)}, u32[]{:S(2)}) copy-start(bf16[128,3072]{1,0:T(8,128)(2,1)} %spans_ref.1) | copy-start | bytes 2359300
  4.2 14.8 %collective-permute-start.6 = (bf16[512,512]{1,0:T(8,128)(2,1)S(1)}, bf16[512,512]{1,0:T(8,128)(2,1)S(1)}, u32[]{:S(2)}, u32[]{:S(2)}) collective-permute-start(bf16[512,512]{1,0:T(8,128)(2,1)S(1)} %shard_map.82), channel_id=1, source_target_pairs={{0,1},{1,0},{2,3},{3,2},{4,5},{5,4},{6,7},{7,6},{8,9},{9,8},{10,11... | collective-permute-start | bytes 1572872 | tf_op jit(solution)/shard_map/ppermute | solution.py:52
  4.9 9.7 %copy-start.6 = (bf16[512,128]{1,0:T(8,128)(2,1)S(1)}, bf16[512,128]{1,0:T(8,128)(2,1)}, u32[]{:S(2)}) copy-start(bf16[512,128]{1,0:T(8,128)(2,1)} %weights_ref.1) | copy-start | bytes 393220
  4.9 9.6 %copy-start.7 = (s32[4]{0:T(128)S(1)}, s32[4]{0:T(128)}, u32[]{:S(2)}) copy-start(s32[4]{0:T(128)} %off_ref.1) | copy-start | bytes 52
  4.9 13.3 %copy-start.1 = (bf16[1024,1024]{1,0:T(8,128)(2,1)S(1)}, bf16[1024,1024]{1,0:T(8,128)(2,1)}, u32[]{:S(2)}) copy-start(bf16[1024,1024]{1,0:T(8,128)(2,1)} %w_ref.8) | copy-start | bytes 6291460
  4.9 13.2 %copy-start.4 = (bf16[512,1024]{1,0:T(8,128)(2,1)S(1)}, bf16[512,1024]{1,0:T(8,128)(2,1)}, u32[]{:S(2)}) copy-start(bf16[512,1024]{1,0:T(8,128)(2,1)} %d_ref.3) | copy-start | bytes 3145732
  5.0 26.8 %collective-permute-start.13 = (bf16[768,256]{1,0:T(8,128)(2,1)S(1)}, bf16[768,256]{1,0:T(8,128)(2,1)S(1)}, u32[]{:S(2)}, u32[]{:S(2)}) collective-permute-start(bf16[768,256]{1,0:T(8,128)(2,1)S(1)} %get-tuple-element.22), channel_id=1, source_target_pairs={{0,2},{1,3},{2,0},{3,1},{4,6},{5,7},{6,4},{7,5},{8,10},{9,11},{10,... | collective-permute-start | bytes 1179656 | tf_op jit(solution)/shard_map/ppermute | solution.py:52
  8.4 8.8 %collective-permute-start = (bf16[128,256]{1,0:T(8,128)(2,1)S(1)}, bf16[128,256]{1,0:T(8,128)(2,1)S(1)}, u32[]{:S(2)}, u32[]{:S(2)}) collective-permute-start(bf16[128,256]{1,0:T(8,128)(2,1)S(1)} %get-tuple-element.13.refs_0_), channel_id=1, source_target_pairs={{0,4},{4,0},{8,12},{12,8},{1,5},{5,1},{9,13},{13,9},{2,6},{6,2},{1... | collective-permute-start | bytes 196616 | tf_op jit(solution)/shard_map/ppermute | solution.py:48
  10.0 7.2 %collective-permute-start.1 = (bf16[128,256]{1,0:T(8,128)(2,1)S(1)}, bf16[128,256]{1,0:T(8,128)(2,1)S(1)}, u32[]{:S(2)}, u32[]{:S(2)}) collective-permute-start(bf16[128,256]{1,0:T(8,128)(2,1)S(1)} %get-tuple-element.13.refs_0_), channel_id=1, source_target_pairs={{0,0},{4,8},{8,4},{12,12},{1,1},{5,9},{9,5},{13,13},{2,2},{6,10},{... | collective-permute-start | bytes 196616 | tf_op jit(solution)/shard_map/ppermute | solution.py:48
  10.7 6.5 %collective-permute-start.2 = (bf16[80,256]{1,0:T(8,128)(2,1)S(1)}, bf16[80,256]{1,0:T(8,128)(2,1)S(1)}, u32[]{:S(2)}, u32[]{:S(2)}) collective-permute-start(bf16[80,256]{1,0:T(8,128)(2,1)S(1)} %get-tuple-element.14), channel_id=1, source_target_pairs={{0,8},{4,12},{8,0},{12,4},{1,9},{5,13},{9,1},{13,5},{2,10},{6,14},... | collective-permute-start | bytes 122888 | tf_op jit(solution)/shard_map/ppermute | solution.py:48
  17.6 15.7 %collective-permute-start.4 = (bf16[512,256]{1,0:T(8,128)(2,1)S(1)}, bf16[512,256]{1,0:T(8,128)(2,1)S(1)}, u32[]{:S(2)}, u32[]{:S(2)}) collective-permute-start(bf16[512,256]{1,0:T(8,128)(2,1)S(1)} %shard_map.79.a_ref), channel_id=1, source_target_pairs={{0,2},{1,3},{2,0},{3,1},{4,6},{5,7},{6,4},{7,5},{8,10},{9,11},{10,... | collective-permute-start | bytes 786440 | tf_op jit(solution)/shard_map/ppermute | solution.py:52
  19.4 10.1 %collective-permute-start.7 = (bf16[128,512]{1,0:T(8,128)(2,1)S(1)}, bf16[128,512]{1,0:T(8,128)(2,1)S(1)}, u32[]{:S(2)}, u32[]{:S(2)}) collective-permute-start(bf16[128,512]{1,0:T(8,128)(2,1)S(1)} %get-tuple-element.17), channel_id=1, source_target_pairs={{0,4},{4,0},{8,12},{12,8},{1,5},{5,1},{9,13},{13,9},{2,6},{6,2},{1... | collective-permute-start | bytes 393224 | tf_op jit(solution)/shard_map/ppermute | solution.py:48
  22.4 7.2 %collective-permute-start.8 = (bf16[128,512]{1,0:T(8,128)(2,1)S(1)}, bf16[128,512]{1,0:T(8,128)(2,1)S(1)}, u32[]{:S(2)}, u32[]{:S(2)}) collective-permute-start(bf16[128,512]{1,0:T(8,128)(2,1)S(1)} %get-tuple-element.18), channel_id=1, source_target_pairs={{0,0},{4,8},{8,4},{12,12},{1,1},{5,9},{9,5},{13,13},{2,2},{6,10},{... | collective-permute-start | bytes 393224 | tf_op jit(solution)/shard_map/ppermute | solution.py:48
  23.1 6.5 %collective-permute-start.9 = (bf16[80,512]{1,0:T(8,128)(2,1)S(1)}, bf16[80,512]{1,0:T(8,128)(2,1)S(1)}, u32[]{:S(2)}, u32[]{:S(2)}) collective-permute-start(bf16[80,512]{1,0:T(8,128)(2,1)S(1)} %get-tuple-element.19), channel_id=1, source_target_pairs={{0,8},{4,12},{8,0},{12,4},{1,9},{5,13},{9,1},{13,5},{2,10},{6,14},... | collective-permute-start | bytes 245768 | tf_op jit(solution)/shard_map/ppermute | solution.py:48
  29.7 5.0 %collective-permute-start.10 = (bf16[128,512]{1,0:T(8,128)(2,1)S(1)}, bf16[128,512]{1,0:T(8,128)(2,1)S(1)}, u32[]{:S(2)}, u32[]{:S(2)}) collective-permute-start(bf16[128,512]{1,0:T(8,128)(2,1)S(1)} %get-tuple-element.21), channel_id=1, source_target_pairs={{0,2},{1,3},{2,0},{3,1},{4,6},{5,7},{6,4},{7,5},{8,10},{9,11},{10,... | collective-permute-start | bytes 393224 | tf_op jit(solution)/shard_map/ppermute | solution.py:52
  31.2 7.2 %collective-permute-start.12 = (bf16[768,256]{1,0:T(8,128)(2,1)S(1)}, bf16[768,256]{1,0:T(8,128)(2,1)S(1)}, u32[]{:S(2)}, u32[]{:S(2)}) collective-permute-start(bf16[768,256]{1,0:T(8,128)(2,1)S(1)} %get-tuple-element.23), channel_id=1, source_target_pairs={{0,1},{1,0},{2,3},{3,2},{4,5},{5,4},{6,7},{7,6},{8,9},{9,8},{10,11... | collective-permute-start | bytes 1179656 | tf_op jit(solution)/shard_map/ppermute | solution.py:52
  31.2 3.5 %collective-permute-start.3 = (bf16[512,256]{1,0:T(8,128)(2,1)S(1)}, bf16[512,256]{1,0:T(8,128)(2,1)S(1)}, u32[]{:S(2)}, u32[]{:S(2)}) collective-permute-start(bf16[512,256]{1,0:T(8,128)(2,1)S(1)} %shard_map.79.a_ref), channel_id=1, source_target_pairs={{0,1},{1,0},{2,3},{3,2},{4,5},{5,4},{6,7},{7,6},{8,9},{9,8},{10,11... | collective-permute-start | bytes 786440 | tf_op jit(solution)/shard_map/ppermute | solution.py:52
  31.7 11.2 %collective-permute-start.14 = (bf16[768,256]{1,0:T(8,128)(2,1)S(1)}, bf16[768,256]{1,0:T(8,128)(2,1)S(1)}, u32[]{:S(2)}, u32[]{:S(2)}) collective-permute-start(bf16[768,256]{1,0:T(8,128)(2,1)S(1)} %collective-permute-done.13.x_ref), channel_id=1, source_target_pairs={{0,16},{16,1},{1,17},{17,0},{2,18},{18,3},{3,19},{19,2},{4,20},{20... | collective-permute-start | bytes 1179656 | tf_op jit(solution)/shard_map/ppermute | solution.py:118
  33.3 9.7 %collective-permute-start.15 = (bf16[768,256]{1,0:T(8,128)(2,1)S(1)}, bf16[768,256]{1,0:T(8,128)(2,1)S(1)}, u32[]{:S(2)}, u32[]{:S(2)}) collective-permute-start(bf16[768,256]{1,0:T(8,128)(2,1)S(1)} %collective-permute-done.13.x_ref), channel_id=1, source_target_pairs={{0,1},{1,0},{2,3},{3,2},{4,5},{5,4},{6,7},{7,6},{8,9},{9,8},{10,11... | collective-permute-start | bytes 1179656 | tf_op jit(solution)/shard_map/ppermute | solution.py:52
  34.7 1.5 %collective-permute-start.5 = (bf16[512,256]{1,0:T(8,128)(2,1)S(1)}, bf16[512,256]{1,0:T(8,128)(2,1)S(1)}, u32[]{:S(2)}, u32[]{:S(2)}) collective-permute-start(bf16[512,256]{1,0:T(8,128)(2,1)S(1)} %collective-permute-done.4.c_ref), channel_id=1, source_target_pairs={{0,1},{1,0},{2,3},{3,2},{4,5},{5,4},{6,7},{7,6},{8,9},{9,8},{10,11... | collective-permute-start | bytes 786440 | tf_op jit(solution)/shard_map/ppermute | solution.py:52
  34.8 8.2 %collective-permute-start.11 = (bf16[128,512]{1,0:T(8,128)(2,1)S(1)}, bf16[128,512]{1,0:T(8,128)(2,1)S(1)}, u32[]{:S(2)}, u32[]{:S(2)}) collective-permute-start(bf16[128,512]{1,0:T(8,128)(2,1)S(1)} %add_convert_fusion.mine_ref), channel_id=1, source_target_pairs={{0,1},{1,0},{2,3},{3,2},{4,5},{5,4},{6,7},{7,6},{8,9},{9,8},{10,11... | collective-permute-start | bytes 393224 | tf_op jit(solution)/shard_map/ppermute | solution.py:52

commit v3 on v2

v3 whole, which is shorter than its diff:
```python
import functools

import jax
import jax.numpy as jnp
from jax import lax
from jax.experimental import pallas as pl
from jax.experimental.pallas import tpu as pltpu
from jax.sharding import PartitionSpec as P

F32, BF16 = jnp.float32, jnp.bfloat16
NOWHERE = -(1 << 20)


def reach(count, blocks, breadth, span_rows):
    usable = count * span_rows - breadth
    last = count * blocks - 1
    most = 0
    for index in range(count):
        low = max(index * blocks * usable // last - span_rows, 0)
        high = min(((index + 1) * blocks - 1) * usable // last + span_rows, usable) + breadth
        most = max(most, (index - 1) * span_rows - low, high - (index + 2) * span_rows)
    most = max(16, -(-most // 16) * 16)
    assert most <= span_rows
    return most


def pairings(count):
    every = [(1, 1), (2, 0), (2, 1), (1, 0)]
    return [p for p in every if any(partner(i, *p, count) != i for i in range(count))]


def partner(index, distance, parity, count):
    up = (index // distance) % 2 == parity
    other = index + distance if up else index - distance
    return other if 0 <= other < count else index


def partner_here(distance, parity, count):
    index = lax.axis_index("seq")
    up = lax.rem(lax.div(index, distance), 2) == parity
    other = jnp.where(up, index + distance, index - distance)
    return other, up, (other >= 0) & (other < count)


def trade(value, pairing, count):
    pairs = []
    for i in range(count):
        other = partner(i, *pairing, count)
        for t in range(4):
            pairs.append((4 * i + t, 4 * other + (t ^ 1 if other == i else t)))
    return lax.ppermute(value, ("seq", "tensor"), pairs)


def swap(value, mask):
    return lax.ppermute(value, "tensor", [(i, i ^ mask) for i in range(4)])


def call(kernel, outs, *args, flops, scalars=(), after=()):
    moved = sum(a.size * a.dtype.itemsize for a in args)
    moved += sum(o.size * o.dtype.itemsize for o in outs)
    spaces = [pltpu.SMEM if k in scalars else pltpu.VMEM for k in range(len(args))]
    spaces += [pl.ANY] * len(after)
    inputs = len(args)

    def run(*refs):
        kernel(*refs[:inputs], *refs[inputs + len(after) : -1])
        refs[-1][...] = jnp.zeros_like(refs[-1])

    return pl.pallas_call(
        run,
        out_shape=list(outs) + [shape((8, 128), F32)],
        name=getattr(kernel, "func", kernel).__name__,
        in_specs=[pl.BlockSpec(memory_space=space) for space in spaces],
        out_specs=[pl.BlockSpec(memory_space=pltpu.VMEM)] * (len(outs) + 1),
        compiler_params=pltpu.CompilerParams(vmem_limit_bytes=16 << 20),
        cost_estimate=pl.CostEstimate(flops=flops, bytes_accessed=moved, transcendentals=0),
    )(*args, *after)


def shape(dims, kind=BF16):
    return jax.ShapeDtypeStruct(dims, kind)


def dot(a, b):
    return jnp.dot(a, b, preferred_element_type=F32)


def dot_t(a, b):
    return lax.dot_general(a, b, (((1,), (1,)), ((), ())), preferred_element_type=F32)


def body(spans, w_in, band_weights, offsets, w_up, d_up):
    count = lax.axis_size("seq")
    groups = lax.axis_size("group")
    blocks, breadth = offsets.shape[0], band_weights.shape[1]
    bytes_here, hidden = d_up.shape
    block = bytes_here // blocks
    span_rows, depth = spans.shape
    width = w_in.shape[1]
    share = depth // 4
    far = reach(count, blocks, breadth, span_rows)
    pairs = pairings(count)
    rows = [span_rows] + [span_rows if d == 1 else far for d, _ in pairs]
    cols = [breadth * k for k in range(len(rows))]
    longs = [p for p in pairs if p[0] == 2]

    def cut_at(distance, parity):
        _, up, _ = partner_here(distance, parity, count)
        return pl.multiple_of(jnp.where(up, span_rows - far, 0), 16)

    def block_of(ref, mask, size):
        at = (lax.axis_index("tensor") ^ mask) * size
        return ref[pl.ds(pl.multiple_of(at, size), size), :]

    here = lax.axis_index("tensor")
    cube = w_in.reshape(4, share, width)

    def quarter(index):
        return lax.dynamic_index_in_dim(cube, index, 0, keepdims=False)

    half = lax.axis_index("group") if groups == 2 else 0
    w_core = swap(quarter(here ^ 1), 1)
    w_x_sent = quarter(here ^ 2 ^ half)
    w_x = swap(w_x_sent, 2)

    total_cols = breadth * len(rows)

    def grad_part(masks, d_ref, w_ref, out_ref):
        for k, mask in enumerate(masks):
            part = dot_t(d_ref[...], block_of(w_ref, mask, width))
            out_ref[:, k * width : (k + 1) * width] = part.astype(out_ref.dtype)

    def spread(off_ref, weights_ref, band_ref, turned_ref):
        starts = [lax.axis_index("seq") * span_rows]
        for distance, parity in pairs:
            other, up, there = partner_here(distance, parity, count)
            skip = 0 if distance == 1 else jnp.where(up, 0, span_rows - far)
            starts.append(jnp.where(there, other * span_rows + skip, NOWHERE))

        def row_ids(along):
            dims = (breadth, total_cols) if along else (total_cols, breadth)
            at = lax.broadcasted_iota(jnp.int32, dims, along)
            ids = NOWHERE
            for start, size, col in zip(starts, rows, cols):
                ids = jnp.where((at >= col) & (at < col + size), at + (start - col), ids)
            return ids, lax.broadcasted_iota(jnp.int32, dims, 1 - along)

        across, down_j = row_ids(1)
        down, across_j = row_ids(0)
        for b in range(blocks):
            part = slice(b * block, (b + 1) * block)
            weights = weights_ref[part, :]
            pick = (across - off_ref[b] == down_j).astype(F32).astype(BF16)
            band_ref[part, :] = dot(weights, pick).astype(BF16)
            pick = (down - off_ref[b] == across_j).astype(F32).astype(BF16)
            turned_ref[:, part] = dot_t(pick, weights).astype(BF16)

    def open_up(
        off_hbm, weights_hbm, d_hbm, w_hbm, band_ref, turned_ref, out_ref, token_ref, off, weights, d_vm, w_vm, sems
    ):
        at = lax.axis_index("tensor")
        loads = []

        def load(source, target):
            copy = pltpu.make_async_copy(source, target, sems.at[len(loads)])
            copy.start()
            loads.append(copy)

        load(off_hbm, off)
        load(weights_hbm, weights)
        for k, mask in enumerate((1, 3)):
            part = pl.ds(pl.multiple_of((at ^ mask) * width, width), width)
            load(w_hbm.at[part, :], w_vm.at[k])
            step = bytes_here // 4
            for q in (2 * k, 2 * k + 1):
                part = pl.ds(q * step, step)
                load(d_hbm.at[part, :], d_vm.at[part, :])
        for copy in loads[:2]:
            copy.wait()
        token_ref[...] = jnp.zeros_like(token_ref)
        spread(off, weights, band_ref, turned_ref)
        for copy in loads[2:]:
            copy.wait()
        for k in range(2):
            out_ref[:, k * width : (k + 1) * width] = dot_t(d_vm[...], w_vm[k]).astype(BF16)

    def fixed(value):
        return pltpu.with_memory_space_constraint(value, pltpu.HBM)

    band, turned, grad_sent, opened = pl.pallas_call(
        open_up,
        out_shape=[
            shape((bytes_here, total_cols)),
            shape((total_cols, bytes_here)),
            shape((bytes_here, 2 * width)),
            shape((8, 128), F32),
        ],
        in_specs=[pl.BlockSpec(memory_space=pltpu.HBM)] * 4,
        out_specs=[pl.BlockSpec(memory_space=pltpu.VMEM)] * 4,
        scratch_shapes=[
            pltpu.SMEM((blocks,), jnp.int32),
            pltpu.VMEM((bytes_here, breadth), BF16),
            pltpu.VMEM((bytes_here, hidden), BF16),
            pltpu.VMEM((2, width, hidden), BF16),
            pltpu.SemaphoreType.DMA((8,)),
        ],
        name="open_up",
        compiler_params=pltpu.CompilerParams(vmem_limit_bytes=16 << 20),
        cost_estimate=pl.CostEstimate(
            flops=4 * bytes_here * width * hidden,
            bytes_accessed=2 * (2 * width + bytes_here) * hidden,
            transcendentals=0,
        ),
    )(fixed(offsets), fixed(band_weights), fixed(d_up), fixed(w_up))
    grad_got = swap(grad_sent, 1)

    def project(spans_ref, w_ref, out_ref, *cut_refs):
        out_ref[...] = dot(spans_ref[...], w_ref[...]).astype(BF16)
        for ref, pairing in zip(cut_refs, longs):
            ref[...] = out_ref[pl.ds(cut_at(*pairing), far), :]

    reduced, *cuts, reduced_done = call(
        project,
        [shape((span_rows, width))] + [shape((far, width)) for _ in longs],
        spans,
        w_in,
        flops=2 * span_rows * depth * width,
        after=(opened,),
    )
    cut_of = dict(zip(longs, cuts))
    pieces = [reduced] + [trade(cut_of.get(p, reduced), p, count) for p in pairs]

    grad_kept, _ = call(
        functools.partial(grad_part, (0, 2)),
        [shape((bytes_here, 2 * width), F32)],
        d_up,
        w_up,
        flops=4 * bytes_here * width * hidden,
        after=(reduced_done,),
    )

    def part_of(turned_ref, k, grad):
        return dot(turned_ref[cols[k] : cols[k] + rows[k], :], grad)

    def first_share(kept_ref, got_ref, turned_ref, grad_ref, out_ref):
        grad_ref[...] = (kept_ref[...] + got_ref[...].astype(F32)).astype(BF16)
        out_ref[...] = part_of(turned_ref, 1, grad_ref[...]).astype(BF16)

    def next_share(k, grad_ref, turned_ref, out_ref):
        out_ref[...] = part_of(turned_ref, k, grad_ref[...]).astype(out_ref.dtype)

    products = [2 * bytes_here * 2 * width * r for r in rows]
    grad, share_sent, share_done = call(
        first_share,
        [shape((bytes_here, 2 * width)), shape((rows[1], 2 * width))],
        grad_kept,
        grad_got,
        turned,
        flops=products[1],
    )
    came = [trade(share_sent, pairs[0], count)]
    for k in range(2, len(rows)):
        share_sent, share_done = call(
            functools.partial(next_share, k),
            [shape((rows[k], 2 * width))],
            grad,
            turned,
            flops=products[k],
            after=(share_done,),
        )
        came.append(trade(share_sent, pairs[k - 1], count))
    own, own_done = call(
        functools.partial(next_share, 0),
        [shape((span_rows, 2 * width), F32)],
        grad,
        turned,
        flops=products[0],
        after=(share_done,),
    )

    if groups == 2:
        ring = []
        for t in range(4):
            ring += [(t, 4 + t), (4 + t, t ^ 1)]
        w_ring = lax.ppermute(w_x, ("group", "tensor"), ring)
        w_side = swap(w_x, 1)
    else:
        w_ring = swap(quarter(here ^ 3), 3)
        w_side = w_ring

    def upsample(band_ref, *refs):
        *piece_refs, out_ref = refs
        acc = 0.0
        for k, ref in enumerate(piece_refs):
            acc += dot(band_ref[:, cols[k] : cols[k] + rows[k]], ref[...])
        out_ref[...] = acc.astype(BF16)

    upsampled, _ = call(
        upsample,
        [shape((bytes_here, width))],
        band,
        *pieces,
        flops=2 * bytes_here * width * sum(rows),
        after=(own_done,),
    )
    up_x = swap(upsampled, 2)
    up_core = swap(upsampled, 1)

    def collect(own_ref, *refs):
        *came_refs, sum_ref, sent_ref = refs
        sum_ref[...] = own_ref[...]
        for ref, (distance, parity) in zip(came_refs, pairs):
            if distance == 1:
                sum_ref[...] += ref[...].astype(F32)
            else:
                sum_ref[pl.ds(cut_at(distance, parity), far), :] += ref[...].astype(F32)
        sent_ref[:, width:] = sum_ref[:, :width].astype(BF16)
        sent_ref[:, :width] = sum_ref[:, width:].astype(BF16)

    summed, sent, _ = call(
        collect,
        [shape((span_rows, 2 * width), F32), shape((span_rows, 2 * width))],
        own,
        *came,
        flops=8 * span_rows * width,
    )
    over_x = swap(sent, 2)
    up_x, summed = lax.optimization_barrier((up_x, summed))
    up_both = swap(up_x, 1)

    def up_project(a_ref, b_ref, c_ref, d_ref, w_ref, ring_ref, out_hbm, out_vm, sems):
        refs = (a_ref, b_ref, c_ref, d_ref)
        step = bytes_here // 4
        copies = []
        for q in range(4):
            part = slice(q * step, (q + 1) * step)
            acc = 0.0
            for mask, ref in enumerate(refs):
                acc += dot(ref[part, :], block_of(w_ref, mask, width))
            out_vm[part, :] = acc.astype(BF16)
            part = pl.ds(q * step, step)
            copies.append(pltpu.make_async_copy(out_vm.at[part, :], out_hbm.at[part, :], sems.at[q]))
            copies[-1].start()
        for copy in copies:
            copy.wait()

    up_proj = pl.pallas_call(
        up_project,
        out_shape=shape((bytes_here, hidden)),
        in_specs=[pl.BlockSpec(memory_space=pltpu.VMEM)] * 5 + [pl.BlockSpec(memory_space=pl.ANY)],
        out_specs=pl.BlockSpec(memory_space=pltpu.HBM),
        scratch_shapes=[pltpu.VMEM((bytes_here, hidden), BF16), pltpu.SemaphoreType.DMA((4,))],
        name="up_project",
        compiler_params=pltpu.CompilerParams(vmem_limit_bytes=16 << 20),
        cost_estimate=pl.CostEstimate(
            flops=8 * bytes_here * width * hidden,
            bytes_accessed=2 * bytes_here * hidden,
            transcendentals=0,
        ),
    )(upsampled, up_core, up_x, up_both, w_up, w_ring)

    summed, up_proj = lax.optimization_barrier((summed, up_proj))
    d_reduced = (summed + over_x.astype(F32)).astype(BF16)
    d_other = swap(d_reduced, 1)

    def finish_mine(mine_ref, w_ref, x_ref, ring_ref, out_ref):
        near = x_ref[...]
        if groups == 2:
            near = jnp.where(lax.axis_index("group") == 0, near, ring_ref[...])
        part = dot_t(mine_ref[:, :width], block_of(w_ref, 0, share))
        out_ref[...] = part + dot_t(mine_ref[:, width:], near)

    def finish(part_ref, other_ref, core_ref, ring_ref, side_ref, out_ref):
        cross = ring_ref[...]
        if groups == 2:
            cross = jnp.where(lax.axis_index("group") == 0, cross, side_ref[...])
        part = part_ref[...] + dot_t(other_ref[:, :width], core_ref[...])
        out_ref[...] = (part + dot_t(other_ref[:, width:], cross)).astype(BF16)

    work = 4 * span_rows * width * share
    mine, _ = call(
        finish_mine, [shape((span_rows, share), F32)], d_reduced, w_in, w_x, w_ring, flops=work
    )
    d_spans, _ = call(
        finish, [shape((span_rows, share))], mine, d_other, w_core, w_ring, w_side, flops=work
    )

    return (up_proj, d_spans)


def solution(mesh):
    placed = (
        P(("group", "seq"), None),
        P(None, "tensor"),
        P(("group", "seq"), None),
        P(("group", "seq")),
        P(None, "tensor"),
        P(("group", "seq"), "tensor"),
    )
    return jax.shard_map(
        body,
        mesh=mesh,
        in_specs=placed,
        out_specs=(P(("group", "seq"), "tensor"), P(("group", "seq"), "tensor")),
        check_vma=False,
    )
```

time: 44.5 us -> 35.9 us (0.81)
  starting transfers between devices: 20.8 us -> 14.9 us
  Pallas kernels: 7.63 us -> 12.5 us
  waiting for transfers between devices: 12 us -> 7.47 us
  local copies, waits for them, and re-layouts: 3.02 us -> 0.07 us
    ppermute x6, starting transfers between devices: 12.6 us -> 7.11 us  [trade(): return lax.ppermute(value, ('seq', 'tensor'), pairs)]
    pallas_call x9 -> x12, Pallas kernels: 7.63 us -> 12.5 us  [the longest x10 7.14 us: call(): pl.pallas_call(run, out_shape=list(outs) + [shape((8, 128), F32)], name=g...]
    ppermute x1, waiting for transfers between devices: 4.5 us -> 1.25 us  [body(): w_ring = lax.ppermute(w_x, ('group', 'tensor'), ring)]
    unnamed x16 -> x8, local copies, waits for them, and re-layouts: 2.97 us -> 0.02 us
    ppermute x9, waiting for transfers between devices: 2.39 us -> 0.82 us  [swap(): return lax.ppermute(value, 'tensor', [(i, i ^ mask) for i in range(4)])]
    ppermute x9, starting transfers between devices: 6.75 us -> 6.24 us  [swap(): return lax.ppermute(value, 'tensor', [(i, i ^ mask) for i in range(4)])]
  transfers between devices with their start and end apart: 16 -> 16, of which waited for: 5 -> 5; matrix products, arithmetic and copies ran while one was open for 0% -> 0% of each run, Pallas kernels for 13% -> 23%
where the time goes in v3:
time: 35.9 us; the launch traced here: 35.7 us
  starting transfers between devices  14.9 us (42%)
  Pallas kernels  12.5 us (35%)
  waiting for transfers between devices  7.47 us (21%)
  between operations  0.74 us (2%)
    pallas_call x10, Pallas kernels, call(): pl.pallas_call(run, out_shape=list(outs) + [shape((8, 128), F32)], name=g...  7.14 us
    ppermute x6, starting transfers between devices, trade(): return lax.ppermute(value, ('seq', 'tensor'), pairs)  7.11 us
    ppermute x9, starting transfers between devices, swap(): return lax.ppermute(value, 'tensor', [(i, i ^ mask) for i in range(4)])  6.24 us
    ppermute x6, waiting for transfers between devices, trade(): return lax.ppermute(value, ('seq', 'tensor'), pairs)  5.41 us
    pallas_call x1, Pallas kernels, body(): pl.pallas_call(open_up, out_shape=[shape((bytes_here, total_cols)), shape...  3.29 us
    pallas_call x1, Pallas kernels, body(): pl.pallas_call(up_project, out_shape=shape((bytes_here, hidden)), in_spec...  2.11 us
    ppermute x1, starting transfers between devices, body(): w_ring = lax.ppermute(w_x, ('group', 'tensor'), ring)  1.52 us
    ppermute x1, waiting for transfers between devices, body(): w_ring = lax.ppermute(w_x, ('group', 'tensor'), ring)  1.25 us
  transfers between devices with their start and end apart: 16, of which 5 were waited for; matrix products, arithmetic and copies ran while one was open for 0% of the time, Pallas kernels for 23%

profile of v3, /device:TPU:0, one launch (start us, length us, event | category | flops | bytes accessed | tf_op | source)
XLA Modules:
  0.0 35.7 jit_solution(5270181282623389254)
XLA Ops:
  0.6 0.0 copy-start.1
  0.6 3.3 %open_up.1 = (bf16[512,512]{1,0:T(8,128)(2,1)S(1)}, bf16[512,512]{1,0:T(8,128)(2,1)S(1)}, bf16[512,512]{1,0:T(8,128)(2,1)}, f32[8,128]{1,0:T(8,128)S(1)}) custom-call(s32[4]{0:T(128)} %off_hbm.1, bf16[512,128]{1,0:T(8,128)(2,1)} %weights_hbm.1, bf16[512,1024]{1,0:T(8,128)(2,1)} %refs_0_.3, bf16[1024,1024]{1,0:T(8,128)(2,1)} %w_ref.1), custom_call_target="tpu_custom_call" | custom-call | flops 536870912 | bytes 2097152 | tf_op jit(solution)/shard_map/open_up/pallas_call | solution.py:190
  3.9 0.0 copy-start.3
  4.0 0.5 %collective-permute-start.3 = (bf16[512,512]{1,0:T(8,128)(2,1)}, bf16[512,512]{1,0:T(8,128)(2,1)}, u32[]{:S(2)}, u32[]{:S(2)}) collective-permute-start(bf16[512,512]{1,0:T(8,128)(2,1)} %get-tuple-element.34), channel_id=1, source_target_pairs={{0,1},{1,0},{2,3},{3,2},{4,5},{5,4},{6,7},{7,6},{8,9},{9,8},{10,11... | collective-permute-start | bytes 1572872 | tf_op jit(solution)/shard_map/ppermute | solution.py:55
  4.5 0.1 dynamic-slice_bitcast_fusion
  4.5 0.0 copy-start
  4.5 2.6 %collective-permute-start.10 = (bf16[768,256]{1,0:T(8,128)(2,1)S(1)}, bf16[768,256]{1,0:T(8,128)(2,1)S(1)}, u32[]{:S(2)}, u32[]{:S(2)}) collective-permute-start(bf16[768,256]{1,0:T(8,128)(2,1)S(1)} %get-tuple-element.55), channel_id=1, source_target_pairs={{0,2},{1,3},{2,0},{3,1},{4,6},{5,7},{6,4},{7,5},{8,10},{9,11},{10,... | collective-permute-start | bytes 1179656 | tf_op jit(solution)/shard_map/ppermute | solution.py:55
  7.2 0.4 %project.1 = (bf16[128,256]{1,0:T(8,128)(2,1)S(1)}, bf16[80,256]{1,0:T(8,128)(2,1)S(1)}, f32[8,128]{1,0:T(8,128)S(1)}) custom-call(bf16[128,3072]{1,0:T(8,128)(2,1)S(1)} %copy-done.3, bf16[3072,256]{1,0:T(8,128)(2,1)S(1)} %copy-done.1, f32[8,128]{1,0:T(8,128)S(1)} %get-tuple-element.29.refs_2_), custom_call_target="tpu_custom_call" | custom-call | flops 201326592 | bytes 2465792 | tf_op jit(solution)/shard_map/project/pallas_call | solution.py:69
  7.5 0.2 collective-permute-start
  7.8 3.0 %collective-permute-start.2 = (bf16[128,256]{1,0:T(8,128)(2,1)S(1)}, bf16[128,256]{1,0:T(8,128)(2,1)S(1)}, u32[]{:S(2)}, u32[]{:S(2)}) collective-permute-start(bf16[128,256]{1,0:T(8,128)(2,1)S(1)} %get-tuple-element.30.refs_1_), channel_id=1, source_target_pairs={{0,4},{1,5},{2,6},{3,7},{4,0},{5,1},{6,2},{7,3},{8,12},{9,13},{10,... | collective-permute-start | bytes 196616 | tf_op jit(solution)/shard_map/ppermute | solution.py:51
  10.8 1.2 %collective-permute-start.1 = (bf16[80,256]{1,0:T(8,128)(2,1)S(1)}, bf16[80,256]{1,0:T(8,128)(2,1)S(1)}, u32[]{:S(2)}, u32[]{:S(2)}) collective-permute-start(bf16[80,256]{1,0:T(8,128)(2,1)S(1)} %get-tuple-element.31), channel_id=1, source_target_pairs={{0,8},{1,9},{2,10},{3,11},{4,12},{5,13},{6,14},{7,15},{8,0},{9,1},... | collective-permute-start | bytes 122888 | tf_op jit(solution)/shard_map/ppermute | solution.py:51
  12.0 1.2 %grad_part.1 = (f32[512,512]{1,0:T(8,128)S(1)}, f32[8,128]{1,0:T(8,128)}) custom-call(bf16[512,1024]{1,0:T(8,128)(2,1)S(1)} %copy-done.2, bf16[1024,1024]{1,0:T(8,128)(2,1)S(1)} %copy-done, f32[8,128]{1,0:T(8,128)S(1)} %get-tuple-element.32.refs_2_), custom_call_target="tpu_custom_call" | custom-call | flops 536870912 | bytes 4194304 | tf_op jit(solution)/shard_map/grad_part/pallas_call | solution.py:69
  13.2 0.0 collective-permute-done.3.refs_1_
  13.2 1.3 %first_share.1 = (bf16[512,512]{1,0:T(8,128)(2,1)S(1)}, bf16[128,512]{1,0:T(8,128)(2,1)S(1)}, f32[8,128]{1,0:T(8,128)S(1)}) custom-call(f32[512,512]{1,0:T(8,128)S(1)} %get-tuple-element.33.refs_0_, bf16[512,512]{1,0:T(8,128)(2,1)} %collective-permute-done.3.refs_1_, bf16[512,512]{1,0:T(8,128)(2,1)S(1)} %get-tuple-element.35.refs_2_.refs_1_), custom_call_target="tpu_custom_call" | custom-call | flops 67108864 | bytes 2752512 | tf_op jit(solution)/shard_map/first_share/pallas_call | solution.py:69
  14.6 0.2 next_share.3
  14.8 0.2 next_share.4
  15.0 0.2 next_share.5
  15.2 0.4 %collective-permute-done.1.refs_3_ = bf16[80,256]{1,0:T(8,128)(2,1)S(1)} collective-permute-done((bf16[80,256]{1,0:T(8,128)(2,1)S(1)}, bf16[80,256]{1,0:T(8,128)(2,1)S(1)}, u32[]{:S(2)}, u32[]{:S(2)}) %collective-permute-start.1) | collective-permute-done | bytes 40992 | tf_op jit(solution)/shard_map/ppermute | solution.py:51
  15.7 0.0 collective-permute-done.refs_2_
  15.7 0.0 collective-permute-done.2.refs_4_
  15.7 0.9 %upsample.1 = (bf16[512,256]{1,0:T(8,128)(2,1)S(1)}, f32[8,128]{1,0:T(8,128)}) custom-call(bf16[512,512]{1,0:T(8,128)(2,1)S(1)} %get-tuple-element.28.refs_0_, bf16[128,256]{1,0:T(8,128)(2,1)S(1)} %get-tuple-element.30.refs_1_, bf16[128,256]{1,0:T(8,128)(2,1)S(1)} %collective-permute-done.refs_2_, bf16[80,256]{1,0:T(8,128)(2,1)S(1)} %collective-permute-done.1.refs_3_, ...), custom_call_target="tpu_custom_call" | custom-call | flops 121634816 | bytes 1024000 | tf_op jit(solution)/shard_map/upsample/pallas_call | solution.py:69
  16.6 0.9 %collective-permute-start.4 = (bf16[512,256]{1,0:T(8,128)(2,1)S(1)}, bf16[512,256]{1,0:T(8,128)(2,1)S(1)}, u32[]{:S(2)}, u32[]{:S(2)}) collective-permute-start(bf16[512,256]{1,0:T(8,128)(2,1)S(1)} %get-tuple-element.41.a_ref), channel_id=1, source_target_pairs={{0,2},{1,3},{2,0},{3,1},{4,6},{5,7},{6,4},{7,5},{8,10},{9,11},{10,... | collective-permute-start | bytes 786440 | tf_op jit(solution)/shard_map/ppermute | solution.py:55
  17.5 0.0 collective-permute-start.5
  17.5 1.9 %collective-permute-start.7 = (bf16[128,512]{1,0:T(8,128)(2,1)S(1)}, bf16[128,512]{1,0:T(8,128)(2,1)S(1)}, u32[]{:S(2)}, u32[]{:S(2)}) collective-permute-start(bf16[128,512]{1,0:T(8,128)(2,1)S(1)} %get-tuple-element.45), channel_id=1, source_target_pairs={{0,4},{1,5},{2,6},{3,7},{4,0},{5,1},{6,2},{7,3},{8,12},{9,13},{10,... | collective-permute-start | bytes 393224 | tf_op jit(solution)/shard_map/ppermute | solution.py:51
  19.4 0.0 collective-permute-done.10.refs_2_
  19.4 1.5 %collective-permute-start.11 = (bf16[768,256]{1,0:T(8,128)(2,1)S(1)}, bf16[768,256]{1,0:T(8,128)(2,1)S(1)}, u32[]{:S(2)}, u32[]{:S(2)}) collective-permute-start(bf16[768,256]{1,0:T(8,128)(2,1)S(1)} %collective-permute-done.10.refs_2_), channel_id=1, source_target_pairs={{0,16},{16,1},{1,17},{17,0},{2,18},{18,3},{3,19},{19,2},{4,20},{20... | collective-permute-start | bytes 1179656 | tf_op jit(solution)/shard_map/ppermute | solution.py:285
  20.9 0.8 %collective-permute-start.6 = (bf16[80,512]{1,0:T(8,128)(2,1)S(1)}, bf16[80,512]{1,0:T(8,128)(2,1)S(1)}, u32[]{:S(2)}, u32[]{:S(2)}) collective-permute-start(bf16[80,512]{1,0:T(8,128)(2,1)S(1)} %get-tuple-element.44), channel_id=1, source_target_pairs={{0,8},{1,9},{2,10},{3,11},{4,12},{5,13},{6,14},{7,15},{8,0},{9,1},... | collective-permute-start | bytes 245768 | tf_op jit(solution)/shard_map/ppermute | solution.py:51
  21.7 5.0 %collective-permute-done.6.refs_2_ = bf16[80,512]{1,0:T(8,128)(2,1)S(1)} collective-permute-done((bf16[80,512]{1,0:T(8,128)(2,1)S(1)}, bf16[80,512]{1,0:T(8,128)(2,1)S(1)}, u32[]{:S(2)}, u32[]{:S(2)}) %collective-permute-start.6) | collective-permute-done | bytes 81952 | tf_op jit(solution)/shard_map/ppermute | solution.py:51
  26.7 0.0 collective-permute-start.8
  26.7 0.0 collective-permute-done.5.refs_1_
  26.7 0.0 collective-permute-done.7.refs_3_
  26.7 0.6 %collect.1 = (f32[128,512]{1,0:T(8,128)S(1)}, bf16[128,512]{1,0:T(8,128)(2,1)S(1)}, f32[8,128]{1,0:T(8,128)}) custom-call(f32[128,512]{1,0:T(8,128)S(1)} %get-tuple-element.42.refs_0_, bf16[128,512]{1,0:T(8,128)(2,1)S(1)} %collective-permute-done.5.refs_1_, bf16[80,512]{1,0:T(8,128)(2,1)S(1)} %collective-permute-done.6.refs_2_, ...), custom_call_target="tpu_custom_call" | custom-call | flops 262144 | bytes 999424 | tf_op jit(solution)/shard_map/collect/pallas_call | solution.py:69
  27.3 0.0 collective-permute-done.4.c_ref
  27.3 0.5 %collective-permute-start.9 = (bf16[512,256]{1,0:T(8,128)(2,1)S(1)}, bf16[512,256]{1,0:T(8,128)(2,1)S(1)}, u32[]{:S(2)}, u32[]{:S(2)}) collective-permute-start(bf16[512,256]{1,0:T(8,128)(2,1)S(1)} %collective-permute-done.4.c_ref), channel_id=1, source_target_pairs={{0,1},{1,0},{2,3},{3,2},{4,5},{5,4},{6,7},{7,6},{8,9},{9,8},{10,11... | collective-permute-start | bytes 786440 | tf_op jit(solution)/shard_map/ppermute | solution.py:55
  27.8 1.2 %collective-permute-start.12 = (bf16[128,512]{1,0:T(8,128)(2,1)S(1)}, bf16[128,512]{1,0:T(8,128)(2,1)S(1)}, u32[]{:S(2)}, u32[]{:S(2)}) collective-permute-start(bf16[128,512]{1,0:T(8,128)(2,1)S(1)} %get-tuple-element.51), channel_id=1, source_target_pairs={{0,2},{1,3},{2,0},{3,1},{4,6},{5,7},{6,4},{7,5},{8,10},{9,11},{10,... | collective-permute-start | bytes 393224 | tf_op jit(solution)/shard_map/ppermute | solution.py:55
  29.0 0.0 collective-permute-start.14
  29.0 0.0 collective-permute-done.8.b_ref
  29.0 0.5 %collective-permute-start.15 = (bf16[768,256]{1,0:T(8,128)(2,1)S(1)}, bf16[768,256]{1,0:T(8,128)(2,1)S(1)}, u32[]{:S(2)}, u32[]{:S(2)}) collective-permute-start(bf16[768,256]{1,0:T(8,128)(2,1)S(1)} %collective-permute-done.10.refs_2_), channel_id=1, source_target_pairs={{0,1},{1,0},{2,3},{3,2},{4,5},{5,4},{6,7},{7,6},{8,9},{9,8},{10,11... | collective-permute-start | bytes 1179656 | tf_op jit(solution)/shard_map/ppermute | solution.py:55
  29.5 1.2 %collective-permute-done.11.ring_ref.refs_3_ = bf16[768,256]{1,0:T(8,128)(2,1)S(1)} collective-permute-done((bf16[768,256]{1,0:T(8,128)(2,1)S(1)}, bf16[768,256]{1,0:T(8,128)(2,1)S(1)}, u32[]{:S(2)}, u32[]{:S(2)}) %collective-permute-start.11) | collective-permute-done | bytes 393248 | tf_op jit(solution)/shard_map/ppermute | solution.py:285
  30.7 0.0 collective-permute-done.9.d_ref
  30.7 2.1 %up_project.1 = bf16[512,1024]{1,0:T(8,128)(2,1)} custom-call(bf16[512,256]{1,0:T(8,128)(2,1)S(1)} %get-tuple-element.41.a_ref, bf16[512,256]{1,0:T(8,128)(2,1)S(1)} %collective-permute-done.8.b_ref, bf16[512,256]{1,0:T(8,128)(2,1)S(1)} %collective-permute-done.4.c_ref, bf16[512,256]{1,0:T(8,128)(2,1)S(1)} %collective-permute-done.9.d_ref, ...), custom_call_target="tpu_custom_call" | custom-call | flops 1073741824 | bytes 1048576 | tf_op jit(solution)/shard_map/up_project/pallas_call | solution.py:347
  32.8 0.4 %collective-permute-done.12 = bf16[128,512]{1,0:T(8,128)(2,1)S(1)} collective-permute-done((bf16[128,512]{1,0:T(8,128)(2,1)S(1)}, bf16[128,512]{1,0:T(8,128)(2,1)S(1)}, u32[]{:S(2)}, u32[]{:S(2)}) %collective-permute-start.12) | collective-permute-done | bytes 131104 | tf_op jit(solution)/shard_map/ppermute | solution.py:55
  33.2 0.1 collective-permute-start.13
  33.3 0.9 %finish_mine.1 = (f32[128,768]{1,0:T(8,128)S(1)}, f32[8,128]{1,0:T(8,128)}) custom-call(bf16[128,512]{1,0:T(8,128)(2,1)S(1)} %add_convert_fusion.refs_0_, bf16[3072,256]{1,0:T(8,128)(2,1)S(1)} %copy-done.1, bf16[768,256]{1,0:T(8,128)(2,1)S(1)} %collective-permute-done.10.refs_2_, bf16[768,256]{1,0:T(8,128)(2,1)S(1)} %collective-permute-done.11.ring_ref.refs_3_), custom_call_target="tpu_custom_call" | custom-call | flops 100663296 | bytes 2883584 | tf_op jit(solution)/shard_map/finish_mine/pallas_call | solution.py:69
  34.2 0.0 collective-permute-done.14.refs_2_
  34.2 0.0 collective-permute-done.15.refs_4_
  34.2 0.4 %collective-permute-done.13.refs_1_ = bf16[128,512]{1,0:T(8,128)(2,1)S(1)} collective-permute-done((bf16[128,512]{1,0:T(8,128)(2,1)S(1)}, bf16[128,512]{1,0:T(8,128)(2,1)S(1)}, u32[]{:S(2)}, u32[]{:S(2)}) %collective-permute-start.13) | collective-permute-done | bytes 131104 | tf_op jit(solution)/shard_map/ppermute | solution.py:55
  34.6 1.1 %finish.1 = (bf16[128,768]{1,0:T(8,128)(2,1)}, f32[8,128]{1,0:T(8,128)}) custom-call(f32[128,768]{1,0:T(8,128)S(1)} %get-tuple-element.52.refs_0_, bf16[128,512]{1,0:T(8,128)(2,1)S(1)} %collective-permute-done.13.refs_1_, bf16[768,256]{1,0:T(8,128)(2,1)S(1)} %collective-permute-done.14.refs_2_, ...), custom_call_target="tpu_custom_call" | custom-call | flops 100663296 | bytes 1900544 | tf_op jit(solution)/shard_map/finish/pallas_call | solution.py:69
  (6 shorter events, 0.0 us)
Async XLA Ops:
  0.6 3.8 %copy-start.1 = (bf16[3072,256]{1,0:T(8,128)(2,1)S(1)}, bf16[3072,256]{1,0:T(8,128)(2,1)}, u32[]{:S(2)}) copy-start(bf16[3072,256]{1,0:T(8,128)(2,1)} %refs_1_.5) | copy-start | bytes 4718596
  3.9 3.2 %copy-start.3 = (bf16[128,3072]{1,0:T(8,128)(2,1)S(1)}, bf16[128,3072]{1,0:T(8,128)(2,1)}, u32[]{:S(2)}) copy-start(bf16[128,3072]{1,0:T(8,128)(2,1)} %refs_0_.2) | copy-start | bytes 2359300
  4.0 9.2 %collective-permute-start.3 = (bf16[512,512]{1,0:T(8,128)(2,1)}, bf16[512,512]{1,0:T(8,128)(2,1)}, u32[]{:S(2)}, u32[]{:S(2)}) collective-permute-start(bf16[512,512]{1,0:T(8,128)(2,1)} %get-tuple-element.34), channel_id=1, source_target_pairs={{0,1},{1,0},{2,3},{3,2},{4,5},{5,4},{6,7},{7,6},{8,9},{9,8},{10,11... | collective-permute-start | bytes 1572872 | tf_op jit(solution)/shard_map/ppermute | solution.py:55
  4.5 7.5 %copy-start.2 = (bf16[512,1024]{1,0:T(8,128)(2,1)S(1)}, bf16[512,1024]{1,0:T(8,128)(2,1)}, u32[]{:S(2)}) copy-start(bf16[512,1024]{1,0:T(8,128)(2,1)} %refs_0_.3) | copy-start | bytes 3145732
  4.5 7.4 %copy-start = (bf16[1024,1024]{1,0:T(8,128)(2,1)S(1)}, bf16[1024,1024]{1,0:T(8,128)(2,1)}, u32[]{:S(2)}) copy-start(bf16[1024,1024]{1,0:T(8,128)(2,1)} %w_ref.1) | copy-start | bytes 6291460
  4.5 14.8 %collective-permute-start.10 = (bf16[768,256]{1,0:T(8,128)(2,1)S(1)}, bf16[768,256]{1,0:T(8,128)(2,1)S(1)}, u32[]{:S(2)}, u32[]{:S(2)}) collective-permute-start(bf16[768,256]{1,0:T(8,128)(2,1)S(1)} %get-tuple-element.55), channel_id=1, source_target_pairs={{0,2},{1,3},{2,0},{3,1},{4,6},{5,7},{6,4},{7,5},{8,10},{9,11},{10,... | collective-permute-start | bytes 1179656 | tf_op jit(solution)/shard_map/ppermute | solution.py:55
  7.5 8.1 %collective-permute-start = (bf16[128,256]{1,0:T(8,128)(2,1)S(1)}, bf16[128,256]{1,0:T(8,128)(2,1)S(1)}, u32[]{:S(2)}, u32[]{:S(2)}) collective-permute-start(bf16[128,256]{1,0:T(8,128)(2,1)S(1)} %get-tuple-element.30.refs_1_), channel_id=1, source_target_pairs={{0,1},{1,0},{2,3},{3,2},{4,8},{5,9},{6,10},{7,11},{8,4},{9,5},{10,... | collective-permute-start | bytes 196616 | tf_op jit(solution)/shard_map/ppermute | solution.py:51
  7.8 7.9 %collective-permute-start.2 = (bf16[128,256]{1,0:T(8,128)(2,1)S(1)}, bf16[128,256]{1,0:T(8,128)(2,1)S(1)}, u32[]{:S(2)}, u32[]{:S(2)}) collective-permute-start(bf16[128,256]{1,0:T(8,128)(2,1)S(1)} %get-tuple-element.30.refs_1_), channel_id=1, source_target_pairs={{0,4},{1,5},{2,6},{3,7},{4,0},{5,1},{6,2},{7,3},{8,12},{9,13},{10,... | collective-permute-start | bytes 196616 | tf_op jit(solution)/shard_map/ppermute | solution.py:51
  10.8 4.9 %collective-permute-start.1 = (bf16[80,256]{1,0:T(8,128)(2,1)S(1)}, bf16[80,256]{1,0:T(8,128)(2,1)S(1)}, u32[]{:S(2)}, u32[]{:S(2)}) collective-permute-start(bf16[80,256]{1,0:T(8,128)(2,1)S(1)} %get-tuple-element.31), channel_id=1, source_target_pairs={{0,8},{1,9},{2,10},{3,11},{4,12},{5,13},{6,14},{7,15},{8,0},{9,1},... | collective-permute-start | bytes 122888 | tf_op jit(solution)/shard_map/ppermute | solution.py:51
  16.6 10.7 %collective-permute-start.4 = (bf16[512,256]{1,0:T(8,128)(2,1)S(1)}, bf16[512,256]{1,0:T(8,128)(2,1)S(1)}, u32[]{:S(2)}, u32[]{:S(2)}) collective-permute-start(bf16[512,256]{1,0:T(8,128)(2,1)S(1)} %get-tuple-element.41.a_ref), channel_id=1, source_target_pairs={{0,2},{1,3},{2,0},{3,1},{4,6},{5,7},{6,4},{7,5},{8,10},{9,11},{10,... | collective-permute-start | bytes 786440 | tf_op jit(solution)/shard_map/ppermute | solution.py:55
  17.5 9.2 %collective-permute-start.5 = (bf16[128,512]{1,0:T(8,128)(2,1)S(1)}, bf16[128,512]{1,0:T(8,128)(2,1)S(1)}, u32[]{:S(2)}, u32[]{:S(2)}) collective-permute-start(bf16[128,512]{1,0:T(8,128)(2,1)S(1)} %get-tuple-element.43), channel_id=1, source_target_pairs={{0,1},{1,0},{2,3},{3,2},{4,8},{5,9},{6,10},{7,11},{8,4},{9,5},{10,... | collective-permute-start | bytes 393224 | tf_op jit(solution)/shard_map/ppermute | solution.py:51
  17.5 9.2 %collective-permute-start.7 = (bf16[128,512]{1,0:T(8,128)(2,1)S(1)}, bf16[128,512]{1,0:T(8,128)(2,1)S(1)}, u32[]{:S(2)}, u32[]{:S(2)}) collective-permute-start(bf16[128,512]{1,0:T(8,128)(2,1)S(1)} %get-tuple-element.45), channel_id=1, source_target_pairs={{0,4},{1,5},{2,6},{3,7},{4,0},{5,1},{6,2},{7,3},{8,12},{9,13},{10,... | collective-permute-start | bytes 393224 | tf_op jit(solution)/shard_map/ppermute | solution.py:51
  19.4 11.3 %collective-permute-start.11 = (bf16[768,256]{1,0:T(8,128)(2,1)S(1)}, bf16[768,256]{1,0:T(8,128)(2,1)S(1)}, u32[]{:S(2)}, u32[]{:S(2)}) collective-permute-start(bf16[768,256]{1,0:T(8,128)(2,1)S(1)} %collective-permute-done.10.refs_2_), channel_id=1, source_target_pairs={{0,16},{16,1},{1,17},{17,0},{2,18},{18,3},{3,19},{19,2},{4,20},{20... | collective-permute-start | bytes 1179656 | tf_op jit(solution)/shard_map/ppermute | solution.py:285
  20.9 5.8 %collective-permute-start.6 = (bf16[80,512]{1,0:T(8,128)(2,1)S(1)}, bf16[80,512]{1,0:T(8,128)(2,1)S(1)}, u32[]{:S(2)}, u32[]{:S(2)}) collective-permute-start(bf16[80,512]{1,0:T(8,128)(2,1)S(1)} %get-tuple-element.44), channel_id=1, source_target_pairs={{0,8},{1,9},{2,10},{3,11},{4,12},{5,13},{6,14},{7,15},{8,0},{9,1},... | collective-permute-start | bytes 245768 | tf_op jit(solution)/shard_map/ppermute | solution.py:51
  26.7 2.3 %collective-permute-start.8 = (bf16[512,256]{1,0:T(8,128)(2,1)S(1)}, bf16[512,256]{1,0:T(8,128)(2,1)S(1)}, u32[]{:S(2)}, u32[]{:S(2)}) collective-permute-start(bf16[512,256]{1,0:T(8,128)(2,1)S(1)} %get-tuple-element.41.a_ref), channel_id=1, source_target_pairs={{0,1},{1,0},{2,3},{3,2},{4,5},{5,4},{6,7},{7,6},{8,9},{9,8},{10,11... | collective-permute-start | bytes 786440 | tf_op jit(solution)/shard_map/ppermute | solution.py:55
  27.3 3.4 %collective-permute-start.9 = (bf16[512,256]{1,0:T(8,128)(2,1)S(1)}, bf16[512,256]{1,0:T(8,128)(2,1)S(1)}, u32[]{:S(2)}, u32[]{:S(2)}) collective-permute-start(bf16[512,256]{1,0:T(8,128)(2,1)S(1)} %collective-permute-done.4.c_ref), channel_id=1, source_target_pairs={{0,1},{1,0},{2,3},{3,2},{4,5},{5,4},{6,7},{7,6},{8,9},{9,8},{10,11... | collective-permute-start | bytes 786440 | tf_op jit(solution)/shard_map/ppermute | solution.py:55
  27.8 5.4 %collective-permute-start.12 = (bf16[128,512]{1,0:T(8,128)(2,1)S(1)}, bf16[128,512]{1,0:T(8,128)(2,1)S(1)}, u32[]{:S(2)}, u32[]{:S(2)}) collective-permute-start(bf16[128,512]{1,0:T(8,128)(2,1)S(1)} %get-tuple-element.51), channel_id=1, source_target_pairs={{0,2},{1,3},{2,0},{3,1},{4,6},{5,7},{6,4},{7,5},{8,10},{9,11},{10,... | collective-permute-start | bytes 393224 | tf_op jit(solution)/shard_map/ppermute | solution.py:55
  29.0 5.3 %collective-permute-start.14 = (bf16[768,256]{1,0:T(8,128)(2,1)S(1)}, bf16[768,256]{1,0:T(8,128)(2,1)S(1)}, u32[]{:S(2)}, u32[]{:S(2)}) collective-permute-start(bf16[768,256]{1,0:T(8,128)(2,1)S(1)} %get-tuple-element.54), channel_id=1, source_target_pairs={{0,1},{1,0},{2,3},{3,2},{4,5},{5,4},{6,7},{7,6},{8,9},{9,8},{10,11... | collective-permute-start | bytes 1179656 | tf_op jit(solution)/shard_map/ppermute | solution.py:55
  29.0 5.2 %collective-permute-start.15 = (bf16[768,256]{1,0:T(8,128)(2,1)S(1)}, bf16[768,256]{1,0:T(8,128)(2,1)S(1)}, u32[]{:S(2)}, u32[]{:S(2)}) collective-permute-start(bf16[768,256]{1,0:T(8,128)(2,1)S(1)} %collective-permute-done.10.refs_2_), channel_id=1, source_target_pairs={{0,1},{1,0},{2,3},{3,2},{4,5},{5,4},{6,7},{7,6},{8,9},{9,8},{10,11... | collective-permute-start | bytes 1179656 | tf_op jit(solution)/shard_map/ppermute | solution.py:55
  33.2 1.4 %collective-permute-start.13 = (bf16[128,512]{1,0:T(8,128)(2,1)S(1)}, bf16[128,512]{1,0:T(8,128)(2,1)S(1)}, u32[]{:S(2)}, u32[]{:S(2)}) collective-permute-start(bf16[128,512]{1,0:T(8,128)(2,1)S(1)} %add_convert_fusion.refs_0_), channel_id=1, source_target_pairs={{0,1},{1,0},{2,3},{3,2},{4,5},{5,4},{6,7},{7,6},{8,9},{9,8},{10,11... | collective-permute-start | bytes 393224 | tf_op jit(solution)/shard_map/ppermute | solution.py:55

commit v4 on v3

--- a/solution.py
+++ b/solution.py
@@ -55,23 +55,26 @@
     return lax.ppermute(value, "tensor", [(i, i ^ mask) for i in range(4)])
 
 
-def call(kernel, outs, *args, flops, scalars=(), after=()):
+def call(kernel, outs, *args, flops, after=(), token=False):
     moved = sum(a.size * a.dtype.itemsize for a in args)
     moved += sum(o.size * o.dtype.itemsize for o in outs)
-    spaces = [pltpu.SMEM if k in scalars else pltpu.VMEM for k in range(len(args))]
-    spaces += [pl.ANY] * len(after)
+    spaces = [pltpu.VMEM] * len(args) + [pl.ANY] * len(after)
     inputs = len(args)
+    outs = list(outs) + [shape((8, 128), F32)] * token
 
     def run(*refs):
-        kernel(*refs[:inputs], *refs[inputs + len(after) : -1])
-        refs[-1][...] = jnp.zeros_like(refs[-1])
+        results = refs[inputs + len(after) :]
+        if token:
+            *results, token_ref = results
+            token_ref[...] = jnp.zeros_like(token_ref)
+        kernel(*refs[:inputs], *results)
 
     return pl.pallas_call(
         run,
-        out_shape=list(outs) + [shape((8, 128), F32)],
+        out_shape=outs,
         name=getattr(kernel, "func", kernel).__name__,
         in_specs=[pl.BlockSpec(memory_space=space) for space in spaces],
-        out_specs=[pl.BlockSpec(memory_space=pltpu.VMEM)] * (len(outs) + 1),
+        out_specs=[pl.BlockSpec(memory_space=pltpu.VMEM)] * len(outs),
         compiler_params=pltpu.CompilerParams(vmem_limit_bytes=16 << 20),
         cost_estimate=pl.CostEstimate(flops=flops, bytes_accessed=moved, transcendentals=0),
     )(*args, *after)
@@ -112,17 +115,6 @@
         at = (lax.axis_index("tensor") ^ mask) * size
         return ref[pl.ds(pl.multiple_of(at, size), size), :]
 
-    here = lax.axis_index("tensor")
-    cube = w_in.reshape(4, share, width)
-
-    def quarter(index):
-        return lax.dynamic_index_in_dim(cube, index, 0, keepdims=False)
-
-    half = lax.axis_index("group") if groups == 2 else 0
-    w_core = swap(quarter(here ^ 1), 1)
-    w_x_sent = quarter(here ^ 2 ^ half)
-    w_x = swap(w_x_sent, 2)
-
     total_cols = breadth * len(rows)
 
     def grad_part(masks, d_ref, w_ref, out_ref):
@@ -155,8 +147,11 @@
             pick = (down - off_ref[b] == across_j).astype(F32).astype(BF16)
             turned_ref[:, part] = dot_t(pick, weights).astype(BF16)
 
+    def half():
+        return lax.axis_index("group") if groups == 2 else 0
+
     def open_up(
-        off_hbm, weights_hbm, d_hbm, w_hbm, band_ref, turned_ref, out_ref, token_ref, off, weights, d_vm, w_vm, sems
+        off_hbm, weights_hbm, d_hbm, w_hbm, in_hbm, band_ref, turned_ref, d_vm, w_vm, x_ref, off, weights, sems
     ):
         at = lax.axis_index("tensor")
         loads = []
@@ -175,34 +170,36 @@
             for q in (2 * k, 2 * k + 1):
                 part = pl.ds(q * step, step)
                 load(d_hbm.at[part, :], d_vm.at[part, :])
+        quarter = at ^ 2 ^ half()
+        load(in_hbm.at[pl.ds(pl.multiple_of(quarter * share, share), share), :], x_ref)
         for copy in loads[:2]:
             copy.wait()
-        token_ref[...] = jnp.zeros_like(token_ref)
         spread(off, weights, band_ref, turned_ref)
         for copy in loads[2:]:
             copy.wait()
+
+    def grad_for_other(d_ref, w_ref, out_ref):
         for k in range(2):
-            out_ref[:, k * width : (k + 1) * width] = dot_t(d_vm[...], w_vm[k]).astype(BF16)
+            out_ref[:, k * width : (k + 1) * width] = dot_t(d_ref[...], w_ref[k]).astype(BF16)
 
     def fixed(value):
         return pltpu.with_memory_space_constraint(value, pltpu.HBM)
 
-    band, turned, grad_sent, opened = pl.pallas_call(
+    band, turned, d_near, w_near, w_for_x = pl.pallas_call(
         open_up,
         out_shape=[
             shape((bytes_here, total_cols)),
             shape((total_cols, bytes_here)),
-            shape((bytes_here, 2 * width)),
-            shape((8, 128), F32),
+            shape((bytes_here, hidden)),
+            shape((2, width, hidden)),
+            shape((share, width)),
         ],
-        in_specs=[pl.BlockSpec(memory_space=pltpu.HBM)] * 4,
-        out_specs=[pl.BlockSpec(memory_space=pltpu.VMEM)] * 4,
+        in_specs=[pl.BlockSpec(memory_space=pltpu.HBM)] * 5,
+        out_specs=[pl.BlockSpec(memory_space=pltpu.VMEM)] * 5,
         scratch_shapes=[
             pltpu.SMEM((blocks,), jnp.int32),
             pltpu.VMEM((bytes_here, breadth), BF16),
-            pltpu.VMEM((bytes_here, hidden), BF16),
-            pltpu.VMEM((2, width, hidden), BF16),
-            pltpu.SemaphoreType.DMA((8,)),
+            pltpu.SemaphoreType.DMA((9,)),
         ],
         name="open_up",
         compiler_params=pltpu.CompilerParams(vmem_limit_bytes=16 << 20),
@@ -211,7 +208,17 @@
             bytes_accessed=2 * (2 * width + bytes_here) * hidden,
             transcendentals=0,
         ),
-    )(fixed(offsets), fixed(band_weights), fixed(d_up), fixed(w_up))
+    )(fixed(offsets), fixed(band_weights), fixed(d_up), fixed(w_up), fixed(w_in))
+    w_x = swap(w_for_x, 2)
+    product = 4 * bytes_here * width * hidden
+    grad_sent, opened = call(
+        grad_for_other,
+        [shape((bytes_here, 2 * width))],
+        d_near,
+        w_near,
+        flops=product,
+        token=True,
+    )
     grad_got = swap(grad_sent, 1)
 
     def project(spans_ref, w_ref, out_ref, *cut_refs):
@@ -226,16 +233,17 @@
         w_in,
         flops=2 * span_rows * depth * width,
         after=(opened,),
+        token=True,
     )
     cut_of = dict(zip(longs, cuts))
     pieces = [reduced] + [trade(cut_of.get(p, reduced), p, count) for p in pairs]
 
-    grad_kept, _ = call(
+    (grad_kept,) = call(
         functools.partial(grad_part, (0, 2)),
         [shape((bytes_here, 2 * width), F32)],
-        d_up,
+        d_near,
         w_up,
-        flops=4 * bytes_here * width * hidden,
+        flops=product,
         after=(reduced_done,),
     )
 
@@ -257,6 +265,7 @@
         grad_got,
         turned,
         flops=products[1],
+        token=True,
     )
     came = [trade(share_sent, pairs[0], count)]
     for k in range(2, len(rows)):
@@ -266,7 +275,8 @@
             grad,
             turned,
             flops=products[k],
-            after=(share_done,),
+            after=(share_done, *pieces[1:]) if k == len(rows) - 1 else (share_done,),
+            token=True,
         )
         came.append(trade(share_sent, pairs[k - 1], count))
     own, own_done = call(
@@ -276,17 +286,8 @@
         turned,
         flops=products[0],
         after=(share_done,),
-    )
-
-    if groups == 2:
-        ring = []
-        for t in range(4):
-            ring += [(t, 4 + t), (4 + t, t ^ 1)]
-        w_ring = lax.ppermute(w_x, ("group", "tensor"), ring)
-        w_side = swap(w_x, 1)
-    else:
-        w_ring = swap(quarter(here ^ 3), 3)
-        w_side = w_ring
+        token=True,
+    )
 
     def upsample(band_ref, *refs):
         *piece_refs, out_ref = refs
@@ -295,16 +296,21 @@
             acc += dot(band_ref[:, cols[k] : cols[k] + rows[k]], ref[...])
         out_ref[...] = acc.astype(BF16)
 
-    upsampled, _ = call(
+    (upsampled,) = call(
         upsample,
         [shape((bytes_here, width))],
         band,
         *pieces,
         flops=2 * bytes_here * width * sum(rows),
-        after=(own_done,),
+        after=(own_done, w_x),
     )
     up_x = swap(upsampled, 2)
-    up_core = swap(upsampled, 1)
+
+    if groups == 2:
+        w_y = lax.ppermute(w_x, "group", [(0, 1), (1, 0)])
+    else:
+        cube = w_in.reshape(4, share, width)
+        w_y = swap(lax.dynamic_index_in_dim(cube, lax.axis_index("tensor") ^ 3, 0, keepdims=False), 2)
 
     def collect(own_ref, *refs):
         *came_refs, sum_ref, sent_ref = refs
@@ -317,74 +323,106 @@
         sent_ref[:, width:] = sum_ref[:, :width].astype(BF16)
         sent_ref[:, :width] = sum_ref[:, width:].astype(BF16)
 
-    summed, sent, _ = call(
+    summed, sent = call(
         collect,
         [shape((span_rows, 2 * width), F32), shape((span_rows, 2 * width))],
         own,
         *came,
-        flops=8 * span_rows * width,
-    )
+        flops=10**10,
+    )
+
     over_x = swap(sent, 2)
-    up_x, summed = lax.optimization_barrier((up_x, summed))
-    up_both = swap(up_x, 1)
-
-    def up_project(a_ref, b_ref, c_ref, d_ref, w_ref, ring_ref, out_hbm, out_vm, sems):
-        refs = (a_ref, b_ref, c_ref, d_ref)
+
+    def up_near(own_ref, came_ref, w_ref, acc_ref):
+        acc = dot(own_ref[...], block_of(w_ref, 0, width))
+        acc_ref[...] = acc + dot(came_ref[...], block_of(w_ref, 2, width))
+
+    (up_acc,) = call(
+        up_near,
+        [shape((bytes_here, hidden), F32)],
+        upsampled,
+        up_x,
+        w_up,
+        flops=product,
+    )
+
+    def pack(own_ref, came_ref, out_ref):
+        out_ref[:, :width] = own_ref[...]
+        out_ref[:, width:] = came_ref[...]
+
+    (up_pair,) = call(pack, [shape((bytes_here, 2 * width))], upsampled, up_x, flops=bytes_here, after=(over_x, w_y, up_acc))
+    up_other = swap(up_pair, 1)
+
+    def combine(sum_ref, came_ref, out_ref):
+        out_ref[...] = (sum_ref[...] + came_ref[...].astype(F32)).astype(BF16)
+
+    (d_reduced,) = call(
+        combine,
+        [shape((span_rows, 2 * width))],
+        summed,
+        over_x,
+        flops=2 * span_rows * width,
+        after=(up_acc, w_y),
+    )
+    def finish_part(mask, mine_ref, w_ref, x_ref, y_ref, out_ref):
+        first = groups != 2 or lax.axis_index("group") == 0
+        near, far = (x_ref, y_ref) if mask == 0 else (y_ref, x_ref)
+        across = near[...] if groups != 2 else jnp.where(first, near[...], far[...])
+        part = dot_t(mine_ref[:, :width], block_of(w_ref, mask, share))
+        out_ref[...] = (part + dot_t(mine_ref[:, width:], across)).astype(out_ref.dtype)
+
+    def finish(mask, kind, after=()):
+        return call(
+            functools.partial(finish_part, mask),
+            [shape((span_rows, share), kind)],
+            d_reduced,
+            w_in,
+            w_x,
+            w_y,
+            flops=4 * span_rows * width * share,
+            after=after,
+        )[0]
+
+    part_sent = finish(1, BF16)
+    part_got = swap(part_sent, 1)
+    part_kept = finish(0, F32, after=(part_sent,))
+
+    def close(acc_ref, other_ref, w_ref, kept_ref, got_ref, up_hbm, spans_hbm, up_vm, spans_vm, sems):
+        copies = []
+
+        def store(source, target):
+            copies.append(pltpu.make_async_copy(source, target, sems.at[len(copies)]))
+            copies[-1].start()
+
+        spans_vm[...] = (kept_ref[...] + got_ref[...].astype(F32)).astype(BF16)
+        store(spans_vm, spans_hbm)
         step = bytes_here // 4
-        copies = []
         for q in range(4):
             part = slice(q * step, (q + 1) * step)
-            acc = 0.0
-            for mask, ref in enumerate(refs):
-                acc += dot(ref[part, :], block_of(w_ref, mask, width))
-            out_vm[part, :] = acc.astype(BF16)
+            acc = acc_ref[part, :] + dot(other_ref[part, :width], block_of(w_ref, 1, width))
+            acc += dot(other_ref[part, width:], block_of(w_ref, 3, width))
+            up_vm[part, :] = acc.astype(BF16)
             part = pl.ds(q * step, step)
-            copies.append(pltpu.make_async_copy(out_vm.at[part, :], out_hbm.at[part, :], sems.at[q]))
-            copies[-1].start()
+            store(up_vm.at[part, :], up_hbm.at[part, :])
         for copy in copies:
             copy.wait()
 
-    up_proj = pl.pallas_call(
-        up_project,
-        out_shape=shape((bytes_here, hidden)),
-        in_specs=[pl.BlockSpec(memory_space=pltpu.VMEM)] * 5 + [pl.BlockSpec(memory_space=pl.ANY)],
-        out_specs=pl.BlockSpec(memory_space=pltpu.HBM),
-        scratch_shapes=[pltpu.VMEM((bytes_here, hidden), BF16), pltpu.SemaphoreType.DMA((4,))],
-        name="up_project",
+    up_proj, d_spans = pl.pallas_call(
+        close,
+        out_shape=[shape((bytes_here, hidden)), shape((span_rows, share))],
+        in_specs=[pl.BlockSpec(memory_space=pltpu.VMEM)] * 5,
+        out_specs=[pl.BlockSpec(memory_space=pltpu.HBM)] * 2,
+        scratch_shapes=[
+            pltpu.VMEM((bytes_here, hidden), BF16),
+            pltpu.VMEM((span_rows, share), BF16),
+            pltpu.SemaphoreType.DMA((5,)),
+        ],
+        name="close",
         compiler_params=pltpu.CompilerParams(vmem_limit_bytes=16 << 20),
         cost_estimate=pl.CostEstimate(
-            flops=8 * bytes_here * width * hidden,
-            bytes_accessed=2 * bytes_here * hidden,
-            transcendentals=0,
+            flops=product, bytes_accessed=2 * bytes_here * hidden, transcendentals=0
         ),
-    )(upsampled, up_core, up_x, up_both, w_up, w_ring)
-
-    summed, up_proj = lax.optimization_barrier((summed, up_proj))
-    d_reduced = (summed + over_x.astype(F32)).astype(BF16)
-    d_other = swap(d_reduced, 1)
-
-    def finish_mine(mine_ref, w_ref, x_ref, ring_ref, out_ref):
-        near = x_ref[...]
-        if groups == 2:
-            near = jnp.where(lax.axis_index("group") == 0, near, ring_ref[...])
-        part = dot_t(mine_ref[:, :width], block_of(w_ref, 0, share))
-        out_ref[...] = part + dot_t(mine_ref[:, width:], near)
-
-    def finish(part_ref, other_ref, core_ref, ring_ref, side_ref, out_ref):
-        cross = ring_ref[...]
-        if groups == 2:
-            cross = jnp.where(lax.axis_index("group") == 0, cross, side_ref[...])
-        part = part_ref[...] + dot_t(other_ref[:, :width], core_ref[...])
-        out_ref[...] = (part + dot_t(other_ref[:, width:], cross)).astype(BF16)
-
-    work = 4 * span_rows * width * share
-    mine, _ = call(
-        finish_mine, [shape((span_rows, share), F32)], d_reduced, w_in, w_x, w_ring, flops=work
-    )
-    d_spans, _ = call(
-        finish, [shape((span_rows, share))], mine, d_other, w_core, w_ring, w_side, flops=work
-    )
-
+    )(up_acc, up_other, w_up, part_kept, part_got)
     return (up_proj, d_spans)
 
 

time: 35.9 us -> 33.7 us (0.939)
  Pallas kernels: 12.5 us -> 8.3 us
  waiting for transfers between devices: 7.47 us -> 10 us
  starting transfers between devices: 14.9 us -> 14.4 us
    ppermute x9 -> x6, waiting for transfers between devices: 0.82 us -> 4.9 us  [swap(): return lax.ppermute(value, 'tensor', [(i, i ^ mask) for i in range(4)])]
    pallas_call x11 -> x15, Pallas kernels: 9.25 us -> 6.46 us  [the longest x14 4.92 us: call(): pl.pallas_call(run, out_shape=outs, name=getattr(kernel, 'func', kernel)....]
    pallas_call x1, Pallas kernels: 3.29 us -> 1.84 us  [body(): pl.pallas_call(open_up, out_shape=[shape((bytes_here, total_cols)), shape...]
    ppermute x9 -> x6, starting transfers between devices: 6.24 us -> 4.91 us  [swap(): return lax.ppermute(value, 'tensor', [(i, i ^ mask) for i in range(4)])]
    ppermute x1, waiting for transfers between devices: 1.25 us -> 0.01 us  [body(): w_y = lax.ppermute(w_x, 'group', [(0, 1), (1, 0)])]
    ppermute x6, starting transfers between devices: 7.11 us -> 7.94 us  [trade(): return lax.ppermute(value, ('seq', 'tensor'), pairs)]
  transfers between devices with their start and end apart: 16 -> 13, of which waited for: 5 -> 5; matrix products, arithmetic and copies ran while one was open for 0% -> 0% of each run, Pallas kernels for 23% -> 12%
where the time goes in v4:
time: 33.7 us; the launch traced here: 33.5 us
  starting transfers between devices  14.4 us (43%)
  waiting for transfers between devices  10 us (30%)
  Pallas kernels  8.3 us (25%)
  between operations  0.78 us (2%)
    ppermute x6, starting transfers between devices, trade(): return lax.ppermute(value, ('seq', 'tensor'), pairs)  7.94 us
    ppermute x6, waiting for transfers between devices, trade(): return lax.ppermute(value, ('seq', 'tensor'), pairs)  5.15 us
    pallas_call x14, Pallas kernels, call(): pl.pallas_call(run, out_shape=outs, name=getattr(kernel, 'func', kernel)....  4.92 us
    ppermute x6, starting transfers between devices, swap(): return lax.ppermute(value, 'tensor', [(i, i ^ mask) for i in range(4)])  4.91 us
    ppermute x6, waiting for transfers between devices, swap(): return lax.ppermute(value, 'tensor', [(i, i ^ mask) for i in range(4)])  4.9 us
    pallas_call x1, Pallas kernels, body(): pl.pallas_call(open_up, out_shape=[shape((bytes_here, total_cols)), shape...  1.84 us
    pallas_call x1, Pallas kernels, body(): pl.pallas_call(close, out_shape=[shape((bytes_here, hidden)), shape((span...  1.54 us
    ppermute x1, starting transfers between devices, body(): w_y = lax.ppermute(w_x, 'group', [(0, 1), (1, 0)])  1.52 us
  transfers between devices with their start and end apart: 13, of which 5 were waited for; matrix products, arithmetic and copies ran while one was open for 0% of the time, Pallas kernels for 12%

profile of v4, /device:TPU:0, one launch (start us, length us, event | category | flops | bytes accessed | tf_op | source)
XLA Modules:
  0.0 33.5 jit_solution(14865608909415152328)
XLA Ops:
  0.6 0.0 copy-start.2
  0.6 1.8 %open_up.1 = (bf16[512,512]{1,0:T(8,128)(2,1)S(1)}, bf16[512,512]{1,0:T(8,128)(2,1)S(1)}, bf16[512,1024]{1,0:T(8,128)(2,1)S(1)}, bf16[2,256,1024]{2,1,0:T(8,128)(2,1)S(1)}, bf16[768,256]{1,0:T(8,128)(2,1)S(1)}) custom-call(s32[4]{0:T(128)} %off_hbm.1, bf16[512,128]{1,0:T(8,128)(2,1)} %weights_hbm.1, bf16[512,1024]{1,0:T(8,128)(2,1)} %d_hbm.1, ...), custom_call_target="tpu_custom_call" | custom-call | flops 536870912 | bytes 2097152 | tf_op jit(solution)/shard_map/open_up/pallas_call | solution.py:188
  2.5 0.0 copy-start.1
  2.5 0.0 copy-start
  2.5 0.7 %grad_for_other.1 = (bf16[512,512]{1,0:T(8,128)(2,1)S(1)}, f32[8,128]{1,0:T(8,128)S(1)}) custom-call(bf16[512,1024]{1,0:T(8,128)(2,1)S(1)} %get-tuple-element.24.refs_0_, bf16[2,256,1024]{2,1,0:T(8,128)(2,1)S(1)} %get-tuple-element.25.refs_1_), custom_call_target="tpu_custom_call" | custom-call | flops 536870912 | bytes 2621440 | tf_op jit(solution)/shard_map/grad_for_other/pallas_call | solution.py:72
  3.3 0.5 %collective-permute-start.3 = (bf16[512,512]{1,0:T(8,128)(2,1)S(1)}, bf16[512,512]{1,0:T(8,128)(2,1)S(1)}, u32[]{:S(2)}, u32[]{:S(2)}) collective-permute-start(bf16[512,512]{1,0:T(8,128)(2,1)S(1)} %get-tuple-element.30), channel_id=1, source_target_pairs={{0,1},{1,0},{2,3},{3,2},{4,5},{5,4},{6,7},{7,6},{8,9},{9,8},{10,11... | collective-permute-start | bytes 1572872 | tf_op jit(solution)/shard_map/ppermute | solution.py:55
  3.8 2.6 %collective-permute-start.4 = (bf16[768,256]{1,0:T(8,128)(2,1)S(1)}, bf16[768,256]{1,0:T(8,128)(2,1)S(1)}, u32[]{:S(2)}, u32[]{:S(2)}) collective-permute-start(bf16[768,256]{1,0:T(8,128)(2,1)S(1)} %get-tuple-element.37), channel_id=1, source_target_pairs={{0,2},{1,3},{2,0},{3,1},{4,6},{5,7},{6,4},{7,5},{8,10},{9,11},{10,... | collective-permute-start | bytes 1179656 | tf_op jit(solution)/shard_map/ppermute | solution.py:55
  6.3 0.0 copy-done.2
  6.3 0.0 copy-done.1
  6.4 0.4 %project.1 = (bf16[128,256]{1,0:T(8,128)(2,1)S(1)}, bf16[80,256]{1,0:T(8,128)(2,1)S(1)}, f32[8,128]{1,0:T(8,128)S(1)}) custom-call(bf16[128,3072]{1,0:T(8,128)(2,1)S(1)} %copy-done.2, bf16[3072,256]{1,0:T(8,128)(2,1)S(1)} %copy-done.1, f32[8,128]{1,0:T(8,128)S(1)} %get-tuple-element.26.refs_2_), custom_call_target="tpu_custom_call" | custom-call | flops 201326592 | bytes 2465792 | tf_op jit(solution)/shard_map/project/pallas_call | solution.py:72
  6.7 0.2 collective-permute-start
  7.0 3.0 %collective-permute-start.2 = (bf16[128,256]{1,0:T(8,128)(2,1)S(1)}, bf16[128,256]{1,0:T(8,128)(2,1)S(1)}, u32[]{:S(2)}, u32[]{:S(2)}) collective-permute-start(bf16[128,256]{1,0:T(8,128)(2,1)S(1)} %get-tuple-element.27.refs_1_), channel_id=1, source_target_pairs={{0,4},{1,5},{2,6},{3,7},{4,0},{5,1},{6,2},{7,3},{8,12},{9,13},{10,... | collective-permute-start | bytes 196616 | tf_op jit(solution)/shard_map/ppermute | solution.py:51
  10.0 1.2 %collective-permute-start.1 = (bf16[80,256]{1,0:T(8,128)(2,1)S(1)}, bf16[80,256]{1,0:T(8,128)(2,1)S(1)}, u32[]{:S(2)}, u32[]{:S(2)}) collective-permute-start(bf16[80,256]{1,0:T(8,128)(2,1)S(1)} %get-tuple-element.28), channel_id=1, source_target_pairs={{0,8},{1,9},{2,10},{3,11},{4,12},{5,13},{6,14},{7,15},{8,0},{9,1},... | collective-permute-start | bytes 122888 | tf_op jit(solution)/shard_map/ppermute | solution.py:51
  11.1 0.0 copy-done
  11.1 0.7 %grad_part.1.refs_0_ = f32[512,512]{1,0:T(8,128)S(1)} custom-call(bf16[512,1024]{1,0:T(8,128)(2,1)S(1)} %get-tuple-element.24.refs_0_, bf16[1024,1024]{1,0:T(8,128)(2,1)S(1)} %copy-done, f32[8,128]{1,0:T(8,128)S(1)} %get-tuple-element.29.refs_2_), custom_call_target="tpu_custom_call" | custom-call | flops 536870912 | bytes 4194304 | tf_op jit(solution)/shard_map/grad_part/pallas_call | solution.py:72
  11.9 0.0 collective-permute-done.3.refs_1_
  11.9 0.3 first_share.1
  12.2 0.2 next_share.3
  12.4 2.4 %collective-permute-done.1.refs_4_.refs_3_ = bf16[80,256]{1,0:T(8,128)(2,1)S(1)} collective-permute-done((bf16[80,256]{1,0:T(8,128)(2,1)S(1)}, bf16[80,256]{1,0:T(8,128)(2,1)S(1)}, u32[]{:S(2)}, u32[]{:S(2)}) %collective-permute-start.1) | collective-permute-done | bytes 40992 | tf_op jit(solution)/shard_map/ppermute | solution.py:51
  14.9 0.0 collective-permute-done.refs_3_.refs_2_
  14.9 0.0 collective-permute-done.2.refs_5_.refs_4_
  14.9 0.2 next_share.4
  15.1 0.1 collective-permute-start.8
  15.2 0.0 collective-permute-start.6
  15.3 3.4 %collective-permute-start.7 = (bf16[80,512]{1,0:T(8,128)(2,1)S(1)}, bf16[80,512]{1,0:T(8,128)(2,1)S(1)}, u32[]{:S(2)}, u32[]{:S(2)}) collective-permute-start(bf16[80,512]{1,0:T(8,128)(2,1)S(1)} %get-tuple-element.40), channel_id=1, source_target_pairs={{0,8},{1,9},{2,10},{3,11},{4,12},{5,13},{6,14},{7,15},{8,0},{9,1},... | collective-permute-start | bytes 245768 | tf_op jit(solution)/shard_map/ppermute | solution.py:51
  18.7 0.0 collective-permute-done.4.refs_6_.refs_2_
  18.7 1.5 %collective-permute-start.10 = (bf16[768,256]{1,0:T(8,128)(2,1)S(1)}, bf16[768,256]{1,0:T(8,128)(2,1)S(1)}, u32[]{:S(2)}, u32[]{:S(2)}) collective-permute-start(bf16[768,256]{1,0:T(8,128)(2,1)S(1)} %collective-permute-done.4.refs_6_.refs_2_), channel_id=1, source_target_pairs={{0,16},{16,0},{1,17},{17,1},{2,18},{18,2},{3,19},{19,3},{4,20},{20... | collective-permute-start | bytes 1179656 | tf_op jit(solution)/shard_map/ppermute | solution.py:310
  20.2 0.2 next_share.5
  20.4 0.4 %upsample.1.refs_0_ = bf16[512,256]{1,0:T(8,128)(2,1)S(1)} custom-call(bf16[512,512]{1,0:T(8,128)(2,1)S(1)} %get-tuple-element.23.refs_0_, bf16[128,256]{1,0:T(8,128)(2,1)S(1)} %get-tuple-element.27.refs_1_, bf16[128,256]{1,0:T(8,128)(2,1)S(1)} %collective-permute-done.refs_3_.refs_2_, bf16[80,256]{1,0:T(8,128)(2,1)S(1)} %collective-permute-done.1.refs_4_.refs_3_, ...), custom_call_target="tpu_custom_call" | custom-call | flops 121634816 | bytes 1024000 | tf_op jit(solution)/shard_map/upsample/pallas_call | solution.py:72
  20.8 0.6 %collective-permute-start.5 = (bf16[512,256]{1,0:T(8,128)(2,1)S(1)}, bf16[512,256]{1,0:T(8,128)(2,1)S(1)}, u32[]{:S(2)}, u32[]{:S(2)}) collective-permute-start(bf16[512,256]{1,0:T(8,128)(2,1)S(1)} %upsample.1.refs_0_), channel_id=1, source_target_pairs={{0,2},{1,3},{2,0},{3,1},{4,6},{5,7},{6,4},{7,5},{8,10},{9,11},{10,... | collective-permute-start | bytes 786440 | tf_op jit(solution)/shard_map/ppermute | solution.py:55
  21.5 2.7 %collective-permute-done.7.refs_2_ = bf16[80,512]{1,0:T(8,128)(2,1)S(1)} collective-permute-done((bf16[80,512]{1,0:T(8,128)(2,1)S(1)}, bf16[80,512]{1,0:T(8,128)(2,1)S(1)}, u32[]{:S(2)}, u32[]{:S(2)}) %collective-permute-start.7) | collective-permute-done | bytes 81952 | tf_op jit(solution)/shard_map/ppermute | solution.py:51
  24.2 0.0 collective-permute-done.8.refs_3_
  24.2 0.0 collective-permute-done.6.refs_1_
  24.2 0.1 collect.1
  24.2 0.6 %collective-permute-start.9 = (bf16[128,512]{1,0:T(8,128)(2,1)S(1)}, bf16[128,512]{1,0:T(8,128)(2,1)S(1)}, u32[]{:S(2)}, u32[]{:S(2)}) collective-permute-start(bf16[128,512]{1,0:T(8,128)(2,1)S(1)} %get-tuple-element.42), channel_id=1, source_target_pairs={{0,2},{1,3},{2,0},{3,1},{4,6},{5,7},{6,4},{7,5},{8,10},{9,11},{10,... | collective-permute-start | bytes 393224 | tf_op jit(solution)/shard_map/ppermute | solution.py:55
  24.8 3.4 %collective-permute-done.5.refs_1_ = bf16[512,256]{1,0:T(8,128)(2,1)S(1)} collective-permute-done((bf16[512,256]{1,0:T(8,128)(2,1)S(1)}, bf16[512,256]{1,0:T(8,128)(2,1)S(1)}, u32[]{:S(2)}, u32[]{:S(2)}) %collective-permute-start.5) | collective-permute-done | bytes 262176 | tf_op jit(solution)/shard_map/ppermute | solution.py:55
  28.3 0.7 %up_near.1.refs_4_.refs_2_.acc_ref = f32[512,1024]{1,0:T(8,128)S(1)} custom-call(bf16[512,256]{1,0:T(8,128)(2,1)S(1)} %upsample.1.refs_0_, bf16[512,256]{1,0:T(8,128)(2,1)S(1)} %collective-permute-done.5.refs_1_, bf16[1024,1024]{1,0:T(8,128)(2,1)S(1)} %copy-done), custom_call_target="tpu_custom_call" | custom-call | flops 536870912 | bytes 4718592 | tf_op jit(solution)/shard_map/up_near/pallas_call | solution.py:72
  29.0 0.7 %collective-permute-done.9.refs_2_.refs_1_ = bf16[128,512]{1,0:T(8,128)(2,1)S(1)} collective-permute-done((bf16[128,512]{1,0:T(8,128)(2,1)S(1)}, bf16[128,512]{1,0:T(8,128)(2,1)S(1)}, u32[]{:S(2)}, u32[]{:S(2)}) %collective-permute-start.9) | collective-permute-done | bytes 131104 | tf_op jit(solution)/shard_map/ppermute | solution.py:55
  29.7 0.0 collective-permute-done.10.refs_3_
  29.7 0.1 collective-permute-start.11
  29.8 0.4 %finish_part.2.refs_4_ = bf16[128,768]{1,0:T(8,128)(2,1)S(1)} custom-call(bf16[128,512]{1,0:T(8,128)(2,1)S(1)} %combine.1.refs_0_, bf16[3072,256]{1,0:T(8,128)(2,1)S(1)} %copy-done.1, bf16[768,256]{1,0:T(8,128)(2,1)S(1)} %collective-permute-done.4.refs_6_.refs_2_, bf16[768,256]{1,0:T(8,128)(2,1)S(1)} %collective-permute-done.10.refs_3_), custom_call_target="tpu_custom_call" | custom-call | flops 100663296 | bytes 2686976 | tf_op jit(solution)/shard_map/finish_part/pallas_call | solution.py:72
  30.2 0.6 %collective-permute-start.12 = (bf16[128,768]{1,0:T(8,128)(2,1)S(1)}, bf16[128,768]{1,0:T(8,128)(2,1)S(1)}, u32[]{:S(2)}, u32[]{:S(2)}) collective-permute-start(bf16[128,768]{1,0:T(8,128)(2,1)S(1)} %finish_part.2.refs_4_), channel_id=1, source_target_pairs={{0,1},{1,0},{2,3},{3,2},{4,5},{5,4},{6,7},{7,6},{8,9},{9,8},{10,11... | collective-permute-start | bytes 589832 | tf_op jit(solution)/shard_map/ppermute | solution.py:55
  30.8 0.4 %finish_part.3.kept_ref = f32[128,768]{1,0:T(8,128)S(1)} custom-call(bf16[128,512]{1,0:T(8,128)(2,1)S(1)} %combine.1.refs_0_, bf16[3072,256]{1,0:T(8,128)(2,1)S(1)} %copy-done.1, bf16[768,256]{1,0:T(8,128)(2,1)S(1)} %collective-permute-done.4.refs_6_.refs_2_, bf16[768,256]{1,0:T(8,128)(2,1)S(1)} %collective-permute-done.10.refs_3_, ...), custom_call_target="tpu_custom_call" | custom-call | flops 100663296 | bytes 2883584 | tf_op jit(solution)/shard_map/finish_part/pallas_call | solution.py:72
  31.2 0.8 %collective-permute-done.12.got_ref = bf16[128,768]{1,0:T(8,128)(2,1)S(1)} collective-permute-done((bf16[128,768]{1,0:T(8,128)(2,1)S(1)}, bf16[128,768]{1,0:T(8,128)(2,1)S(1)}, u32[]{:S(2)}, u32[]{:S(2)}) %collective-permute-start.12) | collective-permute-done | bytes 196640 | tf_op jit(solution)/shard_map/ppermute | solution.py:55
  32.0 0.0 collective-permute-done.11.other_ref
  32.0 1.5 %close.1 = (bf16[512,1024]{1,0:T(8,128)(2,1)}, bf16[128,768]{1,0:T(8,128)(2,1)}) custom-call(f32[512,1024]{1,0:T(8,128)S(1)} %up_near.1.refs_4_.refs_2_.acc_ref, bf16[512,512]{1,0:T(8,128)(2,1)S(1)} %collective-permute-done.11.other_ref, bf16[1024,1024]{1,0:T(8,128)(2,1)S(1)} %copy-done, f32[128,768]{1,0:T(8,128)S(1)} %finish_part.3.kept_ref, ...), custom_call_target="tpu_custom_call" | custom-call | flops 536870912 | bytes 1048576 | tf_op jit(solution)/shard_map/close/pallas_call | solution.py:410
  (2 shorter events, 0.1 us)
Async XLA Ops:
  0.6 5.7 %copy-start.2 = (bf16[128,3072]{1,0:T(8,128)(2,1)S(1)}, bf16[128,3072]{1,0:T(8,128)(2,1)}, u32[]{:S(2)}) copy-start(bf16[128,3072]{1,0:T(8,128)(2,1)} %refs_0_.1) | copy-start | bytes 2359300
  2.5 3.9 %copy-start.1 = (bf16[3072,256]{1,0:T(8,128)(2,1)S(1)}, bf16[3072,256]{1,0:T(8,128)(2,1)}, u32[]{:S(2)}) copy-start(bf16[3072,256]{1,0:T(8,128)(2,1)} %refs_1_.7) | copy-start | bytes 4718596
  2.5 8.6 %copy-start = (bf16[1024,1024]{1,0:T(8,128)(2,1)S(1)}, bf16[1024,1024]{1,0:T(8,128)(2,1)}, u32[]{:S(2)}) copy-start(bf16[1024,1024]{1,0:T(8,128)(2,1)} %w_ref.1) | copy-start | bytes 6291460
  3.3 8.6 %collective-permute-start.3 = (bf16[512,512]{1,0:T(8,128)(2,1)S(1)}, bf16[512,512]{1,0:T(8,128)(2,1)S(1)}, u32[]{:S(2)}, u32[]{:S(2)}) collective-permute-start(bf16[512,512]{1,0:T(8,128)(2,1)S(1)} %get-tuple-element.30), channel_id=1, source_target_pairs={{0,1},{1,0},{2,3},{3,2},{4,5},{5,4},{6,7},{7,6},{8,9},{9,8},{10,11... | collective-permute-start | bytes 1572872 | tf_op jit(solution)/shard_map/ppermute | solution.py:55
  3.8 14.9 %collective-permute-start.4 = (bf16[768,256]{1,0:T(8,128)(2,1)S(1)}, bf16[768,256]{1,0:T(8,128)(2,1)S(1)}, u32[]{:S(2)}, u32[]{:S(2)}) collective-permute-start(bf16[768,256]{1,0:T(8,128)(2,1)S(1)} %get-tuple-element.37), channel_id=1, source_target_pairs={{0,2},{1,3},{2,0},{3,1},{4,6},{5,7},{6,4},{7,5},{8,10},{9,11},{10,... | collective-permute-start | bytes 1179656 | tf_op jit(solution)/shard_map/ppermute | solution.py:55
  6.7 8.1 %collective-permute-start = (bf16[128,256]{1,0:T(8,128)(2,1)S(1)}, bf16[128,256]{1,0:T(8,128)(2,1)S(1)}, u32[]{:S(2)}, u32[]{:S(2)}) collective-permute-start(bf16[128,256]{1,0:T(8,128)(2,1)S(1)} %get-tuple-element.27.refs_1_), channel_id=1, source_target_pairs={{0,1},{1,0},{2,3},{3,2},{4,8},{5,9},{6,10},{7,11},{8,4},{9,5},{10,... | collective-permute-start | bytes 196616 | tf_op jit(solution)/shard_map/ppermute | solution.py:51
  7.0 7.9 %collective-permute-start.2 = (bf16[128,256]{1,0:T(8,128)(2,1)S(1)}, bf16[128,256]{1,0:T(8,128)(2,1)S(1)}, u32[]{:S(2)}, u32[]{:S(2)}) collective-permute-start(bf16[128,256]{1,0:T(8,128)(2,1)S(1)} %get-tuple-element.27.refs_1_), channel_id=1, source_target_pairs={{0,4},{1,5},{2,6},{3,7},{4,0},{5,1},{6,2},{7,3},{8,12},{9,13},{10,... | collective-permute-start | bytes 196616 | tf_op jit(solution)/shard_map/ppermute | solution.py:51
  10.0 4.9 %collective-permute-start.1 = (bf16[80,256]{1,0:T(8,128)(2,1)S(1)}, bf16[80,256]{1,0:T(8,128)(2,1)S(1)}, u32[]{:S(2)}, u32[]{:S(2)}) collective-permute-start(bf16[80,256]{1,0:T(8,128)(2,1)S(1)} %get-tuple-element.28), channel_id=1, source_target_pairs={{0,8},{1,9},{2,10},{3,11},{4,12},{5,13},{6,14},{7,15},{8,0},{9,1},... | collective-permute-start | bytes 122888 | tf_op jit(solution)/shard_map/ppermute | solution.py:51
  15.1 9.0 %collective-permute-start.8 = (bf16[128,512]{1,0:T(8,128)(2,1)S(1)}, bf16[128,512]{1,0:T(8,128)(2,1)S(1)}, u32[]{:S(2)}, u32[]{:S(2)}) collective-permute-start(bf16[128,512]{1,0:T(8,128)(2,1)S(1)} %get-tuple-element.41), channel_id=1, source_target_pairs={{0,4},{1,5},{2,6},{3,7},{4,0},{5,1},{6,2},{7,3},{8,12},{9,13},{10,... | collective-permute-start | bytes 393224 | tf_op jit(solution)/shard_map/ppermute | solution.py:51
  15.2 8.9 %collective-permute-start.6 = (bf16[128,512]{1,0:T(8,128)(2,1)S(1)}, bf16[128,512]{1,0:T(8,128)(2,1)S(1)}, u32[]{:S(2)}, u32[]{:S(2)}) collective-permute-start(bf16[128,512]{1,0:T(8,128)(2,1)S(1)} %get-tuple-element.39), channel_id=1, source_target_pairs={{0,1},{1,0},{2,3},{3,2},{4,8},{5,9},{6,10},{7,11},{8,4},{9,5},{10,... | collective-permute-start | bytes 393224 | tf_op jit(solution)/shard_map/ppermute | solution.py:51
  15.3 8.9 %collective-permute-start.7 = (bf16[80,512]{1,0:T(8,128)(2,1)S(1)}, bf16[80,512]{1,0:T(8,128)(2,1)S(1)}, u32[]{:S(2)}, u32[]{:S(2)}) collective-permute-start(bf16[80,512]{1,0:T(8,128)(2,1)S(1)} %get-tuple-element.40), channel_id=1, source_target_pairs={{0,8},{1,9},{2,10},{3,11},{4,12},{5,13},{6,14},{7,15},{8,0},{9,1},... | collective-permute-start | bytes 245768 | tf_op jit(solution)/shard_map/ppermute | solution.py:51
  18.7 11.0 %collective-permute-start.10 = (bf16[768,256]{1,0:T(8,128)(2,1)S(1)}, bf16[768,256]{1,0:T(8,128)(2,1)S(1)}, u32[]{:S(2)}, u32[]{:S(2)}) collective-permute-start(bf16[768,256]{1,0:T(8,128)(2,1)S(1)} %collective-permute-done.4.refs_6_.refs_2_), channel_id=1, source_target_pairs={{0,16},{16,0},{1,17},{17,1},{2,18},{18,2},{3,19},{19,3},{4,20},{20... | collective-permute-start | bytes 1179656 | tf_op jit(solution)/shard_map/ppermute | solution.py:310
  20.8 7.4 %collective-permute-start.5 = (bf16[512,256]{1,0:T(8,128)(2,1)S(1)}, bf16[512,256]{1,0:T(8,128)(2,1)S(1)}, u32[]{:S(2)}, u32[]{:S(2)}) collective-permute-start(bf16[512,256]{1,0:T(8,128)(2,1)S(1)} %upsample.1.refs_0_), channel_id=1, source_target_pairs={{0,2},{1,3},{2,0},{3,1},{4,6},{5,7},{6,4},{7,5},{8,10},{9,11},{10,... | collective-permute-start | bytes 786440 | tf_op jit(solution)/shard_map/ppermute | solution.py:55
  24.2 5.4 %collective-permute-start.9 = (bf16[128,512]{1,0:T(8,128)(2,1)S(1)}, bf16[128,512]{1,0:T(8,128)(2,1)S(1)}, u32[]{:S(2)}, u32[]{:S(2)}) collective-permute-start(bf16[128,512]{1,0:T(8,128)(2,1)S(1)} %get-tuple-element.42), channel_id=1, source_target_pairs={{0,2},{1,3},{2,0},{3,1},{4,6},{5,7},{6,4},{7,5},{8,10},{9,11},{10,... | collective-permute-start | bytes 393224 | tf_op jit(solution)/shard_map/ppermute | solution.py:55
  29.7 2.3 %collective-permute-start.11 = (bf16[512,512]{1,0:T(8,128)(2,1)S(1)}, bf16[512,512]{1,0:T(8,128)(2,1)S(1)}, u32[]{:S(2)}, u32[]{:S(2)}) collective-permute-start(bf16[512,512]{1,0:T(8,128)(2,1)S(1)} %pack.1), channel_id=1, source_target_pairs={{0,1},{1,0},{2,3},{3,2},{4,5},{5,4},{6,7},{7,6},{8,9},{9,8},{10,11... | collective-permute-start | bytes 1572872 | tf_op jit(solution)/shard_map/ppermute | solution.py:55
  30.2 1.7 %collective-permute-start.12 = (bf16[128,768]{1,0:T(8,128)(2,1)S(1)}, bf16[128,768]{1,0:T(8,128)(2,1)S(1)}, u32[]{:S(2)}, u32[]{:S(2)}) collective-permute-start(bf16[128,768]{1,0:T(8,128)(2,1)S(1)} %finish_part.2.refs_4_), channel_id=1, source_target_pairs={{0,1},{1,0},{2,3},{3,2},{4,5},{5,4},{6,7},{7,6},{8,9},{9,8},{10,11... | collective-permute-start | bytes 589832 | tf_op jit(solution)/shard_map/ppermute | solution.py:55

commit v5 on v4

--- a/solution.py
+++ b/solution.py
@@ -8,6 +8,7 @@
 from jax.sharding import PartitionSpec as P
 
 F32, BF16 = jnp.float32, jnp.bfloat16
+PAD = 16
 NOWHERE = -(1 << 20)
 
 
@@ -252,7 +253,8 @@
 
     def first_share(kept_ref, got_ref, turned_ref, grad_ref, out_ref):
         grad_ref[...] = (kept_ref[...] + got_ref[...].astype(F32)).astype(BF16)
-        out_ref[...] = part_of(turned_ref, 1, grad_ref[...]).astype(BF16)
+        out_ref[: rows[1], :] = part_of(turned_ref, 1, grad_ref[...]).astype(BF16)
+        out_ref[rows[1] :, :] = jnp.zeros((PAD, 2 * width), BF16)
 
     def next_share(k, grad_ref, turned_ref, out_ref):
         out_ref[...] = part_of(turned_ref, k, grad_ref[...]).astype(out_ref.dtype)
@@ -260,7 +262,7 @@
     products = [2 * bytes_here * 2 * width * r for r in rows]
     grad, share_sent, share_done = call(
         first_share,
-        [shape((bytes_here, 2 * width)), shape((rows[1], 2 * width))],
+        [shape((bytes_here, 2 * width)), shape((rows[1] + PAD, 2 * width))],
         grad_kept,
         grad_got,
         turned,
@@ -317,7 +319,7 @@
         sum_ref[...] = own_ref[...]
         for ref, (distance, parity) in zip(came_refs, pairs):
             if distance == 1:
-                sum_ref[...] += ref[...].astype(F32)
+                sum_ref[...] += ref[:span_rows, :].astype(F32)
             else:
                 sum_ref[pl.ds(cut_at(distance, parity), far), :] += ref[...].astype(F32)
         sent_ref[:, width:] = sum_ref[:, :width].astype(BF16)

time: 33.7 us -> 33 us (0.979)
  starting transfers between devices: 14.4 us -> 12.8 us
  waiting for transfers between devices: 10 us -> 10.9 us
    ppermute x6, waiting for transfers between devices: 4.9 us -> 6.88 us  [swap(): return lax.ppermute(value, 'tensor', [(i, i ^ mask) for i in range(4)])]
    ppermute x6, starting transfers between devices: 7.94 us -> 6.34 us  [trade(): return lax.ppermute(value, ('seq', 'tensor'), pairs)]
    ppermute x6, waiting for transfers between devices: 5.15 us -> 4.03 us  [trade(): return lax.ppermute(value, ('seq', 'tensor'), pairs)]
  transfers between devices with their start and end apart: 13 -> 13, of which waited for: 5 -> 5; matrix products, arithmetic and copies ran while one was open for 0% -> 0% of each run, Pallas kernels for 12% -> 13%
where the time goes in v5:
time: 33 us; the launch traced here: 32.8 us
  starting transfers between devices  12.8 us (39%)
  waiting for transfers between devices  10.9 us (33%)
  Pallas kernels  8.31 us (25%)
  between operations  0.79 us (2%)
    ppermute x6, waiting for transfers between devices, swap(): return lax.ppermute(value, 'tensor', [(i, i ^ mask) for i in range(4)])  6.88 us
    ppermute x6, starting transfers between devices, trade(): return lax.ppermute(value, ('seq', 'tensor'), pairs)  6.34 us
    pallas_call x14, Pallas kernels, call(): pl.pallas_call(run, out_shape=outs, name=getattr(kernel, 'func', kernel)....  4.92 us
    ppermute x6, starting transfers between devices, swap(): return lax.ppermute(value, 'tensor', [(i, i ^ mask) for i in range(4)])  4.92 us
    ppermute x6, waiting for transfers between devices, trade(): return lax.ppermute(value, ('seq', 'tensor'), pairs)  4.03 us
    pallas_call x1, Pallas kernels, body(): pl.pallas_call(open_up, out_shape=[shape((bytes_here, total_cols)), shape...  1.84 us
    pallas_call x1, Pallas kernels, body(): pl.pallas_call(close, out_shape=[shape((bytes_here, hidden)), shape((span...  1.55 us
    ppermute x1, starting transfers between devices, body(): w_y = lax.ppermute(w_x, 'group', [(0, 1), (1, 0)])  1.52 us
  transfers between devices with their start and end apart: 13, of which 5 were waited for; matrix products, arithmetic and copies ran while one was open for 0% of the time, Pallas kernels for 13%

profile of v5, /device:TPU:0, one launch (start us, length us, event | category | flops | bytes accessed | tf_op | source)
XLA Modules:
  0.0 32.8 jit_solution(15044502548228986827)
XLA Ops:
  0.6 0.0 copy-start.2
  0.6 1.8 %open_up.1 = (bf16[512,512]{1,0:T(8,128)(2,1)S(1)}, bf16[512,512]{1,0:T(8,128)(2,1)S(1)}, bf16[512,1024]{1,0:T(8,128)(2,1)S(1)}, bf16[2,256,1024]{2,1,0:T(8,128)(2,1)S(1)}, bf16[768,256]{1,0:T(8,128)(2,1)S(1)}) custom-call(s32[4]{0:T(128)} %off_hbm.1, bf16[512,128]{1,0:T(8,128)(2,1)} %weights_hbm.1, bf16[512,1024]{1,0:T(8,128)(2,1)} %d_hbm.1, ...), custom_call_target="tpu_custom_call" | custom-call | flops 536870912 | bytes 2097152 | tf_op jit(solution)/shard_map/open_up/pallas_call | solution.py:189
  2.5 0.0 copy-start.1
  2.5 0.0 copy-start
  2.5 0.7 %grad_for_other.1 = (bf16[512,512]{1,0:T(8,128)(2,1)S(1)}, f32[8,128]{1,0:T(8,128)S(1)}) custom-call(bf16[512,1024]{1,0:T(8,128)(2,1)S(1)} %get-tuple-element.24.refs_0_, bf16[2,256,1024]{2,1,0:T(8,128)(2,1)S(1)} %get-tuple-element.25.refs_1_), custom_call_target="tpu_custom_call" | custom-call | flops 536870912 | bytes 2621440 | tf_op jit(solution)/shard_map/grad_for_other/pallas_call | solution.py:73
  3.3 0.5 %collective-permute-start.3 = (bf16[512,512]{1,0:T(8,128)(2,1)S(1)}, bf16[512,512]{1,0:T(8,128)(2,1)S(1)}, u32[]{:S(2)}, u32[]{:S(2)}) collective-permute-start(bf16[512,512]{1,0:T(8,128)(2,1)S(1)} %get-tuple-element.30), channel_id=1, source_target_pairs={{0,1},{1,0},{2,3},{3,2},{4,5},{5,4},{6,7},{7,6},{8,9},{9,8},{10,11... | collective-permute-start | bytes 1572872 | tf_op jit(solution)/shard_map/ppermute | solution.py:56
  3.8 2.6 %collective-permute-start.4 = (bf16[768,256]{1,0:T(8,128)(2,1)S(1)}, bf16[768,256]{1,0:T(8,128)(2,1)S(1)}, u32[]{:S(2)}, u32[]{:S(2)}) collective-permute-start(bf16[768,256]{1,0:T(8,128)(2,1)S(1)} %get-tuple-element.37), channel_id=1, source_target_pairs={{0,2},{1,3},{2,0},{3,1},{4,6},{5,7},{6,4},{7,5},{8,10},{9,11},{10,... | collective-permute-start | bytes 1179656 | tf_op jit(solution)/shard_map/ppermute | solution.py:56
  6.3 0.0 copy-done.2
  6.3 0.0 copy-done.1
  6.4 0.4 %project.1 = (bf16[128,256]{1,0:T(8,128)(2,1)S(1)}, bf16[80,256]{1,0:T(8,128)(2,1)S(1)}, f32[8,128]{1,0:T(8,128)S(1)}) custom-call(bf16[128,3072]{1,0:T(8,128)(2,1)S(1)} %copy-done.2, bf16[3072,256]{1,0:T(8,128)(2,1)S(1)} %copy-done.1, f32[8,128]{1,0:T(8,128)S(1)} %get-tuple-element.26.refs_2_), custom_call_target="tpu_custom_call" | custom-call | flops 201326592 | bytes 2465792 | tf_op jit(solution)/shard_map/project/pallas_call | solution.py:73
  6.7 0.2 collective-permute-start
  7.0 3.0 %collective-permute-start.2 = (bf16[128,256]{1,0:T(8,128)(2,1)S(1)}, bf16[128,256]{1,0:T(8,128)(2,1)S(1)}, u32[]{:S(2)}, u32[]{:S(2)}) collective-permute-start(bf16[128,256]{1,0:T(8,128)(2,1)S(1)} %get-tuple-element.27.refs_1_), channel_id=1, source_target_pairs={{0,4},{1,5},{2,6},{3,7},{4,0},{5,1},{6,2},{7,3},{8,12},{9,13},{10,... | collective-permute-start | bytes 196616 | tf_op jit(solution)/shard_map/ppermute | solution.py:52
  10.0 1.2 %collective-permute-start.1 = (bf16[80,256]{1,0:T(8,128)(2,1)S(1)}, bf16[80,256]{1,0:T(8,128)(2,1)S(1)}, u32[]{:S(2)}, u32[]{:S(2)}) collective-permute-start(bf16[80,256]{1,0:T(8,128)(2,1)S(1)} %get-tuple-element.28), channel_id=1, source_target_pairs={{0,8},{1,9},{2,10},{3,11},{4,12},{5,13},{6,14},{7,15},{8,0},{9,1},... | collective-permute-start | bytes 122888 | tf_op jit(solution)/shard_map/ppermute | solution.py:52
  11.1 0.0 copy-done
  11.1 0.7 %grad_part.1.refs_0_ = f32[512,512]{1,0:T(8,128)S(1)} custom-call(bf16[512,1024]{1,0:T(8,128)(2,1)S(1)} %get-tuple-element.24.refs_0_, bf16[1024,1024]{1,0:T(8,128)(2,1)S(1)} %copy-done, f32[8,128]{1,0:T(8,128)S(1)} %get-tuple-element.29.refs_2_), custom_call_target="tpu_custom_call" | custom-call | flops 536870912 | bytes 4194304 | tf_op jit(solution)/shard_map/grad_part/pallas_call | solution.py:73
  11.9 0.0 collective-permute-done.3.refs_1_
  11.9 0.3 first_share.1
  12.2 0.1 collective-permute-start.6
  12.3 0.2 next_share.3
  12.5 2.8 %collective-permute-done.1.refs_4_.refs_3_ = bf16[80,256]{1,0:T(8,128)(2,1)S(1)} collective-permute-done((bf16[80,256]{1,0:T(8,128)(2,1)S(1)}, bf16[80,256]{1,0:T(8,128)(2,1)S(1)}, u32[]{:S(2)}, u32[]{:S(2)}) %collective-permute-start.1) | collective-permute-done | bytes 40992 | tf_op jit(solution)/shard_map/ppermute | solution.py:52
  15.3 0.0 collective-permute-done.refs_3_.refs_2_
  15.3 0.0 collective-permute-done.2.refs_5_.refs_4_
  15.3 0.2 next_share.4
  15.5 0.1 collective-permute-start.8
  15.6 1.8 %collective-permute-start.7 = (bf16[80,512]{1,0:T(8,128)(2,1)S(1)}, bf16[80,512]{1,0:T(8,128)(2,1)S(1)}, u32[]{:S(2)}, u32[]{:S(2)}) collective-permute-start(bf16[80,512]{1,0:T(8,128)(2,1)S(1)} %get-tuple-element.40), channel_id=1, source_target_pairs={{0,8},{1,9},{2,10},{3,11},{4,12},{5,13},{6,14},{7,15},{8,0},{9,1},... | collective-permute-start | bytes 245768 | tf_op jit(solution)/shard_map/ppermute | solution.py:52
  17.4 0.0 collective-permute-done.4.refs_6_.refs_2_
  17.4 1.5 %collective-permute-start.10 = (bf16[768,256]{1,0:T(8,128)(2,1)S(1)}, bf16[768,256]{1,0:T(8,128)(2,1)S(1)}, u32[]{:S(2)}, u32[]{:S(2)}) collective-permute-start(bf16[768,256]{1,0:T(8,128)(2,1)S(1)} %collective-permute-done.4.refs_6_.refs_2_), channel_id=1, source_target_pairs={{0,16},{16,0},{1,17},{17,1},{2,18},{18,2},{3,19},{19,3},{4,20},{20... | collective-permute-start | bytes 1179656 | tf_op jit(solution)/shard_map/ppermute | solution.py:312
  19.0 0.2 next_share.5
  19.2 0.4 %upsample.1.refs_0_ = bf16[512,256]{1,0:T(8,128)(2,1)S(1)} custom-call(bf16[512,512]{1,0:T(8,128)(2,1)S(1)} %get-tuple-element.23.refs_0_, bf16[128,256]{1,0:T(8,128)(2,1)S(1)} %get-tuple-element.27.refs_1_, bf16[128,256]{1,0:T(8,128)(2,1)S(1)} %collective-permute-done.refs_3_.refs_2_, bf16[80,256]{1,0:T(8,128)(2,1)S(1)} %collective-permute-done.1.refs_4_.refs_3_, ...), custom_call_target="tpu_custom_call" | custom-call | flops 121634816 | bytes 1024000 | tf_op jit(solution)/shard_map/upsample/pallas_call | solution.py:73
  19.6 0.6 %collective-permute-start.5 = (bf16[512,256]{1,0:T(8,128)(2,1)S(1)}, bf16[512,256]{1,0:T(8,128)(2,1)S(1)}, u32[]{:S(2)}, u32[]{:S(2)}) collective-permute-start(bf16[512,256]{1,0:T(8,128)(2,1)S(1)} %upsample.1.refs_0_), channel_id=1, source_target_pairs={{0,2},{1,3},{2,0},{3,1},{4,6},{5,7},{6,4},{7,5},{8,10},{9,11},{10,... | collective-permute-start | bytes 786440 | tf_op jit(solution)/shard_map/ppermute | solution.py:56
  20.2 1.2 %collective-permute-done.7.refs_2_ = bf16[80,512]{1,0:T(8,128)(2,1)S(1)} collective-permute-done((bf16[80,512]{1,0:T(8,128)(2,1)S(1)}, bf16[80,512]{1,0:T(8,128)(2,1)S(1)}, u32[]{:S(2)}, u32[]{:S(2)}) %collective-permute-start.7) | collective-permute-done | bytes 81952 | tf_op jit(solution)/shard_map/ppermute | solution.py:52
  21.4 0.0 collective-permute-done.8.refs_3_
  21.5 0.0 collective-permute-done.6.refs_1_
  21.5 0.1 collect.1
  21.5 0.6 %collective-permute-start.9 = (bf16[128,512]{1,0:T(8,128)(2,1)S(1)}, bf16[128,512]{1,0:T(8,128)(2,1)S(1)}, u32[]{:S(2)}, u32[]{:S(2)}) collective-permute-start(bf16[128,512]{1,0:T(8,128)(2,1)S(1)} %get-tuple-element.42), channel_id=1, source_target_pairs={{0,2},{1,3},{2,0},{3,1},{4,6},{5,7},{6,4},{7,5},{8,10},{9,11},{10,... | collective-permute-start | bytes 393224 | tf_op jit(solution)/shard_map/ppermute | solution.py:56
  22.1 5.4 %collective-permute-done.5.refs_1_ = bf16[512,256]{1,0:T(8,128)(2,1)S(1)} collective-permute-done((bf16[512,256]{1,0:T(8,128)(2,1)S(1)}, bf16[512,256]{1,0:T(8,128)(2,1)S(1)}, u32[]{:S(2)}, u32[]{:S(2)}) %collective-permute-start.5) | collective-permute-done | bytes 262176 | tf_op jit(solution)/shard_map/ppermute | solution.py:56
  27.6 0.7 %up_near.1.refs_4_.refs_2_.acc_ref = f32[512,1024]{1,0:T(8,128)S(1)} custom-call(bf16[512,256]{1,0:T(8,128)(2,1)S(1)} %upsample.1.refs_0_, bf16[512,256]{1,0:T(8,128)(2,1)S(1)} %collective-permute-done.5.refs_1_, bf16[1024,1024]{1,0:T(8,128)(2,1)S(1)} %copy-done), custom_call_target="tpu_custom_call" | custom-call | flops 536870912 | bytes 4718592 | tf_op jit(solution)/shard_map/up_near/pallas_call | solution.py:73
  28.3 0.0 collective-permute-done.10.refs_3_
  28.3 0.7 %collective-permute-done.9.refs_2_.refs_1_ = bf16[128,512]{1,0:T(8,128)(2,1)S(1)} collective-permute-done((bf16[128,512]{1,0:T(8,128)(2,1)S(1)}, bf16[128,512]{1,0:T(8,128)(2,1)S(1)}, u32[]{:S(2)}, u32[]{:S(2)}) %collective-permute-start.9) | collective-permute-done | bytes 131104 | tf_op jit(solution)/shard_map/ppermute | solution.py:56
  29.0 0.1 collective-permute-start.11
  29.1 0.4 %finish_part.2.refs_4_ = bf16[128,768]{1,0:T(8,128)(2,1)S(1)} custom-call(bf16[128,512]{1,0:T(8,128)(2,1)S(1)} %combine.1.refs_0_, bf16[3072,256]{1,0:T(8,128)(2,1)S(1)} %copy-done.1, bf16[768,256]{1,0:T(8,128)(2,1)S(1)} %collective-permute-done.4.refs_6_.refs_2_, bf16[768,256]{1,0:T(8,128)(2,1)S(1)} %collective-permute-done.10.refs_3_), custom_call_target="tpu_custom_call" | custom-call | flops 100663296 | bytes 2686976 | tf_op jit(solution)/shard_map/finish_part/pallas_call | solution.py:73
  29.5 0.6 %collective-permute-start.12 = (bf16[128,768]{1,0:T(8,128)(2,1)S(1)}, bf16[128,768]{1,0:T(8,128)(2,1)S(1)}, u32[]{:S(2)}, u32[]{:S(2)}) collective-permute-start(bf16[128,768]{1,0:T(8,128)(2,1)S(1)} %finish_part.2.refs_4_), channel_id=1, source_target_pairs={{0,1},{1,0},{2,3},{3,2},{4,5},{5,4},{6,7},{7,6},{8,9},{9,8},{10,11... | collective-permute-start | bytes 589832 | tf_op jit(solution)/shard_map/ppermute | solution.py:56
  30.1 0.4 %finish_part.3.kept_ref = f32[128,768]{1,0:T(8,128)S(1)} custom-call(bf16[128,512]{1,0:T(8,128)(2,1)S(1)} %combine.1.refs_0_, bf16[3072,256]{1,0:T(8,128)(2,1)S(1)} %copy-done.1, bf16[768,256]{1,0:T(8,128)(2,1)S(1)} %collective-permute-done.4.refs_6_.refs_2_, bf16[768,256]{1,0:T(8,128)(2,1)S(1)} %collective-permute-done.10.refs_3_, ...), custom_call_target="tpu_custom_call" | custom-call | flops 100663296 | bytes 2883584 | tf_op jit(solution)/shard_map/finish_part/pallas_call | solution.py:73
  30.5 0.8 %collective-permute-done.12.got_ref = bf16[128,768]{1,0:T(8,128)(2,1)S(1)} collective-permute-done((bf16[128,768]{1,0:T(8,128)(2,1)S(1)}, bf16[128,768]{1,0:T(8,128)(2,1)S(1)}, u32[]{:S(2)}, u32[]{:S(2)}) %collective-permute-start.12) | collective-permute-done | bytes 196640 | tf_op jit(solution)/shard_map/ppermute | solution.py:56
  31.3 0.0 collective-permute-done.11.other_ref
  31.3 1.5 %close.1 = (bf16[512,1024]{1,0:T(8,128)(2,1)}, bf16[128,768]{1,0:T(8,128)(2,1)}) custom-call(f32[512,1024]{1,0:T(8,128)S(1)} %up_near.1.refs_4_.refs_2_.acc_ref, bf16[512,512]{1,0:T(8,128)(2,1)S(1)} %collective-permute-done.11.other_ref, bf16[1024,1024]{1,0:T(8,128)(2,1)S(1)} %copy-done, f32[128,768]{1,0:T(8,128)S(1)} %finish_part.3.kept_ref, ...), custom_call_target="tpu_custom_call" | custom-call | flops 536870912 | bytes 1048576 | tf_op jit(solution)/shard_map/close/pallas_call | solution.py:412
  (2 shorter events, 0.1 us)
Async XLA Ops:
  0.6 5.7 %copy-start.2 = (bf16[128,3072]{1,0:T(8,128)(2,1)S(1)}, bf16[128,3072]{1,0:T(8,128)(2,1)}, u32[]{:S(2)}) copy-start(bf16[128,3072]{1,0:T(8,128)(2,1)} %refs_0_.1) | copy-start | bytes 2359300
  2.5 3.9 %copy-start.1 = (bf16[3072,256]{1,0:T(8,128)(2,1)S(1)}, bf16[3072,256]{1,0:T(8,128)(2,1)}, u32[]{:S(2)}) copy-start(bf16[3072,256]{1,0:T(8,128)(2,1)} %refs_1_.7) | copy-start | bytes 4718596
  2.5 8.6 %copy-start = (bf16[1024,1024]{1,0:T(8,128)(2,1)S(1)}, bf16[1024,1024]{1,0:T(8,128)(2,1)}, u32[]{:S(2)}) copy-start(bf16[1024,1024]{1,0:T(8,128)(2,1)} %w_ref.1) | copy-start | bytes 6291460
  3.3 8.6 %collective-permute-start.3 = (bf16[512,512]{1,0:T(8,128)(2,1)S(1)}, bf16[512,512]{1,0:T(8,128)(2,1)S(1)}, u32[]{:S(2)}, u32[]{:S(2)}) collective-permute-start(bf16[512,512]{1,0:T(8,128)(2,1)S(1)} %get-tuple-element.30), channel_id=1, source_target_pairs={{0,1},{1,0},{2,3},{3,2},{4,5},{5,4},{6,7},{7,6},{8,9},{9,8},{10,11... | collective-permute-start | bytes 1572872 | tf_op jit(solution)/shard_map/ppermute | solution.py:56
  3.8 13.7 %collective-permute-start.4 = (bf16[768,256]{1,0:T(8,128)(2,1)S(1)}, bf16[768,256]{1,0:T(8,128)(2,1)S(1)}, u32[]{:S(2)}, u32[]{:S(2)}) collective-permute-start(bf16[768,256]{1,0:T(8,128)(2,1)S(1)} %get-tuple-element.37), channel_id=1, source_target_pairs={{0,2},{1,3},{2,0},{3,1},{4,6},{5,7},{6,4},{7,5},{8,10},{9,11},{10,... | collective-permute-start | bytes 1179656 | tf_op jit(solution)/shard_map/ppermute | solution.py:56
  6.7 8.6 %collective-permute-start = (bf16[128,256]{1,0:T(8,128)(2,1)S(1)}, bf16[128,256]{1,0:T(8,128)(2,1)S(1)}, u32[]{:S(2)}, u32[]{:S(2)}) collective-permute-start(bf16[128,256]{1,0:T(8,128)(2,1)S(1)} %get-tuple-element.27.refs_1_), channel_id=1, source_target_pairs={{0,1},{1,0},{2,3},{3,2},{4,8},{5,9},{6,10},{7,11},{8,4},{9,5},{10,... | collective-permute-start | bytes 196616 | tf_op jit(solution)/shard_map/ppermute | solution.py:52
  7.0 8.3 %collective-permute-start.2 = (bf16[128,256]{1,0:T(8,128)(2,1)S(1)}, bf16[128,256]{1,0:T(8,128)(2,1)S(1)}, u32[]{:S(2)}, u32[]{:S(2)}) collective-permute-start(bf16[128,256]{1,0:T(8,128)(2,1)S(1)} %get-tuple-element.27.refs_1_), channel_id=1, source_target_pairs={{0,4},{1,5},{2,6},{3,7},{4,0},{5,1},{6,2},{7,3},{8,12},{9,13},{10,... | collective-permute-start | bytes 196616 | tf_op jit(solution)/shard_map/ppermute | solution.py:52
  10.0 5.3 %collective-permute-start.1 = (bf16[80,256]{1,0:T(8,128)(2,1)S(1)}, bf16[80,256]{1,0:T(8,128)(2,1)S(1)}, u32[]{:S(2)}, u32[]{:S(2)}) collective-permute-start(bf16[80,256]{1,0:T(8,128)(2,1)S(1)} %get-tuple-element.28), channel_id=1, source_target_pairs={{0,8},{1,9},{2,10},{3,11},{4,12},{5,13},{6,14},{7,15},{8,0},{9,1},... | collective-permute-start | bytes 122888 | tf_op jit(solution)/shard_map/ppermute | solution.py:52
  12.2 9.2 %collective-permute-start.6 = (bf16[144,512]{1,0:T(8,128)(2,1)S(1)}, bf16[144,512]{1,0:T(8,128)(2,1)S(1)}, u32[]{:S(2)}, u32[]{:S(2)}) collective-permute-start(bf16[144,512]{1,0:T(8,128)(2,1)S(1)} %get-tuple-element.39), channel_id=1, source_target_pairs={{0,1},{1,0},{2,3},{3,2},{4,8},{5,9},{6,10},{7,11},{8,4},{9,5},{10,... | collective-permute-start | bytes 442376 | tf_op jit(solution)/shard_map/ppermute | solution.py:52
  15.5 5.9 %collective-permute-start.8 = (bf16[128,512]{1,0:T(8,128)(2,1)S(1)}, bf16[128,512]{1,0:T(8,128)(2,1)S(1)}, u32[]{:S(2)}, u32[]{:S(2)}) collective-permute-start(bf16[128,512]{1,0:T(8,128)(2,1)S(1)} %get-tuple-element.41), channel_id=1, source_target_pairs={{0,4},{1,5},{2,6},{3,7},{4,0},{5,1},{6,2},{7,3},{8,12},{9,13},{10,... | collective-permute-start | bytes 393224 | tf_op jit(solution)/shard_map/ppermute | solution.py:52
  15.6 5.8 %collective-permute-start.7 = (bf16[80,512]{1,0:T(8,128)(2,1)S(1)}, bf16[80,512]{1,0:T(8,128)(2,1)S(1)}, u32[]{:S(2)}, u32[]{:S(2)}) collective-permute-start(bf16[80,512]{1,0:T(8,128)(2,1)S(1)} %get-tuple-element.40), channel_id=1, source_target_pairs={{0,8},{1,9},{2,10},{3,11},{4,12},{5,13},{6,14},{7,15},{8,0},{9,1},... | collective-permute-start | bytes 245768 | tf_op jit(solution)/shard_map/ppermute | solution.py:52
  17.4 10.8 %collective-permute-start.10 = (bf16[768,256]{1,0:T(8,128)(2,1)S(1)}, bf16[768,256]{1,0:T(8,128)(2,1)S(1)}, u32[]{:S(2)}, u32[]{:S(2)}) collective-permute-start(bf16[768,256]{1,0:T(8,128)(2,1)S(1)} %collective-permute-done.4.refs_6_.refs_2_), channel_id=1, source_target_pairs={{0,16},{16,0},{1,17},{17,1},{2,18},{18,2},{3,19},{19,3},{4,20},{20... | collective-permute-start | bytes 1179656 | tf_op jit(solution)/shard_map/ppermute | solution.py:312
  19.6 7.9 %collective-permute-start.5 = (bf16[512,256]{1,0:T(8,128)(2,1)S(1)}, bf16[512,256]{1,0:T(8,128)(2,1)S(1)}, u32[]{:S(2)}, u32[]{:S(2)}) collective-permute-start(bf16[512,256]{1,0:T(8,128)(2,1)S(1)} %upsample.1.refs_0_), channel_id=1, source_target_pairs={{0,2},{1,3},{2,0},{3,1},{4,6},{5,7},{6,4},{7,5},{8,10},{9,11},{10,... | collective-permute-start | bytes 786440 | tf_op jit(solution)/shard_map/ppermute | solution.py:56
  21.5 7.4 %collective-permute-start.9 = (bf16[128,512]{1,0:T(8,128)(2,1)S(1)}, bf16[128,512]{1,0:T(8,128)(2,1)S(1)}, u32[]{:S(2)}, u32[]{:S(2)}) collective-permute-start(bf16[128,512]{1,0:T(8,128)(2,1)S(1)} %get-tuple-element.42), channel_id=1, source_target_pairs={{0,2},{1,3},{2,0},{3,1},{4,6},{5,7},{6,4},{7,5},{8,10},{9,11},{10,... | collective-permute-start | bytes 393224 | tf_op jit(solution)/shard_map/ppermute | solution.py:56
  29.0 2.3 %collective-permute-start.11 = (bf16[512,512]{1,0:T(8,128)(2,1)S(1)}, bf16[512,512]{1,0:T(8,128)(2,1)S(1)}, u32[]{:S(2)}, u32[]{:S(2)}) collective-permute-start(bf16[512,512]{1,0:T(8,128)(2,1)S(1)} %pack.1), channel_id=1, source_target_pairs={{0,1},{1,0},{2,3},{3,2},{4,5},{5,4},{6,7},{7,6},{8,9},{9,8},{10,11... | collective-permute-start | bytes 1572872 | tf_op jit(solution)/shard_map/ppermute | solution.py:56
  29.5 1.7 %collective-permute-start.12 = (bf16[128,768]{1,0:T(8,128)(2,1)S(1)}, bf16[128,768]{1,0:T(8,128)(2,1)S(1)}, u32[]{:S(2)}, u32[]{:S(2)}) collective-permute-start(bf16[128,768]{1,0:T(8,128)(2,1)S(1)} %finish_part.2.refs_4_), channel_id=1, source_target_pairs={{0,1},{1,0},{2,3},{3,2},{4,5},{5,4},{6,7},{7,6},{8,9},{9,8},{10,11... | collective-permute-start | bytes 589832 | tf_op jit(solution)/shard_map/ppermute | solution.py:56

commit v6 on v5

--- a/solution.py
+++ b/solution.py
@@ -269,7 +269,26 @@
         flops=products[1],
         token=True,
     )
+    first_done = share_done
     came = [trade(share_sent, pairs[0], count)]
+
+    def upsample(band_ref, *refs):
+        *piece_refs, out_ref = refs
+        acc = 0.0
+        for k, ref in enumerate(piece_refs):
+            acc += dot(band_ref[:, cols[k] : cols[k] + rows[k]], ref[...])
+        out_ref[...] = acc.astype(BF16)
+
+    (upsampled,) = call(
+        upsample,
+        [shape((bytes_here, width))],
+        band,
+        *pieces,
+        flops=2 * bytes_here * width * sum(rows),
+        after=(first_done,),
+    )
+    up_x = swap(upsampled, 2)
+
     for k in range(2, len(rows)):
         share_sent, share_done = call(
             functools.partial(next_share, k),
@@ -277,7 +296,7 @@
             grad,
             turned,
             flops=products[k],
-            after=(share_done, *pieces[1:]) if k == len(rows) - 1 else (share_done,),
+            after=(share_done, upsampled) if k == len(rows) - 1 else (share_done,),
             token=True,
         )
         came.append(trade(share_sent, pairs[k - 1], count))
@@ -287,26 +306,10 @@
         grad,
         turned,
         flops=products[0],
-        after=(share_done,),
+        after=(share_done, w_x),
         token=True,
     )
 
-    def upsample(band_ref, *refs):
-        *piece_refs, out_ref = refs
-        acc = 0.0
-        for k, ref in enumerate(piece_refs):
-            acc += dot(band_ref[:, cols[k] : cols[k] + rows[k]], ref[...])
-        out_ref[...] = acc.astype(BF16)
-
-    (upsampled,) = call(
-        upsample,
-        [shape((bytes_here, width))],
-        band,
-        *pieces,
-        flops=2 * bytes_here * width * sum(rows),
-        after=(own_done, w_x),
-    )
-    up_x = swap(upsampled, 2)
 
     if groups == 2:
         w_y = lax.ppermute(w_x, "group", [(0, 1), (1, 0)])

time: 33 us -> 32.2 us (0.976)
  waiting for transfers between devices: 10.9 us -> 9.8 us
  Pallas kernels: 8.31 us -> 8.77 us
    ppermute x6, waiting for transfers between devices: 6.88 us -> 5.72 us  [swap(): return lax.ppermute(value, 'tensor', [(i, i ^ mask) for i in range(4)])]
    pallas_call x14, Pallas kernels: 4.92 us -> 5.38 us  [call(): pl.pallas_call(run, out_shape=outs, name=getattr(kernel, 'func', kernel)....]
  transfers between devices with their start and end apart: 13 -> 13, of which waited for: 5 -> 5; matrix products, arithmetic and copies ran while one was open for 0% -> 0% of each run, Pallas kernels for 13% -> 14%
where the time goes in v6:
time: 32.2 us; the launch traced here: 32.1 us
  starting transfers between devices  12.7 us (39%)
  waiting for transfers between devices  9.8 us (30%)
  Pallas kernels  8.77 us (27%)
  between operations  0.79 us (2%)
    ppermute x6, starting transfers between devices, trade(): return lax.ppermute(value, ('seq', 'tensor'), pairs)  6.34 us
    ppermute x6, waiting for transfers between devices, swap(): return lax.ppermute(value, 'tensor', [(i, i ^ mask) for i in range(4)])  5.72 us
    pallas_call x14, Pallas kernels, call(): pl.pallas_call(run, out_shape=outs, name=getattr(kernel, 'func', kernel)....  5.38 us
    ppermute x6, starting transfers between devices, swap(): return lax.ppermute(value, 'tensor', [(i, i ^ mask) for i in range(4)])  4.85 us
    ppermute x6, waiting for transfers between devices, trade(): return lax.ppermute(value, ('seq', 'tensor'), pairs)  4.07 us
    pallas_call x1, Pallas kernels, body(): pl.pallas_call(open_up, out_shape=[shape((bytes_here, total_cols)), shape...  1.84 us
    pallas_call x1, Pallas kernels, body(): pl.pallas_call(close, out_shape=[shape((bytes_here, hidden)), shape((span...  1.55 us
    ppermute x1, starting transfers between devices, body(): w_y = lax.ppermute(w_x, 'group', [(0, 1), (1, 0)])  1.53 us
  transfers between devices with their start and end apart: 13, of which 5 were waited for; matrix products, arithmetic and copies ran while one was open for 0% of the time, Pallas kernels for 14%

profile of v6, /device:TPU:0, one launch (start us, length us, event | category | flops | bytes accessed | tf_op | source)
XLA Modules:
  0.0 32.1 jit_solution(17155715771209600573)
XLA Ops:
  0.6 0.0 copy-start.2
  0.6 1.8 %open_up.1 = (bf16[512,512]{1,0:T(8,128)(2,1)S(1)}, bf16[512,512]{1,0:T(8,128)(2,1)S(1)}, bf16[512,1024]{1,0:T(8,128)(2,1)S(1)}, bf16[2,256,1024]{2,1,0:T(8,128)(2,1)S(1)}, bf16[768,256]{1,0:T(8,128)(2,1)S(1)}) custom-call(s32[4]{0:T(128)} %off_hbm.1, bf16[512,128]{1,0:T(8,128)(2,1)} %weights_hbm.1, bf16[512,1024]{1,0:T(8,128)(2,1)} %d_hbm.1, ...), custom_call_target="tpu_custom_call" | custom-call | flops 536870912 | bytes 2097152 | tf_op jit(solution)/shard_map/open_up/pallas_call | solution.py:189
  2.5 0.0 copy-start.1
  2.5 0.0 copy-start
  2.5 0.7 %grad_for_other.1 = (bf16[512,512]{1,0:T(8,128)(2,1)S(1)}, f32[8,128]{1,0:T(8,128)S(1)}) custom-call(bf16[512,1024]{1,0:T(8,128)(2,1)S(1)} %get-tuple-element.23.refs_0_, bf16[2,256,1024]{2,1,0:T(8,128)(2,1)S(1)} %get-tuple-element.24.refs_1_), custom_call_target="tpu_custom_call" | custom-call | flops 536870912 | bytes 2621440 | tf_op jit(solution)/shard_map/grad_for_other/pallas_call | solution.py:73
  3.3 0.5 %collective-permute-start.3 = (bf16[512,512]{1,0:T(8,128)(2,1)S(1)}, bf16[512,512]{1,0:T(8,128)(2,1)S(1)}, u32[]{:S(2)}, u32[]{:S(2)}) collective-permute-start(bf16[512,512]{1,0:T(8,128)(2,1)S(1)} %get-tuple-element.29), channel_id=1, source_target_pairs={{0,1},{1,0},{2,3},{3,2},{4,5},{5,4},{6,7},{7,6},{8,9},{9,8},{10,11... | collective-permute-start | bytes 1572872 | tf_op jit(solution)/shard_map/ppermute | solution.py:56
  3.8 2.6 %collective-permute-start.5 = (bf16[768,256]{1,0:T(8,128)(2,1)S(1)}, bf16[768,256]{1,0:T(8,128)(2,1)S(1)}, u32[]{:S(2)}, u32[]{:S(2)}) collective-permute-start(bf16[768,256]{1,0:T(8,128)(2,1)S(1)} %get-tuple-element.35), channel_id=1, source_target_pairs={{0,2},{1,3},{2,0},{3,1},{4,6},{5,7},{6,4},{7,5},{8,10},{9,11},{10,... | collective-permute-start | bytes 1179656 | tf_op jit(solution)/shard_map/ppermute | solution.py:56
  6.3 0.0 copy-done.2
  6.3 0.0 copy-done.1
  6.4 0.4 %project.1 = (bf16[128,256]{1,0:T(8,128)(2,1)S(1)}, bf16[80,256]{1,0:T(8,128)(2,1)S(1)}, f32[8,128]{1,0:T(8,128)S(1)}) custom-call(bf16[128,3072]{1,0:T(8,128)(2,1)S(1)} %copy-done.2, bf16[3072,256]{1,0:T(8,128)(2,1)S(1)} %copy-done.1, f32[8,128]{1,0:T(8,128)S(1)} %get-tuple-element.25.refs_2_), custom_call_target="tpu_custom_call" | custom-call | flops 201326592 | bytes 2465792 | tf_op jit(solution)/shard_map/project/pallas_call | solution.py:73
  6.7 0.2 collective-permute-start
  7.0 3.0 %collective-permute-start.2 = (bf16[128,256]{1,0:T(8,128)(2,1)S(1)}, bf16[128,256]{1,0:T(8,128)(2,1)S(1)}, u32[]{:S(2)}, u32[]{:S(2)}) collective-permute-start(bf16[128,256]{1,0:T(8,128)(2,1)S(1)} %get-tuple-element.26.refs_1_), channel_id=1, source_target_pairs={{0,4},{1,5},{2,6},{3,7},{4,0},{5,1},{6,2},{7,3},{8,12},{9,13},{10,... | collective-permute-start | bytes 196616 | tf_op jit(solution)/shard_map/ppermute | solution.py:52
  10.0 1.2 %collective-permute-start.1 = (bf16[80,256]{1,0:T(8,128)(2,1)S(1)}, bf16[80,256]{1,0:T(8,128)(2,1)S(1)}, u32[]{:S(2)}, u32[]{:S(2)}) collective-permute-start(bf16[80,256]{1,0:T(8,128)(2,1)S(1)} %get-tuple-element.27), channel_id=1, source_target_pairs={{0,8},{1,9},{2,10},{3,11},{4,12},{5,13},{6,14},{7,15},{8,0},{9,1},... | collective-permute-start | bytes 122888 | tf_op jit(solution)/shard_map/ppermute | solution.py:52
  11.1 0.0 copy-done
  11.1 0.7 %grad_part.1.refs_0_ = f32[512,512]{1,0:T(8,128)S(1)} custom-call(bf16[512,1024]{1,0:T(8,128)(2,1)S(1)} %get-tuple-element.23.refs_0_, bf16[1024,1024]{1,0:T(8,128)(2,1)S(1)} %copy-done, f32[8,128]{1,0:T(8,128)S(1)} %get-tuple-element.28.refs_2_), custom_call_target="tpu_custom_call" | custom-call | flops 536870912 | bytes 4194304 | tf_op jit(solution)/shard_map/grad_part/pallas_call | solution.py:73
  11.9 0.0 collective-permute-done.3.refs_1_
  11.9 0.3 first_share.1
  12.2 0.1 collective-permute-start.6
  12.3 0.2 next_share.3
  12.5 2.8 %collective-permute-done.1.refs_3_ = bf16[80,256]{1,0:T(8,128)(2,1)S(1)} collective-permute-done((bf16[80,256]{1,0:T(8,128)(2,1)S(1)}, bf16[80,256]{1,0:T(8,128)(2,1)S(1)}, u32[]{:S(2)}, u32[]{:S(2)}) %collective-permute-start.1) | collective-permute-done | bytes 40992 | tf_op jit(solution)/shard_map/ppermute | solution.py:52
  15.3 0.0 collective-permute-done.refs_2_
  15.3 0.0 collective-permute-done.2.refs_4_
  15.3 0.4 %upsample.1.refs_0_.refs_3_ = bf16[512,256]{1,0:T(8,128)(2,1)S(1)} custom-call(bf16[512,512]{1,0:T(8,128)(2,1)S(1)} %get-tuple-element.22.refs_0_, bf16[128,256]{1,0:T(8,128)(2,1)S(1)} %get-tuple-element.26.refs_1_, bf16[128,256]{1,0:T(8,128)(2,1)S(1)} %collective-permute-done.refs_2_, bf16[80,256]{1,0:T(8,128)(2,1)S(1)} %collective-permute-done.1.refs_3_, ...), custom_call_target="tpu_custom_call" | custom-call | flops 121634816 | bytes 1024000 | tf_op jit(solution)/shard_map/upsample/pallas_call | solution.py:73
  15.7 0.2 next_share.4
  16.0 0.1 collective-permute-start.8
  16.1 1.8 %collective-permute-start.7 = (bf16[80,512]{1,0:T(8,128)(2,1)S(1)}, bf16[80,512]{1,0:T(8,128)(2,1)S(1)}, u32[]{:S(2)}, u32[]{:S(2)}) collective-permute-start(bf16[80,512]{1,0:T(8,128)(2,1)S(1)} %get-tuple-element.38), channel_id=1, source_target_pairs={{0,8},{1,9},{2,10},{3,11},{4,12},{5,13},{6,14},{7,15},{8,0},{9,1},... | collective-permute-start | bytes 245768 | tf_op jit(solution)/shard_map/ppermute | solution.py:52
  17.9 0.0 collective-permute-done.5.refs_3_.refs_2_
  17.9 1.5 %collective-permute-start.10 = (bf16[768,256]{1,0:T(8,128)(2,1)S(1)}, bf16[768,256]{1,0:T(8,128)(2,1)S(1)}, u32[]{:S(2)}, u32[]{:S(2)}) collective-permute-start(bf16[768,256]{1,0:T(8,128)(2,1)S(1)} %collective-permute-done.5.refs_3_.refs_2_), channel_id=1, source_target_pairs={{0,16},{16,0},{1,17},{17,1},{2,18},{18,2},{3,19},{19,3},{4,20},{20... | collective-permute-start | bytes 1179656 | tf_op jit(solution)/shard_map/ppermute | solution.py:315
  19.4 0.5 %collective-permute-start.4 = (bf16[512,256]{1,0:T(8,128)(2,1)S(1)}, bf16[512,256]{1,0:T(8,128)(2,1)S(1)}, u32[]{:S(2)}, u32[]{:S(2)}) collective-permute-start(bf16[512,256]{1,0:T(8,128)(2,1)S(1)} %upsample.1.refs_0_.refs_3_), channel_id=1, source_target_pairs={{0,2},{1,3},{2,0},{3,1},{4,6},{5,7},{6,4},{7,5},{8,10},{9,11},{10,... | collective-permute-start | bytes 786440 | tf_op jit(solution)/shard_map/ppermute | solution.py:56
  19.9 0.7 %next_share.5 = (f32[128,512]{1,0:T(8,128)S(1)}, f32[8,128]{1,0:T(8,128)}) custom-call(bf16[512,512]{1,0:T(8,128)(2,1)S(1)} %get-tuple-element.32.refs_0_, bf16[512,512]{1,0:T(8,128)(2,1)S(1)} %get-tuple-element.30.refs_2_.refs_1_, f32[8,128]{1,0:T(8,128)S(1)} %get-tuple-element.34.refs_2_, bf16[768,256]{1,0:T(8,128)(2,1)S(1)} %collective-permute-done.5.refs_3_.refs_2_), custom_call_target="tpu_custom_call" | custom-call | flops 67108864 | bytes 1310720 | tf_op jit(solution)/shard_map/next_share/pallas_call | solution.py:73
  20.6 1.3 %collective-permute-done.7.refs_2_ = bf16[80,512]{1,0:T(8,128)(2,1)S(1)} collective-permute-done((bf16[80,512]{1,0:T(8,128)(2,1)S(1)}, bf16[80,512]{1,0:T(8,128)(2,1)S(1)}, u32[]{:S(2)}, u32[]{:S(2)}) %collective-permute-start.7) | collective-permute-done | bytes 81952 | tf_op jit(solution)/shard_map/ppermute | solution.py:52
  21.9 0.0 collective-permute-done.8.refs_3_
  21.9 0.0 collective-permute-done.6.refs_1_
  21.9 0.1 collect.1
  22.0 0.6 %collective-permute-start.9 = (bf16[128,512]{1,0:T(8,128)(2,1)S(1)}, bf16[128,512]{1,0:T(8,128)(2,1)S(1)}, u32[]{:S(2)}, u32[]{:S(2)}) collective-permute-start(bf16[128,512]{1,0:T(8,128)(2,1)S(1)} %get-tuple-element.40), channel_id=1, source_target_pairs={{0,2},{1,3},{2,0},{3,1},{4,6},{5,7},{6,4},{7,5},{8,10},{9,11},{10,... | collective-permute-start | bytes 393224 | tf_op jit(solution)/shard_map/ppermute | solution.py:56
  22.6 4.3 %collective-permute-done.4.refs_1_ = bf16[512,256]{1,0:T(8,128)(2,1)S(1)} collective-permute-done((bf16[512,256]{1,0:T(8,128)(2,1)S(1)}, bf16[512,256]{1,0:T(8,128)(2,1)S(1)}, u32[]{:S(2)}, u32[]{:S(2)}) %collective-permute-start.4) | collective-permute-done | bytes 262176 | tf_op jit(solution)/shard_map/ppermute | solution.py:56
  26.8 0.7 %up_near.1.refs_4_.refs_2_.acc_ref = f32[512,1024]{1,0:T(8,128)S(1)} custom-call(bf16[512,256]{1,0:T(8,128)(2,1)S(1)} %upsample.1.refs_0_.refs_3_, bf16[512,256]{1,0:T(8,128)(2,1)S(1)} %collective-permute-done.4.refs_1_, bf16[1024,1024]{1,0:T(8,128)(2,1)S(1)} %copy-done), custom_call_target="tpu_custom_call" | custom-call | flops 536870912 | bytes 4718592 | tf_op jit(solution)/shard_map/up_near/pallas_call | solution.py:73
  27.5 0.0 collective-permute-done.10.refs_3_
  27.6 0.7 %collective-permute-done.9.refs_2_.refs_1_ = bf16[128,512]{1,0:T(8,128)(2,1)S(1)} collective-permute-done((bf16[128,512]{1,0:T(8,128)(2,1)S(1)}, bf16[128,512]{1,0:T(8,128)(2,1)S(1)}, u32[]{:S(2)}, u32[]{:S(2)}) %collective-permute-start.9) | collective-permute-done | bytes 131104 | tf_op jit(solution)/shard_map/ppermute | solution.py:56
  28.3 0.1 collective-permute-start.11
  28.4 0.4 %finish_part.2.refs_4_ = bf16[128,768]{1,0:T(8,128)(2,1)S(1)} custom-call(bf16[128,512]{1,0:T(8,128)(2,1)S(1)} %combine.1.refs_0_, bf16[3072,256]{1,0:T(8,128)(2,1)S(1)} %copy-done.1, bf16[768,256]{1,0:T(8,128)(2,1)S(1)} %collective-permute-done.5.refs_3_.refs_2_, bf16[768,256]{1,0:T(8,128)(2,1)S(1)} %collective-permute-done.10.refs_3_), custom_call_target="tpu_custom_call" | custom-call | flops 100663296 | bytes 2686976 | tf_op jit(solution)/shard_map/finish_part/pallas_call | solution.py:73
  28.8 0.6 %collective-permute-start.12 = (bf16[128,768]{1,0:T(8,128)(2,1)S(1)}, bf16[128,768]{1,0:T(8,128)(2,1)S(1)}, u32[]{:S(2)}, u32[]{:S(2)}) collective-permute-start(bf16[128,768]{1,0:T(8,128)(2,1)S(1)} %finish_part.2.refs_4_), channel_id=1, source_target_pairs={{0,1},{1,0},{2,3},{3,2},{4,5},{5,4},{6,7},{7,6},{8,9},{9,8},{10,11... | collective-permute-start | bytes 589832 | tf_op jit(solution)/shard_map/ppermute | solution.py:56
  29.4 0.4 %finish_part.3.kept_ref = f32[128,768]{1,0:T(8,128)S(1)} custom-call(bf16[128,512]{1,0:T(8,128)(2,1)S(1)} %combine.1.refs_0_, bf16[3072,256]{1,0:T(8,128)(2,1)S(1)} %copy-done.1, bf16[768,256]{1,0:T(8,128)(2,1)S(1)} %collective-permute-done.5.refs_3_.refs_2_, bf16[768,256]{1,0:T(8,128)(2,1)S(1)} %collective-permute-done.10.refs_3_, ...), custom_call_target="tpu_custom_call" | custom-call | flops 100663296 | bytes 2883584 | tf_op jit(solution)/shard_map/finish_part/pallas_call | solution.py:73
  29.8 0.8 %collective-permute-done.12.got_ref = bf16[128,768]{1,0:T(8,128)(2,1)S(1)} collective-permute-done((bf16[128,768]{1,0:T(8,128)(2,1)S(1)}, bf16[128,768]{1,0:T(8,128)(2,1)S(1)}, u32[]{:S(2)}, u32[]{:S(2)}) %collective-permute-start.12) | collective-permute-done | bytes 196640 | tf_op jit(solution)/shard_map/ppermute | solution.py:56
  30.5 0.0 collective-permute-done.11.other_ref
  30.5 1.5 %close.1 = (bf16[512,1024]{1,0:T(8,128)(2,1)}, bf16[128,768]{1,0:T(8,128)(2,1)}) custom-call(f32[512,1024]{1,0:T(8,128)S(1)} %up_near.1.refs_4_.refs_2_.acc_ref, bf16[512,512]{1,0:T(8,128)(2,1)S(1)} %collective-permute-done.11.other_ref, bf16[1024,1024]{1,0:T(8,128)(2,1)S(1)} %copy-done, f32[128,768]{1,0:T(8,128)S(1)} %finish_part.3.kept_ref, ...), custom_call_target="tpu_custom_call" | custom-call | flops 536870912 | bytes 1048576 | tf_op jit(solution)/shard_map/close/pallas_call | solution.py:415
  (2 shorter events, 0.1 us)
Async XLA Ops:
  0.6 5.7 %copy-start.2 = (bf16[128,3072]{1,0:T(8,128)(2,1)S(1)}, bf16[128,3072]{1,0:T(8,128)(2,1)}, u32[]{:S(2)}) copy-start(bf16[128,3072]{1,0:T(8,128)(2,1)} %refs_0_.1) | copy-start | bytes 2359300
  2.5 3.9 %copy-start.1 = (bf16[3072,256]{1,0:T(8,128)(2,1)S(1)}, bf16[3072,256]{1,0:T(8,128)(2,1)}, u32[]{:S(2)}) copy-start(bf16[3072,256]{1,0:T(8,128)(2,1)} %refs_1_.7) | copy-start | bytes 4718596
  2.5 8.6 %copy-start = (bf16[1024,1024]{1,0:T(8,128)(2,1)S(1)}, bf16[1024,1024]{1,0:T(8,128)(2,1)}, u32[]{:S(2)}) copy-start(bf16[1024,1024]{1,0:T(8,128)(2,1)} %w_ref.1) | copy-start | bytes 6291460
  3.3 8.6 %collective-permute-start.3 = (bf16[512,512]{1,0:T(8,128)(2,1)S(1)}, bf16[512,512]{1,0:T(8,128)(2,1)S(1)}, u32[]{:S(2)}, u32[]{:S(2)}) collective-permute-start(bf16[512,512]{1,0:T(8,128)(2,1)S(1)} %get-tuple-element.29), channel_id=1, source_target_pairs={{0,1},{1,0},{2,3},{3,2},{4,5},{5,4},{6,7},{7,6},{8,9},{9,8},{10,11... | collective-permute-start | bytes 1572872 | tf_op jit(solution)/shard_map/ppermute | solution.py:56
  3.8 14.1 %collective-permute-start.5 = (bf16[768,256]{1,0:T(8,128)(2,1)S(1)}, bf16[768,256]{1,0:T(8,128)(2,1)S(1)}, u32[]{:S(2)}, u32[]{:S(2)}) collective-permute-start(bf16[768,256]{1,0:T(8,128)(2,1)S(1)} %get-tuple-element.35), channel_id=1, source_target_pairs={{0,2},{1,3},{2,0},{3,1},{4,6},{5,7},{6,4},{7,5},{8,10},{9,11},{10,... | collective-permute-start | bytes 1179656 | tf_op jit(solution)/shard_map/ppermute | solution.py:56
  6.7 8.6 %collective-permute-start = (bf16[128,256]{1,0:T(8,128)(2,1)S(1)}, bf16[128,256]{1,0:T(8,128)(2,1)S(1)}, u32[]{:S(2)}, u32[]{:S(2)}) collective-permute-start(bf16[128,256]{1,0:T(8,128)(2,1)S(1)} %get-tuple-element.26.refs_1_), channel_id=1, source_target_pairs={{0,1},{1,0},{2,3},{3,2},{4,8},{5,9},{6,10},{7,11},{8,4},{9,5},{10,... | collective-permute-start | bytes 196616 | tf_op jit(solution)/shard_map/ppermute | solution.py:52
  7.0 8.3 %collective-permute-start.2 = (bf16[128,256]{1,0:T(8,128)(2,1)S(1)}, bf16[128,256]{1,0:T(8,128)(2,1)S(1)}, u32[]{:S(2)}, u32[]{:S(2)}) collective-permute-start(bf16[128,256]{1,0:T(8,128)(2,1)S(1)} %get-tuple-element.26.refs_1_), channel_id=1, source_target_pairs={{0,4},{1,5},{2,6},{3,7},{4,0},{5,1},{6,2},{7,3},{8,12},{9,13},{10,... | collective-permute-start | bytes 196616 | tf_op jit(solution)/shard_map/ppermute | solution.py:52
  10.0 5.3 %collective-permute-start.1 = (bf16[80,256]{1,0:T(8,128)(2,1)S(1)}, bf16[80,256]{1,0:T(8,128)(2,1)S(1)}, u32[]{:S(2)}, u32[]{:S(2)}) collective-permute-start(bf16[80,256]{1,0:T(8,128)(2,1)S(1)} %get-tuple-element.27), channel_id=1, source_target_pairs={{0,8},{1,9},{2,10},{3,11},{4,12},{5,13},{6,14},{7,15},{8,0},{9,1},... | collective-permute-start | bytes 122888 | tf_op jit(solution)/shard_map/ppermute | solution.py:52
  12.2 9.7 %collective-permute-start.6 = (bf16[144,512]{1,0:T(8,128)(2,1)S(1)}, bf16[144,512]{1,0:T(8,128)(2,1)S(1)}, u32[]{:S(2)}, u32[]{:S(2)}) collective-permute-start(bf16[144,512]{1,0:T(8,128)(2,1)S(1)} %get-tuple-element.37), channel_id=1, source_target_pairs={{0,1},{1,0},{2,3},{3,2},{4,8},{5,9},{6,10},{7,11},{8,4},{9,5},{10,... | collective-permute-start | bytes 442376 | tf_op jit(solution)/shard_map/ppermute | solution.py:52
  16.0 5.9 %collective-permute-start.8 = (bf16[128,512]{1,0:T(8,128)(2,1)S(1)}, bf16[128,512]{1,0:T(8,128)(2,1)S(1)}, u32[]{:S(2)}, u32[]{:S(2)}) collective-permute-start(bf16[128,512]{1,0:T(8,128)(2,1)S(1)} %get-tuple-element.39), channel_id=1, source_target_pairs={{0,4},{1,5},{2,6},{3,7},{4,0},{5,1},{6,2},{7,3},{8,12},{9,13},{10,... | collective-permute-start | bytes 393224 | tf_op jit(solution)/shard_map/ppermute | solution.py:52
  16.1 5.8 %collective-permute-start.7 = (bf16[80,512]{1,0:T(8,128)(2,1)S(1)}, bf16[80,512]{1,0:T(8,128)(2,1)S(1)}, u32[]{:S(2)}, u32[]{:S(2)}) collective-permute-start(bf16[80,512]{1,0:T(8,128)(2,1)S(1)} %get-tuple-element.38), channel_id=1, source_target_pairs={{0,8},{1,9},{2,10},{3,11},{4,12},{5,13},{6,14},{7,15},{8,0},{9,1},... | collective-permute-start | bytes 245768 | tf_op jit(solution)/shard_map/ppermute | solution.py:52
  17.9 9.7 %collective-permute-start.10 = (bf16[768,256]{1,0:T(8,128)(2,1)S(1)}, bf16[768,256]{1,0:T(8,128)(2,1)S(1)}, u32[]{:S(2)}, u32[]{:S(2)}) collective-permute-start(bf16[768,256]{1,0:T(8,128)(2,1)S(1)} %collective-permute-done.5.refs_3_.refs_2_), channel_id=1, source_target_pairs={{0,16},{16,0},{1,17},{17,1},{2,18},{18,2},{3,19},{19,3},{4,20},{20... | collective-permute-start | bytes 1179656 | tf_op jit(solution)/shard_map/ppermute | solution.py:315
  19.4 7.4 %collective-permute-start.4 = (bf16[512,256]{1,0:T(8,128)(2,1)S(1)}, bf16[512,256]{1,0:T(8,128)(2,1)S(1)}, u32[]{:S(2)}, u32[]{:S(2)}) collective-permute-start(bf16[512,256]{1,0:T(8,128)(2,1)S(1)} %upsample.1.refs_0_.refs_3_), channel_id=1, source_target_pairs={{0,2},{1,3},{2,0},{3,1},{4,6},{5,7},{6,4},{7,5},{8,10},{9,11},{10,... | collective-permute-start | bytes 786440 | tf_op jit(solution)/shard_map/ppermute | solution.py:56
  22.0 6.3 %collective-permute-start.9 = (bf16[128,512]{1,0:T(8,128)(2,1)S(1)}, bf16[128,512]{1,0:T(8,128)(2,1)S(1)}, u32[]{:S(2)}, u32[]{:S(2)}) collective-permute-start(bf16[128,512]{1,0:T(8,128)(2,1)S(1)} %get-tuple-element.40), channel_id=1, source_target_pairs={{0,2},{1,3},{2,0},{3,1},{4,6},{5,7},{6,4},{7,5},{8,10},{9,11},{10,... | collective-permute-start | bytes 393224 | tf_op jit(solution)/shard_map/ppermute | solution.py:56
  28.3 2.3 %collective-permute-start.11 = (bf16[512,512]{1,0:T(8,128)(2,1)S(1)}, bf16[512,512]{1,0:T(8,128)(2,1)S(1)}, u32[]{:S(2)}, u32[]{:S(2)}) collective-permute-start(bf16[512,512]{1,0:T(8,128)(2,1)S(1)} %pack.1), channel_id=1, source_target_pairs={{0,1},{1,0},{2,3},{3,2},{4,5},{5,4},{6,7},{7,6},{8,9},{9,8},{10,11... | collective-permute-start | bytes 1572872 | tf_op jit(solution)/shard_map/ppermute | solution.py:56
  28.8 1.7 %collective-permute-start.12 = (bf16[128,768]{1,0:T(8,128)(2,1)S(1)}, bf16[128,768]{1,0:T(8,128)(2,1)S(1)}, u32[]{:S(2)}, u32[]{:S(2)}) collective-permute-start(bf16[128,768]{1,0:T(8,128)(2,1)S(1)} %finish_part.2.refs_4_), channel_id=1, source_target_pairs={{0,1},{1,0},{2,3},{3,2},{4,5},{5,4},{6,7},{7,6},{8,9},{9,8},{10,11... | collective-permute-start | bytes 589832 | tf_op jit(solution)/shard_map/ppermute | solution.py:56

commit v7 on v6

--- a/solution.py
+++ b/solution.py
@@ -95,7 +95,7 @@
 
 def body(spans, w_in, band_weights, offsets, w_up, d_up):
     count = lax.axis_size("seq")
-    groups = lax.axis_size("group")
+    assert lax.axis_size("group") == 2 and lax.axis_size("tensor") == 4
     blocks, breadth = offsets.shape[0], band_weights.shape[1]
     bytes_here, hidden = d_up.shape
     block = bytes_here // blocks
@@ -148,8 +148,8 @@
             pick = (down - off_ref[b] == across_j).astype(F32).astype(BF16)
             turned_ref[:, part] = dot_t(pick, weights).astype(BF16)
 
-    def half():
-        return lax.axis_index("group") if groups == 2 else 0
+    unit = share // 6
+    x_rows, y_rows = 7 * unit, 5 * unit
 
     def open_up(
         off_hbm, weights_hbm, d_hbm, w_hbm, in_hbm, band_ref, turned_ref, d_vm, w_vm, x_ref, off, weights, sems
@@ -171,8 +171,8 @@
             for q in (2 * k, 2 * k + 1):
                 part = pl.ds(q * step, step)
                 load(d_hbm.at[part, :], d_vm.at[part, :])
-        quarter = at ^ 2 ^ half()
-        load(in_hbm.at[pl.ds(pl.multiple_of(quarter * share, share), share), :], x_ref)
+        start = lax.div(at ^ 2, 2) * (2 * share) + lax.axis_index("group") * y_rows
+        load(in_hbm.at[pl.ds(pl.multiple_of(start, unit), x_rows), :], x_ref)
         for copy in loads[:2]:
             copy.wait()
         spread(off, weights, band_ref, turned_ref)
@@ -193,7 +193,7 @@
             shape((total_cols, bytes_here)),
             shape((bytes_here, hidden)),
             shape((2, width, hidden)),
-            shape((share, width)),
+            shape((x_rows, width)),
         ],
         in_specs=[pl.BlockSpec(memory_space=pltpu.HBM)] * 5,
         out_specs=[pl.BlockSpec(memory_space=pltpu.VMEM)] * 5,
@@ -222,14 +222,17 @@
     )
     grad_got = swap(grad_sent, 1)
 
-    def project(spans_ref, w_ref, out_ref, *cut_refs):
+    def project(spans_ref, w_ref, out_ref, wide_ref, *cut_refs):
         out_ref[...] = dot(spans_ref[...], w_ref[...]).astype(BF16)
+        wide_ref[:span_rows, :] = out_ref[...]
+        wide_ref[span_rows:, :] = jnp.zeros((PAD, width), BF16)
         for ref, pairing in zip(cut_refs, longs):
             ref[...] = out_ref[pl.ds(cut_at(*pairing), far), :]
 
-    reduced, *cuts, reduced_done = call(
+    reduced, wide, *cuts, reduced_done = call(
         project,
-        [shape((span_rows, width))] + [shape((far, width)) for _ in longs],
+        [shape((span_rows, width)), shape((span_rows + PAD, width))]
+        + [shape((far, width)) for _ in longs],
         spans,
         w_in,
         flops=2 * span_rows * depth * width,
@@ -237,6 +240,7 @@
         token=True,
     )
     cut_of = dict(zip(longs, cuts))
+    cut_of[pairs[0]] = wide
     pieces = [reduced] + [trade(cut_of.get(p, reduced), p, count) for p in pairs]
 
     (grad_kept,) = call(
@@ -276,7 +280,7 @@
         *piece_refs, out_ref = refs
         acc = 0.0
         for k, ref in enumerate(piece_refs):
-            acc += dot(band_ref[:, cols[k] : cols[k] + rows[k]], ref[...])
+            acc += dot(band_ref[:, cols[k] : cols[k] + rows[k]], ref[: rows[k], :])
         out_ref[...] = acc.astype(BF16)
 
     (upsampled,) = call(
@@ -311,11 +315,13 @@
     )
 
 
-    if groups == 2:
-        w_y = lax.ppermute(w_x, "group", [(0, 1), (1, 0)])
-    else:
-        cube = w_in.reshape(4, share, width)
-        w_y = swap(lax.dynamic_index_in_dim(cube, lax.axis_index("tensor") ^ 3, 0, keepdims=False), 2)
+    def relay(w_ref, out_ref):
+        start = lax.axis_index("group") * (x_rows - y_rows)
+        out_ref[...] = w_ref[pl.ds(pl.multiple_of(start, unit), y_rows), :]
+
+    (w_for_y,) = call(relay, [shape((y_rows, width))], w_x, flops=1, after=(upsampled,))
+    w_y = lax.ppermute(w_for_y, "group", [(0, 1), (1, 0)])
+
 
     def collect(own_ref, *refs):
         *came_refs, sum_ref, sent_ref = refs
@@ -370,9 +376,18 @@
         after=(up_acc, w_y),
     )
     def finish_part(mask, mine_ref, w_ref, x_ref, y_ref, out_ref):
-        first = groups != 2 or lax.axis_index("group") == 0
-        near, far = (x_ref, y_ref) if mask == 0 else (y_ref, x_ref)
-        across = near[...] if groups != 2 else jnp.where(first, near[...], far[...])
+        group = lax.axis_index("group")
+        first = group == 0
+        tiles = []
+        for k in range(6):
+            at = (lax.rem(lax.axis_index("tensor"), 2) ^ mask) * 6 + k
+            x_at = jnp.clip(at - 5 * group, 0, 6) * unit
+            y_at = jnp.clip(at - 7 * (1 - group), 0, 4) * unit
+            x_tile = x_ref[pl.ds(pl.multiple_of(x_at, unit), unit), :]
+            y_tile = y_ref[pl.ds(pl.multiple_of(y_at, unit), unit), :]
+            by_x = (first & (at < 7)) | (~first & (at >= 5))
+            tiles.append(jnp.where(by_x, x_tile, y_tile))
+        across = jnp.concatenate(tiles, 0)
         part = dot_t(mine_ref[:, :width], block_of(w_ref, mask, share))
         out_ref[...] = (part + dot_t(mine_ref[:, width:], across)).astype(out_ref.dtype)
 

time: 32.2 us -> 31.1 us (0.966)
  waiting for transfers between devices: 9.8 us -> 8.53 us
    ppermute x6, waiting for transfers between devices: 5.72 us -> 4.53 us  [swap(): return lax.ppermute(value, 'tensor', [(i, i ^ mask) for i in range(4)])]
    pallas_call x14 -> x15, Pallas kernels: 5.38 us -> 5.41 us  [call(): pl.pallas_call(run, out_shape=outs, name=getattr(kernel, 'func', kernel)....]
  transfers between devices with their start and end apart: 13 -> 13, of which waited for: 5 -> 6; matrix products, arithmetic and copies ran while one was open for 0% -> 0% of each run, Pallas kernels for 14% -> 15%
where the time goes in v7:
time: 31.1 us; the launch traced here: 30.9 us
  starting transfers between devices  12.8 us (41%)
  Pallas kernels  8.83 us (28%)
  waiting for transfers between devices  8.53 us (27%)
  between operations  0.79 us (3%)
    ppermute x6, starting transfers between devices, trade(): return lax.ppermute(value, ('seq', 'tensor'), pairs)  6.35 us
    pallas_call x15, Pallas kernels, call(): pl.pallas_call(run, out_shape=outs, name=getattr(kernel, 'func', kernel)....  5.41 us
    ppermute x6, starting transfers between devices, swap(): return lax.ppermute(value, 'tensor', [(i, i ^ mask) for i in range(4)])  4.84 us
    ppermute x6, waiting for transfers between devices, swap(): return lax.ppermute(value, 'tensor', [(i, i ^ mask) for i in range(4)])  4.53 us
    ppermute x6, waiting for transfers between devices, trade(): return lax.ppermute(value, ('seq', 'tensor'), pairs)  3.99 us
    pallas_call x1, Pallas kernels, body(): pl.pallas_call(open_up, out_shape=[shape((bytes_here, total_cols)), shape...  1.87 us
    ppermute x1, starting transfers between devices, body(): w_y = lax.ppermute(w_for_y, 'group', [(0, 1), (1, 0)])  1.59 us
    pallas_call x1, Pallas kernels, body(): pl.pallas_call(close, out_shape=[shape((bytes_here, hidden)), shape((span...  1.56 us
  transfers between devices with their start and end apart: 13, of which 6 were waited for; matrix products, arithmetic and copies ran while one was open for 0% of the time, Pallas kernels for 15%

profile of v7, /device:TPU:0, one launch (start us, length us, event | category | flops | bytes accessed | tf_op | source)
XLA Modules:
  0.0 30.9 jit_solution(8602608795749249806)
XLA Ops:
  0.6 0.0 copy-start.2
  0.6 1.9 %open_up.1 = (bf16[512,512]{1,0:T(8,128)(2,1)S(1)}, bf16[512,512]{1,0:T(8,128)(2,1)S(1)}, bf16[512,1024]{1,0:T(8,128)(2,1)S(1)}, bf16[2,256,1024]{2,1,0:T(8,128)(2,1)S(1)}, bf16[896,256]{1,0:T(8,128)(2,1)S(1)}) custom-call(s32[4]{0:T(128)} %off_hbm.1, bf16[512,128]{1,0:T(8,128)(2,1)} %weights_hbm.1, bf16[512,1024]{1,0:T(8,128)(2,1)} %d_hbm.1, ...), custom_call_target="tpu_custom_call" | custom-call | flops 536870912 | bytes 2097152 | tf_op jit(solution)/shard_map/open_up/pallas_call | solution.py:189
  2.5 0.0 copy-start.1
  2.5 0.0 copy-start
  2.5 0.7 %grad_for_other.1 = (bf16[512,512]{1,0:T(8,128)(2,1)S(1)}, f32[8,128]{1,0:T(8,128)S(1)}) custom-call(bf16[512,1024]{1,0:T(8,128)(2,1)S(1)} %get-tuple-element.24.refs_0_, bf16[2,256,1024]{2,1,0:T(8,128)(2,1)S(1)} %get-tuple-element.25.refs_1_), custom_call_target="tpu_custom_call" | custom-call | flops 536870912 | bytes 2621440 | tf_op jit(solution)/shard_map/grad_for_other/pallas_call | solution.py:73
  3.3 0.5 %collective-permute-start.3 = (bf16[512,512]{1,0:T(8,128)(2,1)S(1)}, bf16[512,512]{1,0:T(8,128)(2,1)S(1)}, u32[]{:S(2)}, u32[]{:S(2)}) collective-permute-start(bf16[512,512]{1,0:T(8,128)(2,1)S(1)} %get-tuple-element.31), channel_id=1, source_target_pairs={{0,1},{1,0},{2,3},{3,2},{4,5},{5,4},{6,7},{7,6},{8,9},{9,8},{10,11... | collective-permute-start | bytes 1572872 | tf_op jit(solution)/shard_map/ppermute | solution.py:56
  3.8 2.6 %collective-permute-start.5 = (bf16[896,256]{1,0:T(8,128)(2,1)S(1)}, bf16[896,256]{1,0:T(8,128)(2,1)S(1)}, u32[]{:S(2)}, u32[]{:S(2)}) collective-permute-start(bf16[896,256]{1,0:T(8,128)(2,1)S(1)} %get-tuple-element.37), channel_id=1, source_target_pairs={{0,2},{1,3},{2,0},{3,1},{4,6},{5,7},{6,4},{7,5},{8,10},{9,11},{10,... | collective-permute-start | bytes 1376264 | tf_op jit(solution)/shard_map/ppermute | solution.py:56
  6.4 0.0 copy-done.2
  6.4 0.0 copy-done.1
  6.4 0.4 %project.1 = (bf16[128,256]{1,0:T(8,128)(2,1)S(1)}, bf16[144,256]{1,0:T(8,128)(2,1)S(1)}, bf16[80,256]{1,0:T(8,128)(2,1)S(1)}, f32[8,128]{1,0:T(8,128)S(1)}) custom-call(bf16[128,3072]{1,0:T(8,128)(2,1)S(1)} %copy-done.2, bf16[3072,256]{1,0:T(8,128)(2,1)S(1)} %copy-done.1, f32[8,128]{1,0:T(8,128)S(1)} %get-tuple-element.26.refs_2_), custom_call_target="tpu_custom_call" | custom-call | flops 201326592 | bytes 2539520 | tf_op jit(solution)/shard_map/project/pallas_call | solution.py:73
  6.8 0.2 collective-permute-start
  7.0 3.0 %collective-permute-start.2 = (bf16[128,256]{1,0:T(8,128)(2,1)S(1)}, bf16[128,256]{1,0:T(8,128)(2,1)S(1)}, u32[]{:S(2)}, u32[]{:S(2)}) collective-permute-start(bf16[128,256]{1,0:T(8,128)(2,1)S(1)} %get-tuple-element.27.refs_1_), channel_id=1, source_target_pairs={{0,4},{1,5},{2,6},{3,7},{4,0},{5,1},{6,2},{7,3},{8,12},{9,13},{10,... | collective-permute-start | bytes 196616 | tf_op jit(solution)/shard_map/ppermute | solution.py:52
  10.0 1.2 %collective-permute-start.1 = (bf16[80,256]{1,0:T(8,128)(2,1)S(1)}, bf16[80,256]{1,0:T(8,128)(2,1)S(1)}, u32[]{:S(2)}, u32[]{:S(2)}) collective-permute-start(bf16[80,256]{1,0:T(8,128)(2,1)S(1)} %get-tuple-element.29), channel_id=1, source_target_pairs={{0,8},{1,9},{2,10},{3,11},{4,12},{5,13},{6,14},{7,15},{8,0},{9,1},... | collective-permute-start | bytes 122888 | tf_op jit(solution)/shard_map/ppermute | solution.py:52
  11.2 0.0 copy-done
  11.2 0.7 %grad_part.1.refs_0_ = f32[512,512]{1,0:T(8,128)S(1)} custom-call(bf16[512,1024]{1,0:T(8,128)(2,1)S(1)} %get-tuple-element.24.refs_0_, bf16[1024,1024]{1,0:T(8,128)(2,1)S(1)} %copy-done, f32[8,128]{1,0:T(8,128)S(1)} %get-tuple-element.30.refs_2_), custom_call_target="tpu_custom_call" | custom-call | flops 536870912 | bytes 4194304 | tf_op jit(solution)/shard_map/grad_part/pallas_call | solution.py:73
  11.9 0.0 collective-permute-done.3.refs_1_
  11.9 0.3 first_share.1
  12.2 0.1 collective-permute-start.6
  12.3 0.2 next_share.3
  12.5 2.8 %collective-permute-done.1.refs_3_ = bf16[80,256]{1,0:T(8,128)(2,1)S(1)} collective-permute-done((bf16[80,256]{1,0:T(8,128)(2,1)S(1)}, bf16[80,256]{1,0:T(8,128)(2,1)S(1)}, u32[]{:S(2)}, u32[]{:S(2)}) %collective-permute-start.1) | collective-permute-done | bytes 40992 | tf_op jit(solution)/shard_map/ppermute | solution.py:52
  15.3 0.0 collective-permute-done.2.refs_4_
  15.3 0.0 collective-permute-done.refs_2_
  15.3 0.4 %upsample.1.refs_0_.refs_3_.refs_1_ = bf16[512,256]{1,0:T(8,128)(2,1)S(1)} custom-call(bf16[512,512]{1,0:T(8,128)(2,1)S(1)} %get-tuple-element.23.refs_0_, bf16[128,256]{1,0:T(8,128)(2,1)S(1)} %get-tuple-element.27.refs_1_, bf16[144,256]{1,0:T(8,128)(2,1)S(1)} %collective-permute-done.refs_2_, bf16[80,256]{1,0:T(8,128)(2,1)S(1)} %collective-permute-done.1.refs_3_, ...), custom_call_target="tpu_custom_call" | custom-call | flops 121634816 | bytes 1032192 | tf_op jit(solution)/shard_map/upsample/pallas_call | solution.py:73
  15.8 0.2 next_share.4
  16.0 0.1 collective-permute-start.8
  16.1 1.8 %collective-permute-start.7 = (bf16[80,512]{1,0:T(8,128)(2,1)S(1)}, bf16[80,512]{1,0:T(8,128)(2,1)S(1)}, u32[]{:S(2)}, u32[]{:S(2)}) collective-permute-start(bf16[80,512]{1,0:T(8,128)(2,1)S(1)} %get-tuple-element.40), channel_id=1, source_target_pairs={{0,8},{1,9},{2,10},{3,11},{4,12},{5,13},{6,14},{7,15},{8,0},{9,1},... | collective-permute-start | bytes 245768 | tf_op jit(solution)/shard_map/ppermute | solution.py:52
  17.9 0.5 %collective-permute-start.4 = (bf16[512,256]{1,0:T(8,128)(2,1)S(1)}, bf16[512,256]{1,0:T(8,128)(2,1)S(1)}, u32[]{:S(2)}, u32[]{:S(2)}) collective-permute-start(bf16[512,256]{1,0:T(8,128)(2,1)S(1)} %upsample.1.refs_0_.refs_3_.refs_1_), channel_id=1, source_target_pairs={{0,2},{1,3},{2,0},{3,1},{4,6},{5,7},{6,4},{7,5},{8,10},{9,11},{10,... | collective-permute-start | bytes 786440 | tf_op jit(solution)/shard_map/ppermute | solution.py:56
  18.4 0.0 collective-permute-done.5.refs_3_.refs_0_.refs_2_
  18.4 1.6 %collective-permute-start.10 = (bf16[640,256]{1,0:T(8,128)(2,1)S(1)}, bf16[640,256]{1,0:T(8,128)(2,1)S(1)}, u32[]{:S(2)}, u32[]{:S(2)}) collective-permute-start(bf16[640,256]{1,0:T(8,128)(2,1)S(1)} %relay.1), channel_id=1, source_target_pairs={{0,16},{16,0},{1,17},{17,1},{2,18},{18,2},{3,19},{19,3},{4,20},{20... | collective-permute-start | bytes 983048 | tf_op jit(solution)/shard_map/ppermute | solution.py:323
  20.0 0.7 %next_share.5 = (f32[128,512]{1,0:T(8,128)S(1)}, f32[8,128]{1,0:T(8,128)}) custom-call(bf16[512,512]{1,0:T(8,128)(2,1)S(1)} %get-tuple-element.34.refs_0_, bf16[512,512]{1,0:T(8,128)(2,1)S(1)} %get-tuple-element.32.refs_2_.refs_1_, f32[8,128]{1,0:T(8,128)S(1)} %get-tuple-element.36.refs_2_, bf16[896,256]{1,0:T(8,128)(2,1)S(1)} %collective-permute-done.5.refs_3_.refs_0_.refs_2_), custom_call_target="tpu_custom_call" | custom-call | flops 67108864 | bytes 1310720 | tf_op jit(solution)/shard_map/next_share/pallas_call | solution.py:73
  20.7 1.1 %collective-permute-done.7.refs_2_ = bf16[80,512]{1,0:T(8,128)(2,1)S(1)} collective-permute-done((bf16[80,512]{1,0:T(8,128)(2,1)S(1)}, bf16[80,512]{1,0:T(8,128)(2,1)S(1)}, u32[]{:S(2)}, u32[]{:S(2)}) %collective-permute-start.7) | collective-permute-done | bytes 81952 | tf_op jit(solution)/shard_map/ppermute | solution.py:52
  21.8 0.1 collective-permute-done.8.refs_3_
  21.9 0.0 collective-permute-done.6.refs_1_
  21.9 0.1 collect.1
  22.0 0.6 %collective-permute-start.9 = (bf16[128,512]{1,0:T(8,128)(2,1)S(1)}, bf16[128,512]{1,0:T(8,128)(2,1)S(1)}, u32[]{:S(2)}, u32[]{:S(2)}) collective-permute-start(bf16[128,512]{1,0:T(8,128)(2,1)S(1)} %get-tuple-element.42), channel_id=1, source_target_pairs={{0,2},{1,3},{2,0},{3,1},{4,6},{5,7},{6,4},{7,5},{8,10},{9,11},{10,... | collective-permute-start | bytes 393224 | tf_op jit(solution)/shard_map/ppermute | solution.py:56
  22.6 3.1 %collective-permute-done.4.refs_1_ = bf16[512,256]{1,0:T(8,128)(2,1)S(1)} collective-permute-done((bf16[512,256]{1,0:T(8,128)(2,1)S(1)}, bf16[512,256]{1,0:T(8,128)(2,1)S(1)}, u32[]{:S(2)}, u32[]{:S(2)}) %collective-permute-start.4) | collective-permute-done | bytes 262176 | tf_op jit(solution)/shard_map/ppermute | solution.py:56
  25.7 0.7 %up_near.1.refs_4_.refs_2_.acc_ref = f32[512,1024]{1,0:T(8,128)S(1)} custom-call(bf16[512,256]{1,0:T(8,128)(2,1)S(1)} %upsample.1.refs_0_.refs_3_.refs_1_, bf16[512,256]{1,0:T(8,128)(2,1)S(1)} %collective-permute-done.4.refs_1_, bf16[1024,1024]{1,0:T(8,128)(2,1)S(1)} %copy-done), custom_call_target="tpu_custom_call" | custom-call | flops 536870912 | bytes 4718592 | tf_op jit(solution)/shard_map/up_near/pallas_call | solution.py:73
  26.4 0.7 %collective-permute-done.9.refs_2_.refs_1_ = bf16[128,512]{1,0:T(8,128)(2,1)S(1)} collective-permute-done((bf16[128,512]{1,0:T(8,128)(2,1)S(1)}, bf16[128,512]{1,0:T(8,128)(2,1)S(1)}, u32[]{:S(2)}, u32[]{:S(2)}) %collective-permute-start.9) | collective-permute-done | bytes 131104 | tf_op jit(solution)/shard_map/ppermute | solution.py:56
  27.1 0.0 collective-permute-done.10.refs_3_
  27.1 0.1 collective-permute-start.11
  27.2 0.4 %finish_part.2.refs_4_ = bf16[128,768]{1,0:T(8,128)(2,1)S(1)} custom-call(bf16[128,512]{1,0:T(8,128)(2,1)S(1)} %combine.1.refs_0_, bf16[3072,256]{1,0:T(8,128)(2,1)S(1)} %copy-done.1, bf16[896,256]{1,0:T(8,128)(2,1)S(1)} %collective-permute-done.5.refs_3_.refs_0_.refs_2_, bf16[640,256]{1,0:T(8,128)(2,1)S(1)} %collective-permute-done.10.refs_3_), custom_call_target="tpu_custom_call" | custom-call | flops 100663296 | bytes 2686976 | tf_op jit(solution)/shard_map/finish_part/pallas_call | solution.py:73
  27.7 0.6 %collective-permute-start.12 = (bf16[128,768]{1,0:T(8,128)(2,1)S(1)}, bf16[128,768]{1,0:T(8,128)(2,1)S(1)}, u32[]{:S(2)}, u32[]{:S(2)}) collective-permute-start(bf16[128,768]{1,0:T(8,128)(2,1)S(1)} %finish_part.2.refs_4_), channel_id=1, source_target_pairs={{0,1},{1,0},{2,3},{3,2},{4,5},{5,4},{6,7},{7,6},{8,9},{9,8},{10,11... | collective-permute-start | bytes 589832 | tf_op jit(solution)/shard_map/ppermute | solution.py:56
  28.2 0.4 %finish_part.3.kept_ref = f32[128,768]{1,0:T(8,128)S(1)} custom-call(bf16[128,512]{1,0:T(8,128)(2,1)S(1)} %combine.1.refs_0_, bf16[3072,256]{1,0:T(8,128)(2,1)S(1)} %copy-done.1, bf16[896,256]{1,0:T(8,128)(2,1)S(1)} %collective-permute-done.5.refs_3_.refs_0_.refs_2_, bf16[640,256]{1,0:T(8,128)(2,1)S(1)} %collective-permute-done.10.refs_3_, ...), custom_call_target="tpu_custom_call" | custom-call | flops 100663296 | bytes 2883584 | tf_op jit(solution)/shard_map/finish_part/pallas_call | solution.py:73
  28.6 0.8 %collective-permute-done.12.got_ref = bf16[128,768]{1,0:T(8,128)(2,1)S(1)} collective-permute-done((bf16[128,768]{1,0:T(8,128)(2,1)S(1)}, bf16[128,768]{1,0:T(8,128)(2,1)S(1)}, u32[]{:S(2)}, u32[]{:S(2)}) %collective-permute-start.12) | collective-permute-done | bytes 196640 | tf_op jit(solution)/shard_map/ppermute | solution.py:56
  29.4 0.0 collective-permute-done.11.other_ref
  29.4 1.6 %close.1 = (bf16[512,1024]{1,0:T(8,128)(2,1)}, bf16[128,768]{1,0:T(8,128)(2,1)}) custom-call(f32[512,1024]{1,0:T(8,128)S(1)} %up_near.1.refs_4_.refs_2_.acc_ref, bf16[512,512]{1,0:T(8,128)(2,1)S(1)} %collective-permute-done.11.other_ref, bf16[1024,1024]{1,0:T(8,128)(2,1)S(1)} %copy-done, f32[128,768]{1,0:T(8,128)S(1)} %finish_part.3.kept_ref, ...), custom_call_target="tpu_custom_call" | custom-call | flops 536870912 | bytes 1048576 | tf_op jit(solution)/shard_map/close/pallas_call | solution.py:430
  (3 shorter events, 0.1 us)
Async XLA Ops:
  0.6 5.7 %copy-start.2 = (bf16[128,3072]{1,0:T(8,128)(2,1)S(1)}, bf16[128,3072]{1,0:T(8,128)(2,1)}, u32[]{:S(2)}) copy-start(bf16[128,3072]{1,0:T(8,128)(2,1)} %refs_0_.1) | copy-start | bytes 2359300
  2.5 3.9 %copy-start.1 = (bf16[3072,256]{1,0:T(8,128)(2,1)S(1)}, bf16[3072,256]{1,0:T(8,128)(2,1)}, u32[]{:S(2)}) copy-start(bf16[3072,256]{1,0:T(8,128)(2,1)} %refs_1_.7) | copy-start | bytes 4718596
  2.5 8.6 %copy-start = (bf16[1024,1024]{1,0:T(8,128)(2,1)S(1)}, bf16[1024,1024]{1,0:T(8,128)(2,1)}, u32[]{:S(2)}) copy-start(bf16[1024,1024]{1,0:T(8,128)(2,1)} %w_ref.1) | copy-start | bytes 6291460
  3.3 8.6 %collective-permute-start.3 = (bf16[512,512]{1,0:T(8,128)(2,1)S(1)}, bf16[512,512]{1,0:T(8,128)(2,1)S(1)}, u32[]{:S(2)}, u32[]{:S(2)}) collective-permute-start(bf16[512,512]{1,0:T(8,128)(2,1)S(1)} %get-tuple-element.31), channel_id=1, source_target_pairs={{0,1},{1,0},{2,3},{3,2},{4,5},{5,4},{6,7},{7,6},{8,9},{9,8},{10,11... | collective-permute-start | bytes 1572872 | tf_op jit(solution)/shard_map/ppermute | solution.py:56
  3.8 14.6 %collective-permute-start.5 = (bf16[896,256]{1,0:T(8,128)(2,1)S(1)}, bf16[896,256]{1,0:T(8,128)(2,1)S(1)}, u32[]{:S(2)}, u32[]{:S(2)}) collective-permute-start(bf16[896,256]{1,0:T(8,128)(2,1)S(1)} %get-tuple-element.37), channel_id=1, source_target_pairs={{0,2},{1,3},{2,0},{3,1},{4,6},{5,7},{6,4},{7,5},{8,10},{9,11},{10,... | collective-permute-start | bytes 1376264 | tf_op jit(solution)/shard_map/ppermute | solution.py:56
  6.8 8.6 %collective-permute-start = (bf16[144,256]{1,0:T(8,128)(2,1)S(1)}, bf16[144,256]{1,0:T(8,128)(2,1)S(1)}, u32[]{:S(2)}, u32[]{:S(2)}) collective-permute-start(bf16[144,256]{1,0:T(8,128)(2,1)S(1)} %get-tuple-element.28), channel_id=1, source_target_pairs={{0,1},{1,0},{2,3},{3,2},{4,8},{5,9},{6,10},{7,11},{8,4},{9,5},{10,... | collective-permute-start | bytes 221192 | tf_op jit(solution)/shard_map/ppermute | solution.py:52
  7.0 8.3 %collective-permute-start.2 = (bf16[128,256]{1,0:T(8,128)(2,1)S(1)}, bf16[128,256]{1,0:T(8,128)(2,1)S(1)}, u32[]{:S(2)}, u32[]{:S(2)}) collective-permute-start(bf16[128,256]{1,0:T(8,128)(2,1)S(1)} %get-tuple-element.27.refs_1_), channel_id=1, source_target_pairs={{0,4},{1,5},{2,6},{3,7},{4,0},{5,1},{6,2},{7,3},{8,12},{9,13},{10,... | collective-permute-start | bytes 196616 | tf_op jit(solution)/shard_map/ppermute | solution.py:52
  10.0 5.3 %collective-permute-start.1 = (bf16[80,256]{1,0:T(8,128)(2,1)S(1)}, bf16[80,256]{1,0:T(8,128)(2,1)S(1)}, u32[]{:S(2)}, u32[]{:S(2)}) collective-permute-start(bf16[80,256]{1,0:T(8,128)(2,1)S(1)} %get-tuple-element.29), channel_id=1, source_target_pairs={{0,8},{1,9},{2,10},{3,11},{4,12},{5,13},{6,14},{7,15},{8,0},{9,1},... | collective-permute-start | bytes 122888 | tf_op jit(solution)/shard_map/ppermute | solution.py:52
  12.2 9.7 %collective-permute-start.6 = (bf16[144,512]{1,0:T(8,128)(2,1)S(1)}, bf16[144,512]{1,0:T(8,128)(2,1)S(1)}, u32[]{:S(2)}, u32[]{:S(2)}) collective-permute-start(bf16[144,512]{1,0:T(8,128)(2,1)S(1)} %get-tuple-element.39), channel_id=1, source_target_pairs={{0,1},{1,0},{2,3},{3,2},{4,8},{5,9},{6,10},{7,11},{8,4},{9,5},{10,... | collective-permute-start | bytes 442376 | tf_op jit(solution)/shard_map/ppermute | solution.py:52
  16.0 5.9 %collective-permute-start.8 = (bf16[128,512]{1,0:T(8,128)(2,1)S(1)}, bf16[128,512]{1,0:T(8,128)(2,1)S(1)}, u32[]{:S(2)}, u32[]{:S(2)}) collective-permute-start(bf16[128,512]{1,0:T(8,128)(2,1)S(1)} %get-tuple-element.41), channel_id=1, source_target_pairs={{0,4},{1,5},{2,6},{3,7},{4,0},{5,1},{6,2},{7,3},{8,12},{9,13},{10,... | collective-permute-start | bytes 393224 | tf_op jit(solution)/shard_map/ppermute | solution.py:52
  16.1 5.7 %collective-permute-start.7 = (bf16[80,512]{1,0:T(8,128)(2,1)S(1)}, bf16[80,512]{1,0:T(8,128)(2,1)S(1)}, u32[]{:S(2)}, u32[]{:S(2)}) collective-permute-start(bf16[80,512]{1,0:T(8,128)(2,1)S(1)} %get-tuple-element.40), channel_id=1, source_target_pairs={{0,8},{1,9},{2,10},{3,11},{4,12},{5,13},{6,14},{7,15},{8,0},{9,1},... | collective-permute-start | bytes 245768 | tf_op jit(solution)/shard_map/ppermute | solution.py:52
  17.9 7.8 %collective-permute-start.4 = (bf16[512,256]{1,0:T(8,128)(2,1)S(1)}, bf16[512,256]{1,0:T(8,128)(2,1)S(1)}, u32[]{:S(2)}, u32[]{:S(2)}) collective-permute-start(bf16[512,256]{1,0:T(8,128)(2,1)S(1)} %upsample.1.refs_0_.refs_3_.refs_1_), channel_id=1, source_target_pairs={{0,2},{1,3},{2,0},{3,1},{4,6},{5,7},{6,4},{7,5},{8,10},{9,11},{10,... | collective-permute-start | bytes 786440 | tf_op jit(solution)/shard_map/ppermute | solution.py:56
  18.4 8.6 %collective-permute-start.10 = (bf16[640,256]{1,0:T(8,128)(2,1)S(1)}, bf16[640,256]{1,0:T(8,128)(2,1)S(1)}, u32[]{:S(2)}, u32[]{:S(2)}) collective-permute-start(bf16[640,256]{1,0:T(8,128)(2,1)S(1)} %relay.1), channel_id=1, source_target_pairs={{0,16},{16,0},{1,17},{17,1},{2,18},{18,2},{3,19},{19,3},{4,20},{20... | collective-permute-start | bytes 983048 | tf_op jit(solution)/shard_map/ppermute | solution.py:323
  22.0 5.1 %collective-permute-start.9 = (bf16[128,512]{1,0:T(8,128)(2,1)S(1)}, bf16[128,512]{1,0:T(8,128)(2,1)S(1)}, u32[]{:S(2)}, u32[]{:S(2)}) collective-permute-start(bf16[128,512]{1,0:T(8,128)(2,1)S(1)} %get-tuple-element.42), channel_id=1, source_target_pairs={{0,2},{1,3},{2,0},{3,1},{4,6},{5,7},{6,4},{7,5},{8,10},{9,11},{10,... | collective-permute-start | bytes 393224 | tf_op jit(solution)/shard_map/ppermute | solution.py:56
  27.1 2.3 %collective-permute-start.11 = (bf16[512,512]{1,0:T(8,128)(2,1)S(1)}, bf16[512,512]{1,0:T(8,128)(2,1)S(1)}, u32[]{:S(2)}, u32[]{:S(2)}) collective-permute-start(bf16[512,512]{1,0:T(8,128)(2,1)S(1)} %pack.1), channel_id=1, source_target_pairs={{0,1},{1,0},{2,3},{3,2},{4,5},{5,4},{6,7},{7,6},{8,9},{9,8},{10,11... | collective-permute-start | bytes 1572872 | tf_op jit(solution)/shard_map/ppermute | solution.py:56
  27.7 1.7 %collective-permute-start.12 = (bf16[128,768]{1,0:T(8,128)(2,1)S(1)}, bf16[128,768]{1,0:T(8,128)(2,1)S(1)}, u32[]{:S(2)}, u32[]{:S(2)}) collective-permute-start(bf16[128,768]{1,0:T(8,128)(2,1)S(1)} %finish_part.2.refs_4_), channel_id=1, source_target_pairs={{0,1},{1,0},{2,3},{3,2},{4,5},{5,4},{6,7},{7,6},{8,9},{9,8},{10,11... | collective-permute-start | bytes 589832 | tf_op jit(solution)/shard_map/ppermute | solution.py:56

commit v8 on v7

--- a/solution.py
+++ b/solution.py
@@ -416,8 +416,8 @@
 
         spans_vm[...] = (kept_ref[...] + got_ref[...].astype(F32)).astype(BF16)
         store(spans_vm, spans_hbm)
-        step = bytes_here // 4
-        for q in range(4):
+        step = bytes_here // 2
+        for q in range(2):
             part = slice(q * step, (q + 1) * step)
             acc = acc_ref[part, :] + dot(other_ref[part, :width], block_of(w_ref, 1, width))
             acc += dot(other_ref[part, width:], block_of(w_ref, 3, width))
@@ -435,7 +435,7 @@
         scratch_shapes=[
             pltpu.VMEM((bytes_here, hidden), BF16),
             pltpu.VMEM((span_rows, share), BF16),
-            pltpu.SemaphoreType.DMA((5,)),
+            pltpu.SemaphoreType.DMA((3,)),
         ],
         name="close",
         compiler_params=pltpu.CompilerParams(vmem_limit_bytes=16 << 20),

time: 31.1 us -> 31.2 us (level)
  no operation moved by 1% of the time
where the time goes in v8:
time: 31.2 us; the launch traced here: 31 us
  starting transfers between devices  12.8 us (41%)
  Pallas kernels  8.91 us (29%)
  waiting for transfers between devices  8.53 us (27%)
  between operations  0.79 us (3%)
    ppermute x6, starting transfers between devices, trade(): return lax.ppermute(value, ('seq', 'tensor'), pairs)  6.35 us
    pallas_call x15, Pallas kernels, call(): pl.pallas_call(run, out_shape=outs, name=getattr(kernel, 'func', kernel)....  5.41 us
    ppermute x6, starting transfers between devices, swap(): return lax.ppermute(value, 'tensor', [(i, i ^ mask) for i in range(4)])  4.84 us
    ppermute x6, waiting for transfers between devices, swap(): return lax.ppermute(value, 'tensor', [(i, i ^ mask) for i in range(4)])  4.53 us
    ppermute x6, waiting for transfers between devices, trade(): return lax.ppermute(value, ('seq', 'tensor'), pairs)  3.99 us
    pallas_call x1, Pallas kernels, body(): pl.pallas_call(open_up, out_shape=[shape((bytes_here, total_cols)), shape...  1.87 us
    pallas_call x1, Pallas kernels, body(): pl.pallas_call(close, out_shape=[shape((bytes_here, hidden)), shape((span...  1.63 us
    ppermute x1, starting transfers between devices, body(): w_y = lax.ppermute(w_for_y, 'group', [(0, 1), (1, 0)])  1.59 us
  transfers between devices with their start and end apart: 13, of which 6 were waited for; matrix products, arithmetic and copies ran while one was open for 0% of the time, Pallas kernels for 15%

profile of v8, /device:TPU:0, one launch (start us, length us, event | category | flops | bytes accessed | tf_op | source)
XLA Modules:
  0.0 31.0 jit_solution(7022470432230794961)
XLA Ops:
  0.6 0.0 copy-start.2
  0.6 1.9 %open_up.1 = (bf16[512,512]{1,0:T(8,128)(2,1)S(1)}, bf16[512,512]{1,0:T(8,128)(2,1)S(1)}, bf16[512,1024]{1,0:T(8,128)(2,1)S(1)}, bf16[2,256,1024]{2,1,0:T(8,128)(2,1)S(1)}, bf16[896,256]{1,0:T(8,128)(2,1)S(1)}) custom-call(s32[4]{0:T(128)} %off_hbm.1, bf16[512,128]{1,0:T(8,128)(2,1)} %weights_hbm.1, bf16[512,1024]{1,0:T(8,128)(2,1)} %d_hbm.1, ...), custom_call_target="tpu_custom_call" | custom-call | flops 536870912 | bytes 2097152 | tf_op jit(solution)/shard_map/open_up/pallas_call | solution.py:189
  2.5 0.0 copy-start.1
  2.5 0.0 copy-start
  2.5 0.7 %grad_for_other.1 = (bf16[512,512]{1,0:T(8,128)(2,1)S(1)}, f32[8,128]{1,0:T(8,128)S(1)}) custom-call(bf16[512,1024]{1,0:T(8,128)(2,1)S(1)} %get-tuple-element.24.refs_0_, bf16[2,256,1024]{2,1,0:T(8,128)(2,1)S(1)} %get-tuple-element.25.refs_1_), custom_call_target="tpu_custom_call" | custom-call | flops 536870912 | bytes 2621440 | tf_op jit(solution)/shard_map/grad_for_other/pallas_call | solution.py:73
  3.3 0.5 %collective-permute-start.3 = (bf16[512,512]{1,0:T(8,128)(2,1)S(1)}, bf16[512,512]{1,0:T(8,128)(2,1)S(1)}, u32[]{:S(2)}, u32[]{:S(2)}) collective-permute-start(bf16[512,512]{1,0:T(8,128)(2,1)S(1)} %get-tuple-element.31), channel_id=1, source_target_pairs={{0,1},{1,0},{2,3},{3,2},{4,5},{5,4},{6,7},{7,6},{8,9},{9,8},{10,11... | collective-permute-start | bytes 1572872 | tf_op jit(solution)/shard_map/ppermute | solution.py:56
  3.8 2.6 %collective-permute-start.5 = (bf16[896,256]{1,0:T(8,128)(2,1)S(1)}, bf16[896,256]{1,0:T(8,128)(2,1)S(1)}, u32[]{:S(2)}, u32[]{:S(2)}) collective-permute-start(bf16[896,256]{1,0:T(8,128)(2,1)S(1)} %get-tuple-element.37), channel_id=1, source_target_pairs={{0,2},{1,3},{2,0},{3,1},{4,6},{5,7},{6,4},{7,5},{8,10},{9,11},{10,... | collective-permute-start | bytes 1376264 | tf_op jit(solution)/shard_map/ppermute | solution.py:56
  6.4 0.0 copy-done.2
  6.4 0.0 copy-done.1
  6.4 0.4 %project.1 = (bf16[128,256]{1,0:T(8,128)(2,1)S(1)}, bf16[144,256]{1,0:T(8,128)(2,1)S(1)}, bf16[80,256]{1,0:T(8,128)(2,1)S(1)}, f32[8,128]{1,0:T(8,128)S(1)}) custom-call(bf16[128,3072]{1,0:T(8,128)(2,1)S(1)} %copy-done.2, bf16[3072,256]{1,0:T(8,128)(2,1)S(1)} %copy-done.1, f32[8,128]{1,0:T(8,128)S(1)} %get-tuple-element.26.refs_2_), custom_call_target="tpu_custom_call" | custom-call | flops 201326592 | bytes 2539520 | tf_op jit(solution)/shard_map/project/pallas_call | solution.py:73
  6.8 0.2 collective-permute-start
  7.0 3.0 %collective-permute-start.2 = (bf16[128,256]{1,0:T(8,128)(2,1)S(1)}, bf16[128,256]{1,0:T(8,128)(2,1)S(1)}, u32[]{:S(2)}, u32[]{:S(2)}) collective-permute-start(bf16[128,256]{1,0:T(8,128)(2,1)S(1)} %get-tuple-element.27.refs_1_), channel_id=1, source_target_pairs={{0,4},{1,5},{2,6},{3,7},{4,0},{5,1},{6,2},{7,3},{8,12},{9,13},{10,... | collective-permute-start | bytes 196616 | tf_op jit(solution)/shard_map/ppermute | solution.py:52
  10.0 1.2 %collective-permute-start.1 = (bf16[80,256]{1,0:T(8,128)(2,1)S(1)}, bf16[80,256]{1,0:T(8,128)(2,1)S(1)}, u32[]{:S(2)}, u32[]{:S(2)}) collective-permute-start(bf16[80,256]{1,0:T(8,128)(2,1)S(1)} %get-tuple-element.29), channel_id=1, source_target_pairs={{0,8},{1,9},{2,10},{3,11},{4,12},{5,13},{6,14},{7,15},{8,0},{9,1},... | collective-permute-start | bytes 122888 | tf_op jit(solution)/shard_map/ppermute | solution.py:52
  11.2 0.0 copy-done
  11.2 0.7 %grad_part.1.refs_0_ = f32[512,512]{1,0:T(8,128)S(1)} custom-call(bf16[512,1024]{1,0:T(8,128)(2,1)S(1)} %get-tuple-element.24.refs_0_, bf16[1024,1024]{1,0:T(8,128)(2,1)S(1)} %copy-done, f32[8,128]{1,0:T(8,128)S(1)} %get-tuple-element.30.refs_2_), custom_call_target="tpu_custom_call" | custom-call | flops 536870912 | bytes 4194304 | tf_op jit(solution)/shard_map/grad_part/pallas_call | solution.py:73
  11.9 0.0 collective-permute-done.3.refs_1_
  11.9 0.3 first_share.1
  12.2 0.1 collective-permute-start.6
  12.3 0.2 next_share.3
  12.5 2.8 %collective-permute-done.1.refs_3_ = bf16[80,256]{1,0:T(8,128)(2,1)S(1)} collective-permute-done((bf16[80,256]{1,0:T(8,128)(2,1)S(1)}, bf16[80,256]{1,0:T(8,128)(2,1)S(1)}, u32[]{:S(2)}, u32[]{:S(2)}) %collective-permute-start.1) | collective-permute-done | bytes 40992 | tf_op jit(solution)/shard_map/ppermute | solution.py:52
  15.3 0.0 collective-permute-done.2.refs_4_
  15.3 0.0 collective-permute-done.refs_2_
  15.3 0.4 %upsample.1.refs_0_.refs_3_.refs_1_ = bf16[512,256]{1,0:T(8,128)(2,1)S(1)} custom-call(bf16[512,512]{1,0:T(8,128)(2,1)S(1)} %get-tuple-element.23.refs_0_, bf16[128,256]{1,0:T(8,128)(2,1)S(1)} %get-tuple-element.27.refs_1_, bf16[144,256]{1,0:T(8,128)(2,1)S(1)} %collective-permute-done.refs_2_, bf16[80,256]{1,0:T(8,128)(2,1)S(1)} %collective-permute-done.1.refs_3_, ...), custom_call_target="tpu_custom_call" | custom-call | flops 121634816 | bytes 1032192 | tf_op jit(solution)/shard_map/upsample/pallas_call | solution.py:73
  15.8 0.2 next_share.4
  16.0 0.1 collective-permute-start.8
  16.1 1.8 %collective-permute-start.7 = (bf16[80,512]{1,0:T(8,128)(2,1)S(1)}, bf16[80,512]{1,0:T(8,128)(2,1)S(1)}, u32[]{:S(2)}, u32[]{:S(2)}) collective-permute-start(bf16[80,512]{1,0:T(8,128)(2,1)S(1)} %get-tuple-element.40), channel_id=1, source_target_pairs={{0,8},{1,9},{2,10},{3,11},{4,12},{5,13},{6,14},{7,15},{8,0},{9,1},... | collective-permute-start | bytes 245768 | tf_op jit(solution)/shard_map/ppermute | solution.py:52
  17.9 0.5 %collective-permute-start.4 = (bf16[512,256]{1,0:T(8,128)(2,1)S(1)}, bf16[512,256]{1,0:T(8,128)(2,1)S(1)}, u32[]{:S(2)}, u32[]{:S(2)}) collective-permute-start(bf16[512,256]{1,0:T(8,128)(2,1)S(1)} %upsample.1.refs_0_.refs_3_.refs_1_), channel_id=1, source_target_pairs={{0,2},{1,3},{2,0},{3,1},{4,6},{5,7},{6,4},{7,5},{8,10},{9,11},{10,... | collective-permute-start | bytes 786440 | tf_op jit(solution)/shard_map/ppermute | solution.py:56
  18.4 0.0 collective-permute-done.5.refs_3_.refs_0_.refs_2_
  18.4 1.6 %collective-permute-start.10 = (bf16[640,256]{1,0:T(8,128)(2,1)S(1)}, bf16[640,256]{1,0:T(8,128)(2,1)S(1)}, u32[]{:S(2)}, u32[]{:S(2)}) collective-permute-start(bf16[640,256]{1,0:T(8,128)(2,1)S(1)} %relay.1), channel_id=1, source_target_pairs={{0,16},{16,0},{1,17},{17,1},{2,18},{18,2},{3,19},{19,3},{4,20},{20... | collective-permute-start | bytes 983048 | tf_op jit(solution)/shard_map/ppermute | solution.py:323
  20.0 0.7 %next_share.5 = (f32[128,512]{1,0:T(8,128)S(1)}, f32[8,128]{1,0:T(8,128)}) custom-call(bf16[512,512]{1,0:T(8,128)(2,1)S(1)} %get-tuple-element.34.refs_0_, bf16[512,512]{1,0:T(8,128)(2,1)S(1)} %get-tuple-element.32.refs_2_.refs_1_, f32[8,128]{1,0:T(8,128)S(1)} %get-tuple-element.36.refs_2_, bf16[896,256]{1,0:T(8,128)(2,1)S(1)} %collective-permute-done.5.refs_3_.refs_0_.refs_2_), custom_call_target="tpu_custom_call" | custom-call | flops 67108864 | bytes 1310720 | tf_op jit(solution)/shard_map/next_share/pallas_call | solution.py:73
  20.7 1.1 %collective-permute-done.7.refs_2_ = bf16[80,512]{1,0:T(8,128)(2,1)S(1)} collective-permute-done((bf16[80,512]{1,0:T(8,128)(2,1)S(1)}, bf16[80,512]{1,0:T(8,128)(2,1)S(1)}, u32[]{:S(2)}, u32[]{:S(2)}) %collective-permute-start.7) | collective-permute-done | bytes 81952 | tf_op jit(solution)/shard_map/ppermute | solution.py:52
  21.8 0.1 collective-permute-done.8.refs_3_
  21.9 0.0 collective-permute-done.6.refs_1_
  21.9 0.1 collect.1
  22.0 0.6 %collective-permute-start.9 = (bf16[128,512]{1,0:T(8,128)(2,1)S(1)}, bf16[128,512]{1,0:T(8,128)(2,1)S(1)}, u32[]{:S(2)}, u32[]{:S(2)}) collective-permute-start(bf16[128,512]{1,0:T(8,128)(2,1)S(1)} %get-tuple-element.42), channel_id=1, source_target_pairs={{0,2},{1,3},{2,0},{3,1},{4,6},{5,7},{6,4},{7,5},{8,10},{9,11},{10,... | collective-permute-start | bytes 393224 | tf_op jit(solution)/shard_map/ppermute | solution.py:56
  22.6 3.1 %collective-permute-done.4.refs_1_ = bf16[512,256]{1,0:T(8,128)(2,1)S(1)} collective-permute-done((bf16[512,256]{1,0:T(8,128)(2,1)S(1)}, bf16[512,256]{1,0:T(8,128)(2,1)S(1)}, u32[]{:S(2)}, u32[]{:S(2)}) %collective-permute-start.4) | collective-permute-done | bytes 262176 | tf_op jit(solution)/shard_map/ppermute | solution.py:56
  25.7 0.7 %up_near.1.refs_4_.refs_2_.acc_ref = f32[512,1024]{1,0:T(8,128)S(1)} custom-call(bf16[512,256]{1,0:T(8,128)(2,1)S(1)} %upsample.1.refs_0_.refs_3_.refs_1_, bf16[512,256]{1,0:T(8,128)(2,1)S(1)} %collective-permute-done.4.refs_1_, bf16[1024,1024]{1,0:T(8,128)(2,1)S(1)} %copy-done), custom_call_target="tpu_custom_call" | custom-call | flops 536870912 | bytes 4718592 | tf_op jit(solution)/shard_map/up_near/pallas_call | solution.py:73
  26.4 0.7 %collective-permute-done.9.refs_2_.refs_1_ = bf16[128,512]{1,0:T(8,128)(2,1)S(1)} collective-permute-done((bf16[128,512]{1,0:T(8,128)(2,1)S(1)}, bf16[128,512]{1,0:T(8,128)(2,1)S(1)}, u32[]{:S(2)}, u32[]{:S(2)}) %collective-permute-start.9) | collective-permute-done | bytes 131104 | tf_op jit(solution)/shard_map/ppermute | solution.py:56
  27.1 0.0 collective-permute-done.10.refs_3_
  27.1 0.1 collective-permute-start.11
  27.2 0.4 %finish_part.2.refs_4_ = bf16[128,768]{1,0:T(8,128)(2,1)S(1)} custom-call(bf16[128,512]{1,0:T(8,128)(2,1)S(1)} %combine.1.refs_0_, bf16[3072,256]{1,0:T(8,128)(2,1)S(1)} %copy-done.1, bf16[896,256]{1,0:T(8,128)(2,1)S(1)} %collective-permute-done.5.refs_3_.refs_0_.refs_2_, bf16[640,256]{1,0:T(8,128)(2,1)S(1)} %collective-permute-done.10.refs_3_), custom_call_target="tpu_custom_call" | custom-call | flops 100663296 | bytes 2686976 | tf_op jit(solution)/shard_map/finish_part/pallas_call | solution.py:73
  27.7 0.6 %collective-permute-start.12 = (bf16[128,768]{1,0:T(8,128)(2,1)S(1)}, bf16[128,768]{1,0:T(8,128)(2,1)S(1)}, u32[]{:S(2)}, u32[]{:S(2)}) collective-permute-start(bf16[128,768]{1,0:T(8,128)(2,1)S(1)} %finish_part.2.refs_4_), channel_id=1, source_target_pairs={{0,1},{1,0},{2,3},{3,2},{4,5},{5,4},{6,7},{7,6},{8,9},{9,8},{10,11... | collective-permute-start | bytes 589832 | tf_op jit(solution)/shard_map/ppermute | solution.py:56
  28.2 0.4 %finish_part.3.kept_ref = f32[128,768]{1,0:T(8,128)S(1)} custom-call(bf16[128,512]{1,0:T(8,128)(2,1)S(1)} %combine.1.refs_0_, bf16[3072,256]{1,0:T(8,128)(2,1)S(1)} %copy-done.1, bf16[896,256]{1,0:T(8,128)(2,1)S(1)} %collective-permute-done.5.refs_3_.refs_0_.refs_2_, bf16[640,256]{1,0:T(8,128)(2,1)S(1)} %collective-permute-done.10.refs_3_, ...), custom_call_target="tpu_custom_call" | custom-call | flops 100663296 | bytes 2883584 | tf_op jit(solution)/shard_map/finish_part/pallas_call | solution.py:73
  28.6 0.8 %collective-permute-done.12.got_ref = bf16[128,768]{1,0:T(8,128)(2,1)S(1)} collective-permute-done((bf16[128,768]{1,0:T(8,128)(2,1)S(1)}, bf16[128,768]{1,0:T(8,128)(2,1)S(1)}, u32[]{:S(2)}, u32[]{:S(2)}) %collective-permute-start.12) | collective-permute-done | bytes 196640 | tf_op jit(solution)/shard_map/ppermute | solution.py:56
  29.4 0.0 collective-permute-done.11.other_ref
  29.4 1.6 %close.1 = (bf16[512,1024]{1,0:T(8,128)(2,1)}, bf16[128,768]{1,0:T(8,128)(2,1)}) custom-call(f32[512,1024]{1,0:T(8,128)S(1)} %up_near.1.refs_4_.refs_2_.acc_ref, bf16[512,512]{1,0:T(8,128)(2,1)S(1)} %collective-permute-done.11.other_ref, bf16[1024,1024]{1,0:T(8,128)(2,1)S(1)} %copy-done, f32[128,768]{1,0:T(8,128)S(1)} %finish_part.3.kept_ref, ...), custom_call_target="tpu_custom_call" | custom-call | flops 536870912 | bytes 1048576 | tf_op jit(solution)/shard_map/close/pallas_call | solution.py:430
  (3 shorter events, 0.1 us)
Async XLA Ops:
  0.6 5.7 %copy-start.2 = (bf16[128,3072]{1,0:T(8,128)(2,1)S(1)}, bf16[128,3072]{1,0:T(8,128)(2,1)}, u32[]{:S(2)}) copy-start(bf16[128,3072]{1,0:T(8,128)(2,1)} %refs_0_.1) | copy-start | bytes 2359300
  2.5 3.9 %copy-start.1 = (bf16[3072,256]{1,0:T(8,128)(2,1)S(1)}, bf16[3072,256]{1,0:T(8,128)(2,1)}, u32[]{:S(2)}) copy-start(bf16[3072,256]{1,0:T(8,128)(2,1)} %refs_1_.7) | copy-start | bytes 4718596
  2.5 8.6 %copy-start = (bf16[1024,1024]{1,0:T(8,128)(2,1)S(1)}, bf16[1024,1024]{1,0:T(8,128)(2,1)}, u32[]{:S(2)}) copy-start(bf16[1024,1024]{1,0:T(8,128)(2,1)} %w_ref.1) | copy-start | bytes 6291460
  3.3 8.6 %collective-permute-start.3 = (bf16[512,512]{1,0:T(8,128)(2,1)S(1)}, bf16[512,512]{1,0:T(8,128)(2,1)S(1)}, u32[]{:S(2)}, u32[]{:S(2)}) collective-permute-start(bf16[512,512]{1,0:T(8,128)(2,1)S(1)} %get-tuple-element.31), channel_id=1, source_target_pairs={{0,1},{1,0},{2,3},{3,2},{4,5},{5,4},{6,7},{7,6},{8,9},{9,8},{10,11... | collective-permute-start | bytes 1572872 | tf_op jit(solution)/shard_map/ppermute | solution.py:56
  3.8 14.6 %collective-permute-start.5 = (bf16[896,256]{1,0:T(8,128)(2,1)S(1)}, bf16[896,256]{1,0:T(8,128)(2,1)S(1)}, u32[]{:S(2)}, u32[]{:S(2)}) collective-permute-start(bf16[896,256]{1,0:T(8,128)(2,1)S(1)} %get-tuple-element.37), channel_id=1, source_target_pairs={{0,2},{1,3},{2,0},{3,1},{4,6},{5,7},{6,4},{7,5},{8,10},{9,11},{10,... | collective-permute-start | bytes 1376264 | tf_op jit(solution)/shard_map/ppermute | solution.py:56
  6.8 8.6 %collective-permute-start = (bf16[144,256]{1,0:T(8,128)(2,1)S(1)}, bf16[144,256]{1,0:T(8,128)(2,1)S(1)}, u32[]{:S(2)}, u32[]{:S(2)}) collective-permute-start(bf16[144,256]{1,0:T(8,128)(2,1)S(1)} %get-tuple-element.28), channel_id=1, source_target_pairs={{0,1},{1,0},{2,3},{3,2},{4,8},{5,9},{6,10},{7,11},{8,4},{9,5},{10,... | collective-permute-start | bytes 221192 | tf_op jit(solution)/shard_map/ppermute | solution.py:52
  7.0 8.3 %collective-permute-start.2 = (bf16[128,256]{1,0:T(8,128)(2,1)S(1)}, bf16[128,256]{1,0:T(8,128)(2,1)S(1)}, u32[]{:S(2)}, u32[]{:S(2)}) collective-permute-start(bf16[128,256]{1,0:T(8,128)(2,1)S(1)} %get-tuple-element.27.refs_1_), channel_id=1, source_target_pairs={{0,4},{1,5},{2,6},{3,7},{4,0},{5,1},{6,2},{7,3},{8,12},{9,13},{10,... | collective-permute-start | bytes 196616 | tf_op jit(solution)/shard_map/ppermute | solution.py:52
  10.0 5.3 %collective-permute-start.1 = (bf16[80,256]{1,0:T(8,128)(2,1)S(1)}, bf16[80,256]{1,0:T(8,128)(2,1)S(1)}, u32[]{:S(2)}, u32[]{:S(2)}) collective-permute-start(bf16[80,256]{1,0:T(8,128)(2,1)S(1)} %get-tuple-element.29), channel_id=1, source_target_pairs={{0,8},{1,9},{2,10},{3,11},{4,12},{5,13},{6,14},{7,15},{8,0},{9,1},... | collective-permute-start | bytes 122888 | tf_op jit(solution)/shard_map/ppermute | solution.py:52
  12.2 9.7 %collective-permute-start.6 = (bf16[144,512]{1,0:T(8,128)(2,1)S(1)}, bf16[144,512]{1,0:T(8,128)(2,1)S(1)}, u32[]{:S(2)}, u32[]{:S(2)}) collective-permute-start(bf16[144,512]{1,0:T(8,128)(2,1)S(1)} %get-tuple-element.39), channel_id=1, source_target_pairs={{0,1},{1,0},{2,3},{3,2},{4,8},{5,9},{6,10},{7,11},{8,4},{9,5},{10,... | collective-permute-start | bytes 442376 | tf_op jit(solution)/shard_map/ppermute | solution.py:52
  16.0 5.9 %collective-permute-start.8 = (bf16[128,512]{1,0:T(8,128)(2,1)S(1)}, bf16[128,512]{1,0:T(8,128)(2,1)S(1)}, u32[]{:S(2)}, u32[]{:S(2)}) collective-permute-start(bf16[128,512]{1,0:T(8,128)(2,1)S(1)} %get-tuple-element.41), channel_id=1, source_target_pairs={{0,4},{1,5},{2,6},{3,7},{4,0},{5,1},{6,2},{7,3},{8,12},{9,13},{10,... | collective-permute-start | bytes 393224 | tf_op jit(solution)/shard_map/ppermute | solution.py:52
  16.1 5.7 %collective-permute-start.7 = (bf16[80,512]{1,0:T(8,128)(2,1)S(1)}, bf16[80,512]{1,0:T(8,128)(2,1)S(1)}, u32[]{:S(2)}, u32[]{:S(2)}) collective-permute-start(bf16[80,512]{1,0:T(8,128)(2,1)S(1)} %get-tuple-element.40), channel_id=1, source_target_pairs={{0,8},{1,9},{2,10},{3,11},{4,12},{5,13},{6,14},{7,15},{8,0},{9,1},... | collective-permute-start | bytes 245768 | tf_op jit(solution)/shard_map/ppermute | solution.py:52
  17.9 7.8 %collective-permute-start.4 = (bf16[512,256]{1,0:T(8,128)(2,1)S(1)}, bf16[512,256]{1,0:T(8,128)(2,1)S(1)}, u32[]{:S(2)}, u32[]{:S(2)}) collective-permute-start(bf16[512,256]{1,0:T(8,128)(2,1)S(1)} %upsample.1.refs_0_.refs_3_.refs_1_), channel_id=1, source_target_pairs={{0,2},{1,3},{2,0},{3,1},{4,6},{5,7},{6,4},{7,5},{8,10},{9,11},{10,... | collective-permute-start | bytes 786440 | tf_op jit(solution)/shard_map/ppermute | solution.py:56
  18.4 8.6 %collective-permute-start.10 = (bf16[640,256]{1,0:T(8,128)(2,1)S(1)}, bf16[640,256]{1,0:T(8,128)(2,1)S(1)}, u32[]{:S(2)}, u32[]{:S(2)}) collective-permute-start(bf16[640,256]{1,0:T(8,128)(2,1)S(1)} %relay.1), channel_id=1, source_target_pairs={{0,16},{16,0},{1,17},{17,1},{2,18},{18,2},{3,19},{19,3},{4,20},{20... | collective-permute-start | bytes 983048 | tf_op jit(solution)/shard_map/ppermute | solution.py:323
  22.0 5.1 %collective-permute-start.9 = (bf16[128,512]{1,0:T(8,128)(2,1)S(1)}, bf16[128,512]{1,0:T(8,128)(2,1)S(1)}, u32[]{:S(2)}, u32[]{:S(2)}) collective-permute-start(bf16[128,512]{1,0:T(8,128)(2,1)S(1)} %get-tuple-element.42), channel_id=1, source_target_pairs={{0,2},{1,3},{2,0},{3,1},{4,6},{5,7},{6,4},{7,5},{8,10},{9,11},{10,... | collective-permute-start | bytes 393224 | tf_op jit(solution)/shard_map/ppermute | solution.py:56
  27.1 2.3 %collective-permute-start.11 = (bf16[512,512]{1,0:T(8,128)(2,1)S(1)}, bf16[512,512]{1,0:T(8,128)(2,1)S(1)}, u32[]{:S(2)}, u32[]{:S(2)}) collective-permute-start(bf16[512,512]{1,0:T(8,128)(2,1)S(1)} %pack.1), channel_id=1, source_target_pairs={{0,1},{1,0},{2,3},{3,2},{4,5},{5,4},{6,7},{7,6},{8,9},{9,8},{10,11... | collective-permute-start | bytes 1572872 | tf_op jit(solution)/shard_map/ppermute | solution.py:56
  27.7 1.7 %collective-permute-start.12 = (bf16[128,768]{1,0:T(8,128)(2,1)S(1)}, bf16[128,768]{1,0:T(8,128)(2,1)S(1)}, u32[]{:S(2)}, u32[]{:S(2)}) collective-permute-start(bf16[128,768]{1,0:T(8,128)(2,1)S(1)} %finish_part.2.refs_4_), channel_id=1, source_target_pairs={{0,1},{1,0},{2,3},{3,2},{4,5},{5,4},{6,7},{7,6},{8,9},{9,8},{10,11... | collective-permute-start | bytes 589832 | tf_op jit(solution)/shard_map/ppermute | solution.py:56
